TPU v7x, 32 devices: a whole 2x2x4 slice. The times are simulated.
32 devices in a mesh: mp: 2 (over x), proj: 16 (over z, y, core).
Axes of the slice: x: 2, y: 2, z: 4, core: 2. Of those that a mesh axis runs over, the one named last changes fastest.
Arguments:
- normed_hidden_input: bfloat16 [2048, 5120], P('proj', 'mp'), may hold values from -6 to 6
- attention_mixture: bfloat16 [2048, 5120], P('proj', 'mp'), may hold values from -6 to 6
- normed_gate_input: bfloat16 [2048, 5120], P('proj', 'mp'), may hold values from -6 to 6
- down_projection_input: bfloat16 [2048, 27648], P('proj', 'mp'), may hold values from -6 to 6
- query_out_cotangent: bfloat16 [2048, 5120], P('proj', 'mp'), may hold values from -6 to 6
- key_value_cotangents: bfloat16 [2048, 2, 1024], P('proj', None, 'mp'), may hold values from -6 to 6
- attention_out_cotangent: bfloat16 [2048, 5120], P('proj', 'mp'), may hold values from -6 to 6
- gate_up_cotangents: bfloat16 [2048, 2, 27648], P('proj', None, 'mp'), may hold values from -6 to 6
- down_out_cotangent: bfloat16 [2048, 5120], P('proj', 'mp'), may hold values from -6 to 6
- adapter_input_factors: bfloat16 [6, 8, 5120], P(None, None, 'mp'), may hold values from -0.078125 to 0.078125
- down_adapter_input_factor: bfloat16 [8, 27648], P(None, 'mp'), may hold values from -0.0390625 to 0.0390625
- adapter_output_factors: bfloat16 [3, 8, 5120], P(None, None, 'mp'), may hold values from -0.078125 to 0.078125
- key_value_adapter_output: bfloat16 [2, 8, 1024], P(None, None, 'mp'), may hold values from -0.1875 to 0.1875
- gate_up_adapter_output: bfloat16 [2, 8, 27648], P(None, None, 'mp'), may hold values from -0.0390625 to 0.0390625
- verified_loss_mask: int32 [2048], P('proj'), may hold values 0 or 1
- block_projector_seeds: int32 [14], replicated, may hold values from 0 to 16777215
Outputs:
- features: float32 [1, 2048], P(None, ('mp', 'proj'))
All inputs are finite; a program needn't handle non-finite values. No bound on the sum of `verified_loss_mask` on one device may be relied on, other than what follows from the above.
Results may differ from a plain program's by a relative error of at most 0.0028.
Values sent between devices are 32-bit elements; how exact they have to be, the bound alone decides.
No kernel may reach another device: no remote copies, remote signals or barrier semaphores. Data moves between devices by JAX's collectives and lax.ppermute only.
A program may use at most 64 MiB of HBM per device.

v0:
```python
import math

import jax
import jax.numpy as jnp
from jax import lax
from jax.sharding import PartitionSpec as P

K = 2048
LENGTH = 2048


def mix_bits(row_keys, col_keys):
    hashed = row_keys[:, None] ^ col_keys[None, :]
    hashed = hashed ^ hashed >> 16 & 65535
    hashed = hashed * -2048144789
    hashed = hashed ^ hashed >> 13 & 524287
    hashed = hashed * -1028477387
    hashed = hashed ^ hashed >> 16 & 65535
    byte_sum = (hashed & 255) + (hashed >> 8 & 255) + (hashed >> 16 & 255) + (hashed >> 24 & 255)
    return (byte_sum - 510).astype(jnp.float32)


def project_rows(gradients, row_keys, col_keys, block_limit):
    row_count = gradients.shape[1]
    block_rows = math.gcd(row_count, block_limit)

    def add_block(number, accumulated):
        first_row = (number * block_rows).astype(jnp.int32)
        grad_block = lax.dynamic_slice_in_dim(gradients, first_row, block_rows, 1)
        key_block = lax.dynamic_slice_in_dim(row_keys, first_row, block_rows, 0)
        table = mix_bits(key_block, col_keys)
        return accumulated + jnp.dot(
            grad_block, table, precision=lax.Precision.HIGHEST, preferred_element_type=jnp.float32
        )

    zero_acc = jnp.zeros((gradients.shape[0], col_keys.shape[0]), jnp.float32)
    return lax.fori_loop(0, row_count // block_rows, add_block, zero_acc)


def owned_keys(positions, widths, adapter_rank_count, block_projector_seeds, model_shard):
    key_table = jnp.zeros_like(positions)
    lower_edge = 0
    for segment, seg_width in enumerate(widths):
        upper_edge = lower_edge + adapter_rank_count * seg_width
        offset_pos = positions - lower_edge
        rank_pos = offset_pos // seg_width
        feature = model_shard * seg_width + offset_pos % seg_width
        seg_keys = (
            block_projector_seeds[segment] * 1103515245
            + (feature * adapter_rank_count + rank_pos) * 668265263
        )
        inside = (positions >= lower_edge) & (positions < upper_edge)
        key_table = jnp.where(inside, seg_keys, key_table)
        lower_edge = upper_edge
    return key_table


def shards(
    normed_hidden_input,
    attention_mixture,
    normed_gate_input,
    down_projection_input,
    query_out_cotangent,
    key_value_cotangents,
    attention_out_cotangent,
    gate_up_cotangents,
    down_out_cotangent,
    adapter_input_factors,
    down_adapter_input_factor,
    adapter_output_factors,
    key_value_adapter_output,
    gate_up_adapter_output,
    verified_loss_mask,
    block_projector_seeds,
):
    block_triplets = [
        (
            normed_hidden_input,
            query_out_cotangent,
            adapter_input_factors[0],
            adapter_output_factors[0],
        ),
        (
            normed_hidden_input,
            key_value_cotangents[:, 0],
            adapter_input_factors[1],
            key_value_adapter_output[0],
        ),
        (
            normed_hidden_input,
            key_value_cotangents[:, 1],
            adapter_input_factors[2],
            key_value_adapter_output[1],
        ),
        (
            attention_mixture,
            attention_out_cotangent,
            adapter_input_factors[3],
            adapter_output_factors[1],
        ),
        (
            normed_gate_input,
            gate_up_cotangents[:, 0],
            adapter_input_factors[4],
            gate_up_adapter_output[0],
        ),
        (
            normed_gate_input,
            gate_up_cotangents[:, 1],
            adapter_input_factors[5],
            gate_up_adapter_output[1],
        ),
        (
            down_projection_input,
            down_out_cotangent,
            down_adapter_input_factor,
            adapter_output_factors[2],
        ),
    ]
    factors = []
    for inputs, cotangent, factor_a, factor_b in block_triplets:
        factors.append(
            jnp.einsum("tf,rf->tr", inputs, factor_a, preferred_element_type=jnp.float32)
        )
        factors.append(
            jnp.einsum("tf,rf->tr", cotangent, factor_b, preferred_element_type=jnp.float32)
        )
    summed_factors = lax.psum(jnp.concatenate(factors, axis=1), "mp")
    adapter_rank_count = down_adapter_input_factor.shape[0]
    weights = verified_loss_mask.astype(jnp.float32)[:, None]
    flat_parts = []
    widths = []
    for number, (inputs, cotangent, factor_a, factor_b) in enumerate(block_triplets):
        act_a = summed_factors[
            :, 2 * number * adapter_rank_count : (2 * number + 1) * adapter_rank_count
        ]
        act_b = summed_factors[
            :, (2 * number + 1) * adapter_rank_count : (2 * number + 2) * adapter_rank_count
        ]
        masked_v = (weights * act_a).astype(jnp.bfloat16)
        masked_u = (weights * act_b).astype(jnp.bfloat16)
        grad_a = jnp.einsum("tr,tf->rf", masked_u, inputs, preferred_element_type=jnp.float32)
        grad_b = jnp.einsum("tr,tf->rf", masked_v, cotangent, preferred_element_type=jnp.float32)
        flat_parts.append(grad_a.reshape(-1))
        flat_parts.append(grad_b.reshape(-1))
        widths.append(inputs.shape[1])
        widths.append(cotangent.shape[1])
    local_grads = jnp.concatenate(flat_parts)
    model_shard = lax.axis_index("mp")
    owner_index = lax.axis_index("proj")
    owner_count = lax.axis_size("proj")
    tok_rows = verified_loss_mask.shape[0]
    examples = owner_count * tok_rows // LENGTH
    col_keys = jnp.arange(K, dtype=jnp.int32) * -1640531535
    slice_len = local_grads.shape[0] // owner_count
    received = lax.all_to_all(
        local_grads.reshape(owner_count, slice_len), "proj", split_axis=0, concat_axis=0, tiled=True
    )
    owned_grads = received.reshape(examples, owner_count // examples, slice_len).sum(axis=1)
    positions = owner_index * slice_len + jnp.arange(slice_len, dtype=jnp.int32)
    row_keys = owned_keys(positions, widths, adapter_rank_count, block_projector_seeds, model_shard)
    partial_proj = project_rows(owned_grads, row_keys, col_keys, 1024)
    summed = lax.psum_scatter(partial_proj, ("mp", "proj"), scatter_dimension=1, tiled=True)
    scale_out = 1.0 / (LENGTH * math.sqrt(21845.0 * K))
    return summed * scale_out


def solution(mesh):
    in_specs = (
        P("proj", "mp"),
        P("proj", "mp"),
        P("proj", "mp"),
        P("proj", "mp"),
        P("proj", "mp"),
        P("proj", None, "mp"),
        P("proj", "mp"),
        P("proj", None, "mp"),
        P("proj", "mp"),
        P(None, None, "mp"),
        P(None, "mp"),
        P(None, None, "mp"),
        P(None, None, "mp"),
        P(None, None, "mp"),
        P("proj"),
        P(),
    )
    out_specs = P(None, ("mp", "proj"))
    return jax.shard_map(shards, mesh=mesh, in_specs=in_specs, out_specs=out_specs, check_vma=False)
```

profile of v0, /device:TPU:0, one launch (start us, length us, event | category | flops | bytes accessed | tf_op | source)
XLA Modules:
  0.0 653.7 jit_solution(15178860365198345535)
XLA Ops:
  7.3 2.1 convolution_dynamic-update-slice_fusion.11
  9.5 2.0 convolution_dynamic-update-slice_fusion.10
  11.4 2.0 convolution_dynamic-update-slice_fusion.9
  13.4 1.5 fusion.347
  15.0 1.5 convolution_dynamic-update-slice_fusion.8
  16.4 2.0 convolution_dynamic-update-slice_fusion.7
  18.4 14.1 %fusion.346 = (bf16[128,1,13824]{2,1,0:T(2,128)(2,1)S(1)}, bf16[128,1,13824]{2,1,0:T(2,128)(2,1)S(1)}) fusion(bf16[128,2,13824]{2,1,0:T(2,128)(2,1)} %param.25), kind=kLoop, calls=%fused_computation.428 | loop fusion | bytes 14155776 | tf_op jit(solution)/shard_map/slice | solution.py:109
  35.0 1.5 convolution_dynamic-update-slice_fusion.4
  37.6 1.6 fusion.58
  40.1 1.6 fusion.57
  41.7 1.6 convolution_dynamic-update-slice_fusion.1
  44.2 11.5 %psum.7 = f32[128,112]{0,1:T(8,128)} all-reduce(f32[128,112]{0,1:T(8,128)} %convolution_dynamic-update-slice_fusion), channel_id=1, replica_groups=mesh['mp'=2,'proj'=16] {'mp'}, use_global_device_ids=true, to_apply=%region_0.0 | all-reduce | flops 14336 | bytes 114688 | tf_op jit(solution)/shard_map/psum | solution.py:128
  55.8 4.5 fusion.55
  60.3 4.5 fusion.53
  74.5 1.8 reshape.102
  76.3 1.8 reshape.104
  78.1 1.5 reshape.106
  79.6 1.5 reshape.103
  81.2 1.5 reshape.101
  82.7 1.5 reshape.100
  84.2 1.5 reshape.99
  85.7 1.5 reshape.97
  87.2 1.5 reshape.95
  88.8 1.5 reshape.94
  90.3 1.5 reshape.93
  91.8 1.8 reshape.105
  106.0 5.8 all-to-all-start
  121.5 3.0 fusion.68
  124.5 28.4 %all-to-all-done = f32[16,1,32768]{2,1,0:T(1,128)} async-done(((f32[16,1,32768]{2,1,0:T(1,128)}), f32[16,1,32768]{2,1,0:T(1,128)}, u32[]{:S(2)}, u32[]{:S(2)}) %all-to-all-start) | async-done | bytes 2097184 | tf_op jit(solution)/shard_map/all_to_all | solution.py:156
  152.9 3.6 reduce_sum.11
  156.5 345.3 %while.16 = (s32[]{:T(128)}, f32[1,2048]{1,0:T(1,128)S(1)}, f32[1,32768]{1,0:T(1,128)}, s32[32768]{0:T(1024)}, s32[]{:T(128)}, /*index=5*/s32[]{:T(128)}, s32[]{:T(128)}, s32[]{:T(128)}) while((s32[]{:T(128)}, f32[1,2048]{1,0:T(1,128)S(1)}, f32[1,32768]{1,0:T(1,128)}, s32[32768]{0:T(1024)}, s32[]{:T(128)}, /*index=5*/s32[]{:T(128)}, ...), condition=%wide.region_3.4_spmd.clone, body=%wide.region_2.3_spmd.clone.sunk | while | flops 75503624 | bytes 49309 | solution.py:37
  157.2 10.1 %fusion.375 = f32[1,2048]{1,0:T(1,128)S(1)} fusion(s32[2048]{0:T(1024)S(1)} %iota_multiply_fusion.2, s32[1024]{0:T(1024)S(1)} %dynamic_slice.29, f32[1,2048]{1,0:T(1,128)S(1)} %get-tuple-element.215, pred[]{:T(512)S(6)} %compare.9, f32[1,32768]{1,0:T(1,128)} %get-tuple-element.224, s32[]{:T(128)S(6)} %select_n.490), kind=kOutput, calls=%fused_computation.37.clone.1 | convolution fusion | flops 75501568 | bytes 32773 | tf_op jit(solution)/shard_map/while/body/eval_jaxpr/dot_general | solution.py:32
  167.9 10.1 %fusion.375 = f32[1,2048]{1,0:T(1,128)S(1)} fusion(s32[2048]{0:T(1024)S(1)} %iota_multiply_fusion.2, s32[1024]{0:T(1024)S(1)} %dynamic_slice.29, f32[1,2048]{1,0:T(1,128)S(1)} %get-tuple-element.215, pred[]{:T(512)S(6)} %compare.9, f32[1,32768]{1,0:T(1,128)} %get-tuple-element.224, s32[]{:T(128)S(6)} %select_n.490), kind=kOutput, calls=%fused_computation.37.clone.1 | convolution fusion | flops 75501568 | bytes 32773 | tf_op jit(solution)/shard_map/while/body/eval_jaxpr/dot_general | solution.py:32
  178.7 10.1 %fusion.375 = f32[1,2048]{1,0:T(1,128)S(1)} fusion(s32[2048]{0:T(1024)S(1)} %iota_multiply_fusion.2, s32[1024]{0:T(1024)S(1)} %dynamic_slice.29, f32[1,2048]{1,0:T(1,128)S(1)} %get-tuple-element.215, pred[]{:T(512)S(6)} %compare.9, f32[1,32768]{1,0:T(1,128)} %get-tuple-element.224, s32[]{:T(128)S(6)} %select_n.490), kind=kOutput, calls=%fused_computation.37.clone.1 | convolution fusion | flops 75501568 | bytes 32773 | tf_op jit(solution)/shard_map/while/body/eval_jaxpr/dot_general | solution.py:32
  189.5 10.1 %fusion.375 = f32[1,2048]{1,0:T(1,128)S(1)} fusion(s32[2048]{0:T(1024)S(1)} %iota_multiply_fusion.2, s32[1024]{0:T(1024)S(1)} %dynamic_slice.29, f32[1,2048]{1,0:T(1,128)S(1)} %get-tuple-element.215, pred[]{:T(512)S(6)} %compare.9, f32[1,32768]{1,0:T(1,128)} %get-tuple-element.224, s32[]{:T(128)S(6)} %select_n.490), kind=kOutput, calls=%fused_computation.37.clone.1 | convolution fusion | flops 75501568 | bytes 32773 | tf_op jit(solution)/shard_map/while/body/eval_jaxpr/dot_general | solution.py:32
  200.3 10.1 %fusion.375 = f32[1,2048]{1,0:T(1,128)S(1)} fusion(s32[2048]{0:T(1024)S(1)} %iota_multiply_fusion.2, s32[1024]{0:T(1024)S(1)} %dynamic_slice.29, f32[1,2048]{1,0:T(1,128)S(1)} %get-tuple-element.215, pred[]{:T(512)S(6)} %compare.9, f32[1,32768]{1,0:T(1,128)} %get-tuple-element.224, s32[]{:T(128)S(6)} %select_n.490), kind=kOutput, calls=%fused_computation.37.clone.1 | convolution fusion | flops 75501568 | bytes 32773 | tf_op jit(solution)/shard_map/while/body/eval_jaxpr/dot_general | solution.py:32
  211.1 10.1 %fusion.375 = f32[1,2048]{1,0:T(1,128)S(1)} fusion(s32[2048]{0:T(1024)S(1)} %iota_multiply_fusion.2, s32[1024]{0:T(1024)S(1)} %dynamic_slice.29, f32[1,2048]{1,0:T(1,128)S(1)} %get-tuple-element.215, pred[]{:T(512)S(6)} %compare.9, f32[1,32768]{1,0:T(1,128)} %get-tuple-element.224, s32[]{:T(128)S(6)} %select_n.490), kind=kOutput, calls=%fused_computation.37.clone.1 | convolution fusion | flops 75501568 | bytes 32773 | tf_op jit(solution)/shard_map/while/body/eval_jaxpr/dot_general | solution.py:32
  221.9 10.1 %fusion.375 = f32[1,2048]{1,0:T(1,128)S(1)} fusion(s32[2048]{0:T(1024)S(1)} %iota_multiply_fusion.2, s32[1024]{0:T(1024)S(1)} %dynamic_slice.29, f32[1,2048]{1,0:T(1,128)S(1)} %get-tuple-element.215, pred[]{:T(512)S(6)} %compare.9, f32[1,32768]{1,0:T(1,128)} %get-tuple-element.224, s32[]{:T(128)S(6)} %select_n.490), kind=kOutput, calls=%fused_computation.37.clone.1 | convolution fusion | flops 75501568 | bytes 32773 | tf_op jit(solution)/shard_map/while/body/eval_jaxpr/dot_general | solution.py:32
  232.7 10.1 %fusion.375 = f32[1,2048]{1,0:T(1,128)S(1)} fusion(s32[2048]{0:T(1024)S(1)} %iota_multiply_fusion.2, s32[1024]{0:T(1024)S(1)} %dynamic_slice.29, f32[1,2048]{1,0:T(1,128)S(1)} %get-tuple-element.215, pred[]{:T(512)S(6)} %compare.9, f32[1,32768]{1,0:T(1,128)} %get-tuple-element.224, s32[]{:T(128)S(6)} %select_n.490), kind=kOutput, calls=%fused_computation.37.clone.1 | convolution fusion | flops 75501568 | bytes 32773 | tf_op jit(solution)/shard_map/while/body/eval_jaxpr/dot_general | solution.py:32
  243.5 10.1 %fusion.375 = f32[1,2048]{1,0:T(1,128)S(1)} fusion(s32[2048]{0:T(1024)S(1)} %iota_multiply_fusion.2, s32[1024]{0:T(1024)S(1)} %dynamic_slice.29, f32[1,2048]{1,0:T(1,128)S(1)} %get-tuple-element.215, pred[]{:T(512)S(6)} %compare.9, f32[1,32768]{1,0:T(1,128)} %get-tuple-element.224, s32[]{:T(128)S(6)} %select_n.490), kind=kOutput, calls=%fused_computation.37.clone.1 | convolution fusion | flops 75501568 | bytes 32773 | tf_op jit(solution)/shard_map/while/body/eval_jaxpr/dot_general | solution.py:32
  254.3 10.1 %fusion.375 = f32[1,2048]{1,0:T(1,128)S(1)} fusion(s32[2048]{0:T(1024)S(1)} %iota_multiply_fusion.2, s32[1024]{0:T(1024)S(1)} %dynamic_slice.29, f32[1,2048]{1,0:T(1,128)S(1)} %get-tuple-element.215, pred[]{:T(512)S(6)} %compare.9, f32[1,32768]{1,0:T(1,128)} %get-tuple-element.224, s32[]{:T(128)S(6)} %select_n.490), kind=kOutput, calls=%fused_computation.37.clone.1 | convolution fusion | flops 75501568 | bytes 32773 | tf_op jit(solution)/shard_map/while/body/eval_jaxpr/dot_general | solution.py:32
  265.1 10.1 %fusion.375 = f32[1,2048]{1,0:T(1,128)S(1)} fusion(s32[2048]{0:T(1024)S(1)} %iota_multiply_fusion.2, s32[1024]{0:T(1024)S(1)} %dynamic_slice.29, f32[1,2048]{1,0:T(1,128)S(1)} %get-tuple-element.215, pred[]{:T(512)S(6)} %compare.9, f32[1,32768]{1,0:T(1,128)} %get-tuple-element.224, s32[]{:T(128)S(6)} %select_n.490), kind=kOutput, calls=%fused_computation.37.clone.1 | convolution fusion | flops 75501568 | bytes 32773 | tf_op jit(solution)/shard_map/while/body/eval_jaxpr/dot_general | solution.py:32
  275.9 10.1 %fusion.375 = f32[1,2048]{1,0:T(1,128)S(1)} fusion(s32[2048]{0:T(1024)S(1)} %iota_multiply_fusion.2, s32[1024]{0:T(1024)S(1)} %dynamic_slice.29, f32[1,2048]{1,0:T(1,128)S(1)} %get-tuple-element.215, pred[]{:T(512)S(6)} %compare.9, f32[1,32768]{1,0:T(1,128)} %get-tuple-element.224, s32[]{:T(128)S(6)} %select_n.490), kind=kOutput, calls=%fused_computation.37.clone.1 | convolution fusion | flops 75501568 | bytes 32773 | tf_op jit(solution)/shard_map/while/body/eval_jaxpr/dot_general | solution.py:32
  286.7 10.1 %fusion.375 = f32[1,2048]{1,0:T(1,128)S(1)} fusion(s32[2048]{0:T(1024)S(1)} %iota_multiply_fusion.2, s32[1024]{0:T(1024)S(1)} %dynamic_slice.29, f32[1,2048]{1,0:T(1,128)S(1)} %get-tuple-element.215, pred[]{:T(512)S(6)} %compare.9, f32[1,32768]{1,0:T(1,128)} %get-tuple-element.224, s32[]{:T(128)S(6)} %select_n.490), kind=kOutput, calls=%fused_computation.37.clone.1 | convolution fusion | flops 75501568 | bytes 32773 | tf_op jit(solution)/shard_map/while/body/eval_jaxpr/dot_general | solution.py:32
  297.4 10.1 %fusion.375 = f32[1,2048]{1,0:T(1,128)S(1)} fusion(s32[2048]{0:T(1024)S(1)} %iota_multiply_fusion.2, s32[1024]{0:T(1024)S(1)} %dynamic_slice.29, f32[1,2048]{1,0:T(1,128)S(1)} %get-tuple-element.215, pred[]{:T(512)S(6)} %compare.9, f32[1,32768]{1,0:T(1,128)} %get-tuple-element.224, s32[]{:T(128)S(6)} %select_n.490), kind=kOutput, calls=%fused_computation.37.clone.1 | convolution fusion | flops 75501568 | bytes 32773 | tf_op jit(solution)/shard_map/while/body/eval_jaxpr/dot_general | solution.py:32
  308.2 10.1 %fusion.375 = f32[1,2048]{1,0:T(1,128)S(1)} fusion(s32[2048]{0:T(1024)S(1)} %iota_multiply_fusion.2, s32[1024]{0:T(1024)S(1)} %dynamic_slice.29, f32[1,2048]{1,0:T(1,128)S(1)} %get-tuple-element.215, pred[]{:T(512)S(6)} %compare.9, f32[1,32768]{1,0:T(1,128)} %get-tuple-element.224, s32[]{:T(128)S(6)} %select_n.490), kind=kOutput, calls=%fused_computation.37.clone.1 | convolution fusion | flops 75501568 | bytes 32773 | tf_op jit(solution)/shard_map/while/body/eval_jaxpr/dot_general | solution.py:32
  319.0 10.1 %fusion.375 = f32[1,2048]{1,0:T(1,128)S(1)} fusion(s32[2048]{0:T(1024)S(1)} %iota_multiply_fusion.2, s32[1024]{0:T(1024)S(1)} %dynamic_slice.29, f32[1,2048]{1,0:T(1,128)S(1)} %get-tuple-element.215, pred[]{:T(512)S(6)} %compare.9, f32[1,32768]{1,0:T(1,128)} %get-tuple-element.224, s32[]{:T(128)S(6)} %select_n.490), kind=kOutput, calls=%fused_computation.37.clone.1 | convolution fusion | flops 75501568 | bytes 32773 | tf_op jit(solution)/shard_map/while/body/eval_jaxpr/dot_general | solution.py:32
  329.8 10.1 %fusion.375 = f32[1,2048]{1,0:T(1,128)S(1)} fusion(s32[2048]{0:T(1024)S(1)} %iota_multiply_fusion.2, s32[1024]{0:T(1024)S(1)} %dynamic_slice.29, f32[1,2048]{1,0:T(1,128)S(1)} %get-tuple-element.215, pred[]{:T(512)S(6)} %compare.9, f32[1,32768]{1,0:T(1,128)} %get-tuple-element.224, s32[]{:T(128)S(6)} %select_n.490), kind=kOutput, calls=%fused_computation.37.clone.1 | convolution fusion | flops 75501568 | bytes 32773 | tf_op jit(solution)/shard_map/while/body/eval_jaxpr/dot_general | solution.py:32
  340.6 10.1 %fusion.375 = f32[1,2048]{1,0:T(1,128)S(1)} fusion(s32[2048]{0:T(1024)S(1)} %iota_multiply_fusion.2, s32[1024]{0:T(1024)S(1)} %dynamic_slice.29, f32[1,2048]{1,0:T(1,128)S(1)} %get-tuple-element.215, pred[]{:T(512)S(6)} %compare.9, f32[1,32768]{1,0:T(1,128)} %get-tuple-element.224, s32[]{:T(128)S(6)} %select_n.490), kind=kOutput, calls=%fused_computation.37.clone.1 | convolution fusion | flops 75501568 | bytes 32773 | tf_op jit(solution)/shard_map/while/body/eval_jaxpr/dot_general | solution.py:32
  351.4 10.1 %fusion.375 = f32[1,2048]{1,0:T(1,128)S(1)} fusion(s32[2048]{0:T(1024)S(1)} %iota_multiply_fusion.2, s32[1024]{0:T(1024)S(1)} %dynamic_slice.29, f32[1,2048]{1,0:T(1,128)S(1)} %get-tuple-element.215, pred[]{:T(512)S(6)} %compare.9, f32[1,32768]{1,0:T(1,128)} %get-tuple-element.224, s32[]{:T(128)S(6)} %select_n.490), kind=kOutput, calls=%fused_computation.37.clone.1 | convolution fusion | flops 75501568 | bytes 32773 | tf_op jit(solution)/shard_map/while/body/eval_jaxpr/dot_general | solution.py:32
  362.2 10.1 %fusion.375 = f32[1,2048]{1,0:T(1,128)S(1)} fusion(s32[2048]{0:T(1024)S(1)} %iota_multiply_fusion.2, s32[1024]{0:T(1024)S(1)} %dynamic_slice.29, f32[1,2048]{1,0:T(1,128)S(1)} %get-tuple-element.215, pred[]{:T(512)S(6)} %compare.9, f32[1,32768]{1,0:T(1,128)} %get-tuple-element.224, s32[]{:T(128)S(6)} %select_n.490), kind=kOutput, calls=%fused_computation.37.clone.1 | convolution fusion | flops 75501568 | bytes 32773 | tf_op jit(solution)/shard_map/while/body/eval_jaxpr/dot_general | solution.py:32
  373.0 10.1 %fusion.375 = f32[1,2048]{1,0:T(1,128)S(1)} fusion(s32[2048]{0:T(1024)S(1)} %iota_multiply_fusion.2, s32[1024]{0:T(1024)S(1)} %dynamic_slice.29, f32[1,2048]{1,0:T(1,128)S(1)} %get-tuple-element.215, pred[]{:T(512)S(6)} %compare.9, f32[1,32768]{1,0:T(1,128)} %get-tuple-element.224, s32[]{:T(128)S(6)} %select_n.490), kind=kOutput, calls=%fused_computation.37.clone.1 | convolution fusion | flops 75501568 | bytes 32773 | tf_op jit(solution)/shard_map/while/body/eval_jaxpr/dot_general | solution.py:32
  383.8 10.1 %fusion.375 = f32[1,2048]{1,0:T(1,128)S(1)} fusion(s32[2048]{0:T(1024)S(1)} %iota_multiply_fusion.2, s32[1024]{0:T(1024)S(1)} %dynamic_slice.29, f32[1,2048]{1,0:T(1,128)S(1)} %get-tuple-element.215, pred[]{:T(512)S(6)} %compare.9, f32[1,32768]{1,0:T(1,128)} %get-tuple-element.224, s32[]{:T(128)S(6)} %select_n.490), kind=kOutput, calls=%fused_computation.37.clone.1 | convolution fusion | flops 75501568 | bytes 32773 | tf_op jit(solution)/shard_map/while/body/eval_jaxpr/dot_general | solution.py:32
  394.6 10.1 %fusion.375 = f32[1,2048]{1,0:T(1,128)S(1)} fusion(s32[2048]{0:T(1024)S(1)} %iota_multiply_fusion.2, s32[1024]{0:T(1024)S(1)} %dynamic_slice.29, f32[1,2048]{1,0:T(1,128)S(1)} %get-tuple-element.215, pred[]{:T(512)S(6)} %compare.9, f32[1,32768]{1,0:T(1,128)} %get-tuple-element.224, s32[]{:T(128)S(6)} %select_n.490), kind=kOutput, calls=%fused_computation.37.clone.1 | convolution fusion | flops 75501568 | bytes 32773 | tf_op jit(solution)/shard_map/while/body/eval_jaxpr/dot_general | solution.py:32
  405.3 10.1 %fusion.375 = f32[1,2048]{1,0:T(1,128)S(1)} fusion(s32[2048]{0:T(1024)S(1)} %iota_multiply_fusion.2, s32[1024]{0:T(1024)S(1)} %dynamic_slice.29, f32[1,2048]{1,0:T(1,128)S(1)} %get-tuple-element.215, pred[]{:T(512)S(6)} %compare.9, f32[1,32768]{1,0:T(1,128)} %get-tuple-element.224, s32[]{:T(128)S(6)} %select_n.490), kind=kOutput, calls=%fused_computation.37.clone.1 | convolution fusion | flops 75501568 | bytes 32773 | tf_op jit(solution)/shard_map/while/body/eval_jaxpr/dot_general | solution.py:32
  416.1 10.1 %fusion.375 = f32[1,2048]{1,0:T(1,128)S(1)} fusion(s32[2048]{0:T(1024)S(1)} %iota_multiply_fusion.2, s32[1024]{0:T(1024)S(1)} %dynamic_slice.29, f32[1,2048]{1,0:T(1,128)S(1)} %get-tuple-element.215, pred[]{:T(512)S(6)} %compare.9, f32[1,32768]{1,0:T(1,128)} %get-tuple-element.224, s32[]{:T(128)S(6)} %select_n.490), kind=kOutput, calls=%fused_computation.37.clone.1 | convolution fusion | flops 75501568 | bytes 32773 | tf_op jit(solution)/shard_map/while/body/eval_jaxpr/dot_general | solution.py:32
  426.9 10.1 %fusion.375 = f32[1,2048]{1,0:T(1,128)S(1)} fusion(s32[2048]{0:T(1024)S(1)} %iota_multiply_fusion.2, s32[1024]{0:T(1024)S(1)} %dynamic_slice.29, f32[1,2048]{1,0:T(1,128)S(1)} %get-tuple-element.215, pred[]{:T(512)S(6)} %compare.9, f32[1,32768]{1,0:T(1,128)} %get-tuple-element.224, s32[]{:T(128)S(6)} %select_n.490), kind=kOutput, calls=%fused_computation.37.clone.1 | convolution fusion | flops 75501568 | bytes 32773 | tf_op jit(solution)/shard_map/while/body/eval_jaxpr/dot_general | solution.py:32
  437.7 10.1 %fusion.375 = f32[1,2048]{1,0:T(1,128)S(1)} fusion(s32[2048]{0:T(1024)S(1)} %iota_multiply_fusion.2, s32[1024]{0:T(1024)S(1)} %dynamic_slice.29, f32[1,2048]{1,0:T(1,128)S(1)} %get-tuple-element.215, pred[]{:T(512)S(6)} %compare.9, f32[1,32768]{1,0:T(1,128)} %get-tuple-element.224, s32[]{:T(128)S(6)} %select_n.490), kind=kOutput, calls=%fused_computation.37.clone.1 | convolution fusion | flops 75501568 | bytes 32773 | tf_op jit(solution)/shard_map/while/body/eval_jaxpr/dot_general | solution.py:32
  448.5 10.1 %fusion.375 = f32[1,2048]{1,0:T(1,128)S(1)} fusion(s32[2048]{0:T(1024)S(1)} %iota_multiply_fusion.2, s32[1024]{0:T(1024)S(1)} %dynamic_slice.29, f32[1,2048]{1,0:T(1,128)S(1)} %get-tuple-element.215, pred[]{:T(512)S(6)} %compare.9, f32[1,32768]{1,0:T(1,128)} %get-tuple-element.224, s32[]{:T(128)S(6)} %select_n.490), kind=kOutput, calls=%fused_computation.37.clone.1 | convolution fusion | flops 75501568 | bytes 32773 | tf_op jit(solution)/shard_map/while/body/eval_jaxpr/dot_general | solution.py:32
  459.3 10.1 %fusion.375 = f32[1,2048]{1,0:T(1,128)S(1)} fusion(s32[2048]{0:T(1024)S(1)} %iota_multiply_fusion.2, s32[1024]{0:T(1024)S(1)} %dynamic_slice.29, f32[1,2048]{1,0:T(1,128)S(1)} %get-tuple-element.215, pred[]{:T(512)S(6)} %compare.9, f32[1,32768]{1,0:T(1,128)} %get-tuple-element.224, s32[]{:T(128)S(6)} %select_n.490), kind=kOutput, calls=%fused_computation.37.clone.1 | convolution fusion | flops 75501568 | bytes 32773 | tf_op jit(solution)/shard_map/while/body/eval_jaxpr/dot_general | solution.py:32
  470.1 10.1 %fusion.375 = f32[1,2048]{1,0:T(1,128)S(1)} fusion(s32[2048]{0:T(1024)S(1)} %iota_multiply_fusion.2, s32[1024]{0:T(1024)S(1)} %dynamic_slice.29, f32[1,2048]{1,0:T(1,128)S(1)} %get-tuple-element.215, pred[]{:T(512)S(6)} %compare.9, f32[1,32768]{1,0:T(1,128)} %get-tuple-element.224, s32[]{:T(128)S(6)} %select_n.490), kind=kOutput, calls=%fused_computation.37.clone.1 | convolution fusion | flops 75501568 | bytes 32773 | tf_op jit(solution)/shard_map/while/body/eval_jaxpr/dot_general | solution.py:32
  480.9 10.1 %fusion.375 = f32[1,2048]{1,0:T(1,128)S(1)} fusion(s32[2048]{0:T(1024)S(1)} %iota_multiply_fusion.2, s32[1024]{0:T(1024)S(1)} %dynamic_slice.29, f32[1,2048]{1,0:T(1,128)S(1)} %get-tuple-element.215, pred[]{:T(512)S(6)} %compare.9, f32[1,32768]{1,0:T(1,128)} %get-tuple-element.224, s32[]{:T(128)S(6)} %select_n.490), kind=kOutput, calls=%fused_computation.37.clone.1 | convolution fusion | flops 75501568 | bytes 32773 | tf_op jit(solution)/shard_map/while/body/eval_jaxpr/dot_general | solution.py:32
  491.7 10.1 %fusion.375 = f32[1,2048]{1,0:T(1,128)S(1)} fusion(s32[2048]{0:T(1024)S(1)} %iota_multiply_fusion.2, s32[1024]{0:T(1024)S(1)} %dynamic_slice.29, f32[1,2048]{1,0:T(1,128)S(1)} %get-tuple-element.215, pred[]{:T(512)S(6)} %compare.9, f32[1,32768]{1,0:T(1,128)} %get-tuple-element.224, s32[]{:T(128)S(6)} %select_n.490), kind=kOutput, calls=%fused_computation.37.clone.1 | convolution fusion | flops 75501568 | bytes 32773 | tf_op jit(solution)/shard_map/while/body/eval_jaxpr/dot_general | solution.py:32
  503.2 142.3 %reduce-scatter.4.cloned.1.call-done = f32[64,1]{1,0:T(8,128)} async-done(((f32[2048,1]{1,0:T(8,128)}), f32[64,1]{1,0:T(8,128)}) %reduce-scatter.4.cloned.1.call-update) | async-done | bytes 272
  (157 shorter events, 53.8 us)
Async XLA Ops:
  6.5 35.2 %copy-start = (bf16[128,13824]{1,0:T(8,128)(2,1)S(1)}, bf16[128,13824]{1,0:T(8,128)(2,1)}, u32[]{:S(2)}) copy-start(bf16[128,13824]{1,0:T(8,128)(2,1)} %param.21) | copy-start | bytes 10616836
  14.9 1.5 copy-start.14
  14.9 17.7 %copy-start.16 = (bf16[128,1,512]{2,1,0:T(2,128)(2,1)}, bf16[128,1,512]{2,1,0:T(2,128)(2,1)S(1)}, u32[]{:S(2)}) copy-start(bf16[128,1,512]{2,1,0:T(2,128)(2,1)S(1)} %get-tuple-element.165) | copy-start | bytes 393220
  18.4 14.2 %copy-start.25 = (bf16[2,8,512]{2,1,0:T(8,128)(2,1)S(1)}, bf16[2,8,512]{2,1,0:T(8,128)(2,1)}, u32[]{:S(2)}) copy-start(bf16[2,8,512]{2,1,0:T(8,128)(2,1)} %param.30) | copy-start | bytes 49156
  18.4 15.1 %copy-start.10 = (bf16[128,2560]{1,0:T(8,128)(2,1)S(1)}, bf16[128,2560]{1,0:T(8,128)(2,1)}, u32[]{:S(2)}) copy-start(bf16[128,2560]{1,0:T(8,128)(2,1)} %param.19) | copy-start | bytes 1966084
  18.4 15.1 %copy-start.19 = (bf16[6,8,2560]{2,1,0:T(8,128)(2,1)S(1)}, bf16[6,8,2560]{2,1,0:T(8,128)(2,1)}, u32[]{:S(2)}) copy-start(bf16[6,8,2560]{2,1,0:T(8,128)(2,1)} %param.27) | copy-start | bytes 737284
  18.4 16.6 %copy-start.8 = (bf16[128,2560]{1,0:T(8,128)(2,1)S(1)}, bf16[128,2560]{1,0:T(8,128)(2,1)}, u32[]{:S(2)}) copy-start(bf16[128,2560]{1,0:T(8,128)(2,1)} %param.24) | copy-start | bytes 1966084
  18.4 16.6 %copy-start.22 = (bf16[3,8,2560]{2,1,0:T(8,128)(2,1)S(1)}, bf16[3,8,2560]{2,1,0:T(8,128)(2,1)}, u32[]{:S(2)}) copy-start(bf16[3,8,2560]{2,1,0:T(8,128)(2,1)} %param.29) | copy-start | bytes 368644
  18.4 18.1 %copy-start.4 = (bf16[128,2560]{1,0:T(8,128)(2,1)S(1)}, bf16[128,2560]{1,0:T(8,128)(2,1)}, u32[]{:S(2)}) copy-start(bf16[128,2560]{1,0:T(8,128)(2,1)} %param.20) | copy-start | bytes 1966084
  18.4 19.2 %copy-start.24 = (bf16[2,8,13824]{2,1,0:T(8,128)(2,1)S(1)}, bf16[2,8,13824]{2,1,0:T(8,128)(2,1)}, u32[]{:S(2)}) copy-start(bf16[2,8,13824]{2,1,0:T(8,128)(2,1)} %param.31) | copy-start | bytes 1327108
  32.6 7.5 %copy-start.2 = (bf16[128,1,13824]{2,1,0:T(2,128)(2,1)}, bf16[128,1,13824]{2,1,0:T(2,128)(2,1)S(1)}, u32[]{:S(2)}) copy-start(bf16[128,1,13824]{2,1,0:T(2,128)(2,1)S(1)} %get-tuple-element.164) | copy-start | bytes 10616836
  32.6 7.5 %copy-start.3 = (bf16[128,1,13824]{2,1,0:T(2,128)(2,1)}, bf16[128,1,13824]{2,1,0:T(2,128)(2,1)S(1)}, u32[]{:S(2)}) copy-start(bf16[128,1,13824]{2,1,0:T(2,128)(2,1)S(1)} %get-tuple-element.163) | copy-start | bytes 10616836
  39.3 2.5 copy-start.21
  40.1 3.2 copy-start.6
  55.7 4.5 copy-start.20
  55.7 9.0 %copy-start.17 = (bf16[128,1,512]{2,1,0:T(2,128)(2,1)S(1)}, bf16[128,1,512]{2,1,0:T(2,128)(2,1)}, u32[]{:S(2)}) copy-start(bf16[128,1,512]{2,1,0:T(2,128)(2,1)} %copy-done.16) | copy-start | bytes 393220
  55.7 9.1 %copy-start.15 = (bf16[128,1,512]{2,1,0:T(2,128)(2,1)S(1)}, bf16[128,1,512]{2,1,0:T(2,128)(2,1)}, u32[]{:S(2)}) copy-start(bf16[128,1,512]{2,1,0:T(2,128)(2,1)} %copy-done.14) | copy-start | bytes 393220
  55.8 9.3 %copy-start.7 = (bf16[128,2560]{1,0:T(8,128)(2,1)S(1)}, bf16[128,2560]{1,0:T(8,128)(2,1)}, u32[]{:S(2)}) copy-start(bf16[128,2560]{1,0:T(8,128)(2,1)} %param.26) | copy-start | bytes 1966084
  55.8 10.1 %copy-start.5 = (bf16[128,2560]{1,0:T(8,128)(2,1)S(1)}, bf16[128,2560]{1,0:T(8,128)(2,1)}, u32[]{:S(2)}) copy-start(bf16[128,2560]{1,0:T(8,128)(2,1)} %param.20) | copy-start | bytes 1966084
  60.3 7.3 %copy-start.9 = (bf16[128,2560]{1,0:T(8,128)(2,1)S(1)}, bf16[128,2560]{1,0:T(8,128)(2,1)}, u32[]{:S(2)}) copy-start(bf16[128,2560]{1,0:T(8,128)(2,1)} %param.24) | copy-start | bytes 1966084
  60.3 8.1 %copy-start.11 = (bf16[128,2560]{1,0:T(8,128)(2,1)S(1)}, bf16[128,2560]{1,0:T(8,128)(2,1)}, u32[]{:S(2)}) copy-start(bf16[128,2560]{1,0:T(8,128)(2,1)} %param.19) | copy-start | bytes 1966084
  60.3 8.9 %copy-start.1 = (bf16[128,2560]{1,0:T(8,128)(2,1)S(1)}, bf16[128,2560]{1,0:T(8,128)(2,1)}, u32[]{:S(2)}) copy-start(bf16[128,2560]{1,0:T(8,128)(2,1)} %param.18) | copy-start | bytes 1966084
  64.8 6.1 copy-start.12
  93.6 11.1 %copy-start.18 = (f32[20480]{0:T(1024)S(1)}, f32[20480]{0:T(1024)}, u32[]{:S(2)}) copy-start(f32[20480]{0:T(1024)} %reshape.106) | copy-start | bytes 245764
  100.6 11.3 %copy-start.23 = (s32[14]{0:T(128)S(1)}, s32[14]{0:T(128)}, u32[]{:S(2)}) copy-start(s32[14]{0:T(128)} %param.33) | copy-start | bytes 172
  104.7 1.3 copy-start.13
  106.0 46.9 %all-to-all-start = ((f32[16,1,32768]{2,1,0:T(1,128)}), f32[16,1,32768]{2,1,0:T(1,128)}, u32[]{:S(2)}, u32[]{:S(2)}) async-start(f32[16,1,32768]{2,1,0:T(1,128)} %bitcast.112), calls=%async_computation | async-start | bytes 4194304 | tf_op jit(solution)/shard_map/all_to_all | solution.py:156
  111.8 533.7 %reduce-scatter.4.cloned.1.call-start = ((), (), s32[]{:S(2)}) async-start(), calls=%async_computation.2 | async-start | bytes 1081344
Sparse Core Ops, SparseCore 0:
  503.3 142.1 reduce-scatter.3
where the time goes:
time: 657 us; the launch traced here: 654 us
  matrix products  362 us (55%)
  waiting for transfers between devices  171 us (26%)
  local copies, waits for them, and re-layouts  72.7 us (11%)
  between operations  22.5 us (3%)
  blocking collectives  11.5 us (2%)
  other arithmetic  8.05 us (1%)
    dot_general x32, matrix products, add_block(): jnp.dot(grad_block, table, precision=lax.Precision.HIGHEST, preferred_ele...  323 us
    unnamed x2, waiting for transfers between devices  142 us
    all_to_all x1, waiting for transfers between devices, shards(): lax.all_to_all(local_grads.reshape(owner_count, slice_len), 'proj', split...  28.4 us
    dynamic_slice x32, local copies, waits for them, and re-layouts, add_block(): key_block = lax.dynamic_slice_in_dim(row_keys, first_row, block_rows, 0)  21.9 us
    unnamed x69, local copies, waits for them, and re-layouts  15.3 us
    slice x1, local copies, waits for them, and re-layouts, shards(): gate_up_cotangents[:, 1]  14.1 us
  transfers between devices with their start and end apart: 2, of which 2 were waited for; matrix products, arithmetic and copies ran while one was open for 1% of the time, Pallas kernels for 0%

commit v1 on v0

v1 whole, which is shorter than its diff:
```python
import math

import jax
import jax.numpy as jnp
import numpy as np
from jax import lax
from jax.experimental import pallas as pl
from jax.experimental.pallas import tpu as pltpu
from jax.sharding import PartitionSpec as P

K = 2048
LENGTH = 2048
RANK = 8
ROWS = 256
SEED_MULT = 1103515245
ROW_MULT = 668265263
COL_MULT = -1640531535
MIX_A = -2048144789
MIX_B = -1028477387
STORED_STEPS = (4, 8, 10, 6, 4)

srl = lax.shift_right_logical


def chunk_of(width, unit, limit=4608):
    for parts in range(1, width // unit + 1):
        if width % (parts * unit) == 0 and width // parts <= limit:
            return width // parts
    return width


def wrapped(number):
    return (number + 2**31) % 2**32 - 2**31


def rows_of(parts):
    return jnp.concatenate(parts, axis=0) if len(parts) > 1 else parts[0]


class Plan:
    def __init__(self, widths, tokens, owners):
        self.widths = widths
        self.tokens = tokens
        self.owners = owners
        hid, att, gin, dwn, qry, kvw, aow, guw, dow = widths
        self.pieces = [
            (0, (24, 32, 40), (0, 2, 4), hid),
            (4, (0,), (1,), qry),
            (5, (8, 16), (3, 5), kvw),
            (1, (56,), (6,), att),
            (6, (48,), (7,), aow),
            (2, (80, 88), (8, 10), gin),
            (7, (64, 72), (9, 11), guw),
            (3, (104,), (12,), dwn),
            (8, (96,), (13,), dow),
        ]
        self.block = 0
        for _, _, _, width in self.pieces:
            self.block = math.gcd(self.block, width)
        while self.block > 512:
            self.block //= 2
        seg_tab, off_tab, width_tab = [], [], []
        self.first_block = {}
        for _, _, segs, width in self.pieces:
            for seg in segs:
                self.first_block[seg] = len(seg_tab)
                for number in range(width // self.block):
                    seg_tab.append(seg)
                    off_tab.append(number * self.block)
                    width_tab.append(width)
        self.blocks = len(seg_tab)
        self.table = np.array([seg_tab, off_tab, width_tab], np.int32)
        self.group = LENGTH // tokens
        self.examples = owners // self.group
        self.own_blocks = self.blocks // owners
        self.sub = min(ROWS, self.block)
        self.steps = self.own_blocks * (self.block // self.sub) * RANK
        bits = self.group.bit_length() - 1
        self.bits = ([0, 1] + list(reversed(range(2, bits))))[:bits]

    def first_own(self):
        j = lax.axis_index("proj")
        piece = 0
        for bit in self.bits:
            piece = piece * 2 + ((j >> bit) & 1)
        return piece * (self.blocks // self.group) + (j // self.group) * self.own_blocks


def product_kernel(plan):
    def kernel(*refs):
        data = refs[:9]
        aif, daf, aof, kvb, gub = refs[9:14]
        out = refs[14]
        bufs = refs[15:24]
        pairs = refs[24]
        sems = refs[25]
        order = [(0, lambda c: rows_of([aif[i, :, c] for i in (0, 1, 2)]), (0,)),
                 (4, lambda c: aof[0, :, c], (24,)),
                 (5, lambda c: rows_of([kvb[i, :, c] for i in (0, 1)]), (32, 40)),
                 (1, lambda c: aif[3, :, c], (48,)),
                 (6, lambda c: aof[1, :, c], (56,)),
                 (2, lambda c: rows_of([aif[i, :, c] for i in (4, 5)]), (64,)),
                 (7, lambda c: rows_of([gub[i, :, c] for i in (0, 1)]), (80, 88)),
                 (3, lambda c: daf[:, c], (96,)),
                 (8, lambda c: aof[2, :, c], (104,))]
        copies = []
        for arg, _, _ in order:
            width = plan.widths[arg]
            step = chunk_of(width, plan.block)
            for start in range(0, width, step):
                view = (slice(None),) * (len(data[arg].shape) - 1) + (pl.ds(start, step),)
                copies.append((arg, start, step, pltpu.make_async_copy(
                    data[arg].at[view], bufs[arg].at[view], sems.at[len(copies)])))
        for copy in copies:
            copy[3].start()
        for arg, factor, places in order:
            total = None
            for one, start, step, copy in copies:
                if one != arg:
                    continue
                copy.wait()
                cols = pl.ds(start, step)
                if len(data[arg].shape) == 3:
                    left = bufs[arg][:, :, cols].reshape(2 * plan.tokens, step)
                else:
                    left = bufs[arg][:, cols]
                part = lax.dot_general(left, factor(cols), (((1,), (1,)), ((), ())),
                                       preferred_element_type=jnp.float32)
                total = part if total is None else total + part
            if len(places) == 2:
                pairs[:, 0:2 * RANK] = total
                for i, place in enumerate(places):
                    got = pairs[pl.ds(i, plan.tokens, stride=2), :]
                    out[:, place:place + RANK] = got[:, i * RANK:(i + 1) * RANK]
            else:
                out[:, places[0]:places[0] + total.shape[1]] = total
        out[:, 112:] = jnp.zeros((plan.tokens, 16), jnp.float32)

    return kernel


def copy_count(plan):
    return sum(width // chunk_of(width, plan.block) for width in plan.widths)


def data_buffers(plan, data):
    return [pltpu.VMEM(x.shape, jnp.bfloat16) for x in data]


def products(plan, data, factors):
    anywhere = pl.BlockSpec(memory_space=pl.ANY)
    whole = pl.BlockSpec(memory_space=pltpu.VMEM)
    return pl.pallas_call(
        product_kernel(plan),
        in_specs=[anywhere] * 9 + [whole] * 5,
        out_specs=whole,
        out_shape=jax.ShapeDtypeStruct((plan.tokens, 128), jnp.float32),
        scratch_shapes=data_buffers(plan, data)
        + [pltpu.VMEM((2 * plan.tokens, 128), jnp.float32), pltpu.SemaphoreType.DMA((copy_count(plan),))],
        name="products",
    )(*data, *factors)


def gradient_kernel(plan, split):
    def kernel(*refs):
        data = refs[:9]
        own, other, mask = refs[9:12]
        keep, send = refs[12:14]
        bufs = refs[14:23]
        grads, sems, out_sems = refs[23:26]
        copies = {}
        number = 0
        for arg, _, _, width in plan.pieces:
            step = chunk_of(width, plan.block)
            for start in range(0, width, step):
                view = (slice(None),) * (len(data[arg].shape) - 1) + (pl.ds(start, step),)
                copies[arg, start] = pltpu.make_async_copy(data[arg].at[view], bufs[arg].at[view], sems.at[number])
                number += 1
        for copy in copies.values():
            copy.start()
        total = own[...] + other[...]
        turned = total.T * mask[...].astype(jnp.float32)
        tokens = plan.tokens
        half = plan.blocks // 2
        for arg, places, segs, width in plan.pieces:
            left = rows_of([turned[p:p + RANK] for p in places]).astype(jnp.bfloat16)
            if len(data[arg].shape) == 3:
                t = lax.broadcasted_iota(jnp.int32, (tokens, 2 * tokens), 0)
                u = lax.broadcasted_iota(jnp.int32, (tokens, 2 * tokens), 1)
                parts = []
                for i in range(2):
                    spread = (u == 2 * t + i).astype(jnp.float32).astype(jnp.bfloat16)
                    one = turned[places[i]:places[i] + RANK].astype(jnp.bfloat16)
                    parts.append(jnp.dot(one, spread, preferred_element_type=jnp.float32))
                left = rows_of(parts).astype(jnp.bfloat16)
            step = chunk_of(width, plan.block)
            for start in range(0, width, step):
                copies[arg, start].wait()
                cols = pl.ds(start, step)
                if len(data[arg].shape) == 3:
                    right = bufs[arg][:, :, cols].reshape(2 * tokens, step)
                else:
                    right = bufs[arg][:, cols]
                got = jnp.dot(left, right, preferred_element_type=jnp.float32)
                for i, seg in enumerate(segs):
                    for k in range(step // plan.block):
                        block = plan.first_block[seg] + start // plan.block + k
                        grads[block // half, block % half] = got[
                            i * RANK:(i + 1) * RANK, k * plan.block:(k + 1) * plan.block]
        bit = (lax.axis_index("proj") >> split) & 1
        first = pltpu.make_async_copy(grads.at[1 - bit], send, out_sems.at[0])
        second = pltpu.make_async_copy(grads.at[bit], keep, out_sems.at[1])
        first.start()
        second.start()
        first.wait()
        second.wait()

    return kernel


def gradients(plan, data, own, other, mask, split):
    anywhere = pl.BlockSpec(memory_space=pl.ANY)
    whole = pl.BlockSpec(memory_space=pltpu.VMEM)
    half = jax.ShapeDtypeStruct((plan.blocks // 2, RANK, plan.block), jnp.float32)
    return pl.pallas_call(
        gradient_kernel(plan, split),
        in_specs=[anywhere] * 9 + [whole] * 3,
        out_specs=[anywhere] * 2,
        out_shape=[half, half],
        scratch_shapes=data_buffers(plan, data)
        + [
            pltpu.VMEM((2, plan.blocks // 2, RANK, plan.block), jnp.float32),
            pltpu.SemaphoreType.DMA((copy_count(plan),)),
            pltpu.SemaphoreType.DMA((2,)),
        ],
        name="gradients",
    )(*data, own, other, mask)


def hashed(plan, step, seeds, table, columns):
    number = step // RANK
    rank = step % RANK
    parts = plan.block // plan.sub
    block = plan.first_own() + number // parts
    seg = table[0, block]
    feature = lax.axis_index("mp") * table[2, block] + table[1, block] + (number % parts) * plan.sub
    base = seeds[seg] * SEED_MULT + (feature * RANK + rank) * ROW_MULT
    key = base + lax.broadcasted_iota(jnp.int32, (plan.sub, 1), 0) * wrapped(RANK * ROW_MULT)
    return key ^ srl(key, 16)


def column_keys():
    cols = lax.broadcasted_iota(jnp.int32, (1, K), 1) * COL_MULT
    return cols ^ srl(cols, 16)


def mixed(rows, cols):
    h = (rows ^ cols) * MIX_A
    h = h ^ srl(h, 13)
    return h * MIX_B


def centred_sum(h):
    h = h ^ srl(h, 16)
    s = (h & 0x00FF00FF) + (srl(h, 8) | -0xFF0100)
    return (s * 0x10001).astype(jnp.float32).astype(jnp.bfloat16)


def byte_planes(h):
    low = h.astype(jnp.int16)
    high = srl(h, 16).astype(jnp.int16)
    low = low ^ high
    eight = jnp.int16(8)
    planes = [low, high, srl(low, eight), srl(high, eight)]
    return [p.astype(jnp.uint8).astype(jnp.bfloat16) for p in planes]


COLS = 256


def table_kernel(plan, first):
    def kernel(table, seeds, *refs):
        out = refs[-1]
        step = pl.program_id(0) + first
        columns = column_keys()
        rows = hashed(plan, step, seeds, table, columns)
        for c in range(0, K, COLS):
            out[0, :, c:c + COLS] = centred_sum(mixed(rows, columns[:, c:c + COLS]))

    return kernel


def stored_table(plan, table, seeds, first, count, total, after, so_far):
    smem = pl.BlockSpec(memory_space=pltpu.SMEM)
    anywhere = pl.BlockSpec(memory_space=pl.ANY)
    extra = [after] + ([so_far] if so_far is not None else [])
    return pl.pallas_call(
        table_kernel(plan, first),
        grid=(count,),
        in_specs=[smem, smem] + [anywhere] * len(extra),
        out_specs=pl.BlockSpec((1, plan.sub, K), lambda i: (i + first, 0, 0)),
        out_shape=jax.ShapeDtypeStruct((total, plan.sub, K), jnp.bfloat16),
        input_output_aliases={3: 0} if so_far is not None else {},
        name="stored_table",
    )(table, seeds, *extra)


def project_kernel(plan, stored, scale):
    fresh = plan.steps - stored
    depth = 2 * RANK * plan.examples

    def pick(grads, step):
        rank = step % RANK
        rows = lax.broadcasted_iota(jnp.int32, (RANK, plan.sub), 0) == rank
        parts = []
        for e in range(plan.examples):
            g = jnp.where(rows, grads[e, 0], 0.0)
            top = g.astype(jnp.bfloat16).astype(jnp.float32)
            parts += [top, g - top]
        return rows_of(parts).astype(jnp.bfloat16)

    def kernel(table, seeds, grads, old_grads, tiles, out, acc):
        i = pl.program_id(0)

        @pl.when(i == 0)
        def _():
            acc[...] = jnp.zeros_like(acc)

        columns = column_keys()
        rows = hashed(plan, i + stored, seeds, table, columns)
        left = pick(grads, i + stored)
        fix = -510.0 * jnp.sum(left.astype(jnp.float32), axis=1, keepdims=True)
        old = pick(old_grads, i)
        old = jnp.where(i < stored, old.astype(jnp.float32), 0.0)
        fix = fix + jnp.sum(old, axis=1, keepdims=True)
        old = (old * (1.0 / 65536.0)).astype(jnp.bfloat16)
        for c in range(0, K, COLS):
            a = acc[:, c:c + COLS] + fix
            for plane in byte_planes(mixed(rows, columns[:, c:c + COLS])):
                a = a + jnp.dot(left, plane, preferred_element_type=jnp.float32)
            a = a + jnp.dot(old, tiles[0, :, c:c + COLS], preferred_element_type=jnp.float32)
            acc[:, c:c + COLS] = a

        @pl.when(i == fresh - 1)
        def _():
            for e in range(plan.examples):
                part = acc[e * 2 * RANK:(e + 1) * 2 * RANK, :]
                out[e:e + 1, :] = jnp.sum(part, axis=0, keepdims=True) * scale

    return kernel, depth, fresh


def project(plan, table, seeds, grads, tiles, stored, scale):
    kernel, depth, fresh = project_kernel(plan, stored, scale)
    smem = pl.BlockSpec(memory_space=pltpu.SMEM)
    parts = plan.block // plan.sub

    def place(step):
        number = step // RANK
        return (0, number // parts, 0, number % parts)

    last = stored - 1
    return pl.pallas_call(
        kernel,
        grid=(fresh,),
        in_specs=[
            smem,
            smem,
            pl.BlockSpec((plan.examples, 1, RANK, plan.sub), lambda i: place(i + stored)),
            pl.BlockSpec((plan.examples, 1, RANK, plan.sub), lambda i: place(jnp.minimum(i, last))),
            pl.BlockSpec((1, plan.sub, K), lambda i: (jnp.minimum(i, last), 0, 0)),
        ],
        out_specs=pl.BlockSpec((plan.examples, K), lambda i: (0, 0)),
        out_shape=jax.ShapeDtypeStruct((plan.examples, K), jnp.float32),
        scratch_shapes=[pltpu.VMEM((depth, K), jnp.float32)],
        name="project",
    )(table, seeds, grads, grads, tiles)


def swap(x, axis, bit):
    size = lax.axis_size(axis)
    return lax.ppermute(x, axis, [(i, i ^ (1 << bit)) for i in range(size)])


def shards(*args):
    data = args[:9]
    factors = args[9:14]
    mask, seeds = args[14:16]
    plan = Plan(tuple(x.shape[-1] for x in data), data[0].shape[0], lax.axis_size("proj"))
    table = jnp.asarray(plan.table)
    counts = [max(1, c * plan.steps // 128) for c in STORED_STEPS][:1 + len(plan.bits)]
    stored = sum(counts)
    tiles = None
    first = 0

    def cover(received, sent, number):
        nonlocal tiles, first
        tiles = stored_table(plan, table, seeds, first, counts[number], stored, sent, tiles)
        first += counts[number]
        received, tiles = lax.optimization_barrier((received, tiles))
        return received

    own = products(plan, data, factors)
    if lax.axis_size("mp") == 2:
        other = swap(own, "mp", 0)
    else:
        own = lax.psum(own, "mp")
        other = jnp.zeros_like(own)
    other = cover(other, own, 0)
    keep, send = gradients(plan, data, own, other, mask.reshape(1, -1), plan.bits[0])
    j = lax.axis_index("proj")
    x = None
    for number, bit in enumerate(plan.bits):
        if number > 0:
            half = x.shape[0] // 2
            side = (j >> bit) & 1
            send = lax.dynamic_slice_in_dim(x, (1 - side) * half, half, 0)
            keep = lax.dynamic_slice_in_dim(x, side * half, half, 0)
        received = cover(swap(send, "proj", bit), send, number + 1)
        x = keep + received
    x = x[None]
    if plan.examples > 1:
        groups = [[e * plan.group + i for e in range(plan.examples)] for i in range(plan.group)]
        x = x.reshape((plan.examples, plan.own_blocks) + x.shape[2:])
        x = lax.all_to_all(x, "proj", 0, 0, axis_index_groups=groups, tiled=True)
    scale = 1.0 / (LENGTH * math.sqrt(21845.0 * K))
    partial = project(plan, table, seeds, x, tiles, stored, scale)
    devices = lax.axis_size("mp") * plan.owners
    pieces = partial.reshape(plan.examples, devices, K // devices).transpose(1, 0, 2)
    got = lax.all_to_all(pieces, ("mp", "proj"), 0, 0, tiled=True)
    return got.sum(axis=0)


def solution(mesh):
    in_specs = (
        P("proj", "mp"),
        P("proj", "mp"),
        P("proj", "mp"),
        P("proj", "mp"),
        P("proj", "mp"),
        P("proj", None, "mp"),
        P("proj", "mp"),
        P("proj", None, "mp"),
        P("proj", "mp"),
        P(None, None, "mp"),
        P(None, "mp"),
        P(None, None, "mp"),
        P(None, None, "mp"),
        P(None, None, "mp"),
        P("proj"),
        P(),
    )
    out_specs = P(None, ("mp", "proj"))
    return jax.shard_map(shards, mesh=mesh, in_specs=in_specs, out_specs=out_specs, check_vma=False)
```

time: 657 us -> 208 us (0.32)
  matrix products: 362 us -> 0 us
  Pallas kernels: 0 us -> 178 us
  waiting for transfers between devices: 171 us -> 5.03 us
  local copies, waits for them, and re-layouts: 72.7 us -> 1.3 us
  between operations: 22.5 us -> 0.12 us
    dot_general x60 -> x0, matrix products: 362 us -> none  [the longest x32 323 us: add_block(): jnp.dot(grad_block, table, precision=lax.Precision.HIGHEST, preferred_ele...]
    pallas_call x0 -> x8, Pallas kernels: none -> 178 us  [the longest x1 117 us: project(): pl.pallas_call(kernel, grid=(fresh,), in_specs=[smem, smem, pl.BlockSpec(...]
    unnamed x2 -> x0, waiting for transfers between devices: 142 us -> none
    all_to_all x1 -> x0, waiting for transfers between devices: 28.4 us -> none  [shards(): lax.all_to_all(local_grads.reshape(owner_count, slice_len), 'proj', split...]
    dynamic_slice x32 -> x3, local copies, waits for them, and re-layouts: 21.9 us -> 0.09 us  [shards(): send = lax.dynamic_slice_in_dim(x, (1 - side) * half, half, 0)]
    reshape x12 -> x0, local copies, waits for them, and re-layouts: 19.1 us -> none  [the longest x7 10.9 us: shards(): flat_parts.append(grad_a.reshape(-1))]
    slice x3 -> x0, local copies, waits for them, and re-layouts: 16.4 us -> none  [the longest x1 14.1 us: shards(): gate_up_cotangents[:, 1]]
    unnamed x69 -> x10, local copies, waits for them, and re-layouts: 15.3 us -> 0.63 us
  transfers between devices with their start and end apart: 2 -> 5, of which waited for: 2 -> 2; matrix products, arithmetic and copies ran while one was open for 1% -> 0% of each run, Pallas kernels for 0% -> 20%
where the time goes in v1:
time: 208 us; the launch traced here: 207 us
  Pallas kernels  178 us (86%)
  blocking collectives  11.7 us (6%)
  starting transfers between devices  8.09 us (4%)
  waiting for transfers between devices  5.03 us (2%)
  other arithmetic  2.91 us (1%)
    pallas_call x1, Pallas kernels, project(): pl.pallas_call(kernel, grid=(fresh,), in_specs=[smem, smem, pl.BlockSpec(...  117 us
    pallas_call x5, Pallas kernels, stored_table(): pl.pallas_call(table_kernel(plan, first), grid=(count,), in_specs=[smem,...  40.7 us
    pallas_call x1, Pallas kernels, products(): pl.pallas_call(product_kernel(plan), in_specs=[anywhere] * 9 + [whole] *...  12.2 us
    all_to_all x1, blocking collectives, shards(): got = lax.all_to_all(pieces, ('mp', 'proj'), 0, 0, tiled=True)  11.7 us
    ppermute x5, starting transfers between devices, swap(): return lax.ppermute(x, axis, [(i, i ^ 1 << bit) for i in range(size)])  8.09 us
    pallas_call x1, Pallas kernels, gradients(): pl.pallas_call(gradient_kernel(plan, split), in_specs=[anywhere] * 9 + [w...  7.9 us
    ppermute x5, waiting for transfers between devices, swap(): return lax.ppermute(x, axis, [(i, i ^ 1 << bit) for i in range(size)])  5.03 us
  transfers between devices with their start and end apart: 5, of which 2 were waited for; matrix products, arithmetic and copies ran while one was open for 0% of the time, Pallas kernels for 20%

profile of v1, /device:TPU:0, one launch (start us, length us, event | category | flops | bytes accessed | tf_op | source)
XLA Modules:
  0.0 207.0 jit_solution(10147318072433718164)
XLA Ops:
  0.0 12.2 %products.1.refs_0_.refs_9_ = f32[128,128]{1,0:T(8,128)} custom-call(bf16[128,2560]{1,0:T(8,128)(2,1)} %refs_0_.3, bf16[128,2560]{1,0:T(8,128)(2,1)} %refs_1_.3, bf16[128,2560]{1,0:T(8,128)(2,1)} %refs_2_.3, bf16[128,13824]{1,0:T(8,128)(2,1)} %refs_3_.3, bf16[128,2560]{1,0:T(8,128)(2,1)} %refs_4_.3, bf16[128,2,512]{2,1,0:T(2,128)(2,1)} %refs_5_.3, ...), custom_call_target="tpu_custom_call" | custom-call | tf_op jit(solution)/shard_map/products/pallas_call | solution.py:153
  12.2 3.0 %collective-permute-start = (f32[128,128]{1,0:T(8,128)}, f32[128,128]{1,0:T(8,128)S(1)}, u32[]{:S(2)}, u32[]{:S(2)}) collective-permute-start(f32[128,128]{1,0:T(8,128)} %products.1.refs_0_.refs_9_), channel_id=1, source_target_pairs={{0,16},{16,0},{1,17},{17,1},{2,18},{18,2},{3,19},{19,3},{4,20},{20... | collective-permute-start | bytes 196616 | tf_op jit(solution)/shard_map/ppermute | solution.py:382
  15.3 5.7 %stored_table.5.refs_1_ = bf16[32,256,2048]{2,1,0:T(8,128)(2,1)} custom-call(s32[3,128]{1,0:T(4,128)} %constant.24.clone.table, s32[14]{0:T(128)} %seeds.11, f32[128,128]{1,0:T(8,128)} %products.1.refs_0_.refs_9_), custom_call_target="tpu_custom_call" | custom-call | tf_op jit(solution)/shard_map/stored_table/pallas_call | solution.py:297
  20.9 0.0 collective-permute-done.refs_10_
  20.9 0.0 copy-start.4
  20.9 0.6 copy-done.4
  21.6 7.9 %gradients.1 = (f32[64,8,512]{2,1,0:T(8,128)}, f32[64,8,512]{2,1,0:T(8,128)}) custom-call(bf16[128,2560]{1,0:T(8,128)(2,1)} %refs_0_.3, bf16[128,2560]{1,0:T(8,128)(2,1)} %refs_1_.3, bf16[128,2560]{1,0:T(8,128)(2,1)} %refs_2_.3, bf16[128,13824]{1,0:T(8,128)(2,1)} %refs_3_.3, bf16[128,2560]{1,0:T(8,128)(2,1)} %refs_4_.3, bf16[128,2,512]{2,1,0:T(2,128)(2,1)} %refs_5_.3, ...), custom_call_target="tpu_custom_call" | custom-call | tf_op jit(solution)/shard_map/gradients/pallas_call | solution.py:225
  29.5 0.1 collective-permute-start.1
  29.6 0.0 copy-start.2
  29.6 9.9 %stored_table.6.refs_1_ = bf16[32,256,2048]{2,1,0:T(8,128)(2,1)} custom-call(s32[3,128]{1,0:T(4,128)} %constant.24.clone.table, s32[14]{0:T(128)} %seeds.11, f32[64,8,512]{2,1,0:T(8,128)} %get-tuple-element.19.refs_0_, bf16[32,256,2048]{2,1,0:T(8,128)(2,1)} %stored_table.5.refs_1_), custom_call_target="tpu_custom_call", output_to_operand_aliasing={{}: (3, {})} | custom-call | tf_op jit(solution)/shard_map/stored_table/pallas_call | solution.py:297
  39.4 0.0 collective-permute-done.1
  39.5 0.0 copy-done.2
  39.5 0.2 add.30
  39.7 0.0 copy-start
  39.7 1.6 collective-permute-start.2
  41.3 0.0 copy-done
  41.3 11.7 %stored_table.7.refs_1_ = bf16[32,256,2048]{2,1,0:T(8,128)(2,1)} custom-call(s32[3,128]{1,0:T(4,128)} %constant.24.clone.table, s32[14]{0:T(128)} %seeds.11, f32[32,8,512]{2,1,0:T(8,128)} %copy-done, bf16[32,256,2048]{2,1,0:T(8,128)(2,1)} %stored_table.6.refs_1_), custom_call_target="tpu_custom_call", output_to_operand_aliasing={{}: (3, {})} | custom-call | tf_op jit(solution)/shard_map/stored_table/pallas_call | solution.py:297
  53.1 1.0 collective-permute-done.2
  54.1 0.1 dynamic-slice_add_fusion
  54.2 0.0 copy-start.1
  54.2 2.7 %collective-permute-start.3 = (f32[16,8,512]{2,1,0:T(8,128)S(1)}, f32[16,8,512]{2,1,0:T(8,128)S(1)}, u32[]{:S(2)}, u32[]{:S(2)}) collective-permute-start(f32[16,8,512]{2,1,0:T(8,128)S(1)} %constant_dynamic-slice_fusion.1.refs_0_), channel_id=1, source_target_pairs={{0,8},{1,9},{2,10},{3,11},{4,12},{5,13},{6,14},{7,15},{8,0},{9,1},... | collective-permute-start | bytes 786440 | tf_op jit(solution)/shard_map/ppermute | solution.py:382
  56.9 0.0 copy-done.1
  56.9 7.7 %stored_table.8.refs_1_ = bf16[32,256,2048]{2,1,0:T(8,128)(2,1)} custom-call(s32[3,128]{1,0:T(4,128)} %constant.24.clone.table, s32[14]{0:T(128)} %seeds.11, f32[16,8,512]{2,1,0:T(8,128)} %copy-done.1, bf16[32,256,2048]{2,1,0:T(8,128)(2,1)} %stored_table.7.refs_1_), custom_call_target="tpu_custom_call", output_to_operand_aliasing={{}: (3, {})} | custom-call | tf_op jit(solution)/shard_map/stored_table/pallas_call | solution.py:297
  64.6 4.0 %collective-permute-done.3 = f32[16,8,512]{2,1,0:T(8,128)S(1)} collective-permute-done((f32[16,8,512]{2,1,0:T(8,128)S(1)}, f32[16,8,512]{2,1,0:T(8,128)S(1)}, u32[]{:S(2)}, u32[]{:S(2)}) %collective-permute-start.3) | collective-permute-done | bytes 262176 | tf_op jit(solution)/shard_map/ppermute | solution.py:382
  68.7 0.0 copy-start.3
  68.7 0.7 collective-permute-start.4
  69.4 0.0 copy-done.3
  69.4 5.7 %stored_table.9.tiles = bf16[32,256,2048]{2,1,0:T(8,128)(2,1)} custom-call(s32[3,128]{1,0:T(4,128)} %constant.24.clone.table, s32[14]{0:T(128)} %seeds.11, f32[8,8,512]{2,1,0:T(8,128)} %copy-done.3, bf16[32,256,2048]{2,1,0:T(8,128)(2,1)} %stored_table.8.refs_1_), custom_call_target="tpu_custom_call", output_to_operand_aliasing={{}: (3, {})} | custom-call | tf_op jit(solution)/shard_map/stored_table/pallas_call | solution.py:297
  75.1 0.0 collective-permute-done.4
  75.1 0.7 add_bitcast_fusion.grads.old_grads
  75.8 117.1 %project.1 = f32[1,2048]{1,0:T(1,128)} custom-call(s32[3,128]{1,0:T(4,128)} %constant.24.clone.table, s32[14]{0:T(128)} %seeds.11, f32[1,8,8,512]{3,2,1,0:T(8,128)} %add_bitcast_fusion.grads.old_grads, f32[1,8,8,512]{3,2,1,0:T(8,128)} %add_bitcast_fusion.grads.old_grads, bf16[32,256,2048]{2,1,0:T(8,128)(2,1)} %stored_table.9.tiles), custom_call_target="tpu_custom_call" | custom-call | tf_op jit(solution)/shard_map/project/pallas_call | solution.py:363
  192.8 0.5 broadcast.3
  193.3 1.4 reduce.4
  194.7 0.1 transpose_reshape.3
  194.8 11.7 %all_to_all.5 = f32[32,1,64]{2,1,0:T(1,128)S(1)} all-to-all(f32[32,1,64]{2,1,0:T(1,128)S(1)} %bitcast.5), channel_id=1, replica_groups=mesh['mp'=2,'proj'=16] {'mp','proj'}, dimensions={0} | all-to-all | bytes 16384 | tf_op jit(solution)/shard_map/all_to_all | solution.py:430
  206.5 0.6 reduce_sum.11
  (4 shorter events, 0.1 us)
Async XLA Ops:
  12.2 8.7 %collective-permute-start = (f32[128,128]{1,0:T(8,128)}, f32[128,128]{1,0:T(8,128)S(1)}, u32[]{:S(2)}, u32[]{:S(2)}) collective-permute-start(f32[128,128]{1,0:T(8,128)} %products.1.refs_0_.refs_9_), channel_id=1, source_target_pairs={{0,16},{16,0},{1,17},{17,1},{2,18},{18,2},{3,19},{19,3},{4,20},{20... | collective-permute-start | bytes 196616 | tf_op jit(solution)/shard_map/ppermute | solution.py:382
  20.9 0.6 copy-start.4
  29.5 10.0 %collective-permute-start.1 = (f32[64,8,512]{2,1,0:T(8,128)}, f32[64,8,512]{2,1,0:T(8,128)S(1)}, u32[]{:S(2)}, u32[]{:S(2)}) collective-permute-start(f32[64,8,512]{2,1,0:T(8,128)} %get-tuple-element.19.refs_0_), channel_id=1, source_target_pairs={{0,1},{1,0},{2,3},{3,2},{4,5},{5,4},{6,7},{7,6},{8,9},{9,8},{10,11... | collective-permute-start | bytes 3145736 | tf_op jit(solution)/shard_map/ppermute | solution.py:382
  29.6 9.9 %copy-start.2 = (f32[64,8,512]{2,1,0:T(8,128)S(1)}, f32[64,8,512]{2,1,0:T(8,128)}, u32[]{:S(2)}) copy-start(f32[64,8,512]{2,1,0:T(8,128)} %get-tuple-element.18) | copy-start | bytes 3145732
  39.7 1.6 copy-start
  39.7 14.3 %collective-permute-start.2 = (f32[32,8,512]{2,1,0:T(8,128)S(1)}, f32[32,8,512]{2,1,0:T(8,128)S(1)}, u32[]{:S(2)}, u32[]{:S(2)}) collective-permute-start(f32[32,8,512]{2,1,0:T(8,128)S(1)} %constant_dynamic-slice_fusion.2.refs_0_), channel_id=1, source_target_pairs={{0,2},{1,3},{2,0},{3,1},{4,6},{5,7},{6,4},{7,5},{8,10},{9,11},{10,... | collective-permute-start | bytes 1572872 | tf_op jit(solution)/shard_map/ppermute | solution.py:382
  54.2 2.7 %copy-start.1 = (f32[16,8,512]{2,1,0:T(8,128)}, f32[16,8,512]{2,1,0:T(8,128)S(1)}, u32[]{:S(2)}) copy-start(f32[16,8,512]{2,1,0:T(8,128)S(1)} %constant_dynamic-slice_fusion.1.refs_0_) | copy-start | bytes 786436
  54.2 14.4 %collective-permute-start.3 = (f32[16,8,512]{2,1,0:T(8,128)S(1)}, f32[16,8,512]{2,1,0:T(8,128)S(1)}, u32[]{:S(2)}, u32[]{:S(2)}) collective-permute-start(f32[16,8,512]{2,1,0:T(8,128)S(1)} %constant_dynamic-slice_fusion.1.refs_0_), channel_id=1, source_target_pairs={{0,8},{1,9},{2,10},{3,11},{4,12},{5,13},{6,14},{7,15},{8,0},{9,1},... | collective-permute-start | bytes 786440 | tf_op jit(solution)/shard_map/ppermute | solution.py:382
  68.7 0.8 copy-start.3
  68.7 6.4 %collective-permute-start.4 = (f32[8,8,512]{2,1,0:T(8,128)S(1)}, f32[8,8,512]{2,1,0:T(8,128)S(1)}, u32[]{:S(2)}, u32[]{:S(2)}) collective-permute-start(f32[8,8,512]{2,1,0:T(8,128)S(1)} %constant_dynamic-slice_fusion.refs_0_), channel_id=1, source_target_pairs={{0,4},{1,5},{2,6},{3,7},{4,0},{5,1},{6,2},{7,3},{8,12},{9,13},{10,... | collective-permute-start | bytes 393224 | tf_op jit(solution)/shard_map/ppermute | solution.py:382

commit v2 on v1

--- a/solution.py
+++ b/solution.py
@@ -17,7 +17,7 @@
 COL_MULT = -1640531535
 MIX_A = -2048144789
 MIX_B = -1028477387
-STORED_STEPS = (4, 8, 10, 6, 4)
+STORED_STEPS = (6, 3, 5, 6, 10, 7, 3)
 
 srl = lax.shift_right_logical
 
@@ -86,14 +86,17 @@
         return piece * (self.blocks // self.group) + (j // self.group) * self.own_blocks
 
 
-def product_kernel(plan):
+def product_kernel(plan, count):
     def kernel(*refs):
         data = refs[:9]
-        aif, daf, aof, kvb, gub = refs[9:14]
-        out = refs[14]
-        bufs = refs[15:24]
-        pairs = refs[24]
-        sems = refs[25]
+        weights = refs[9:14]
+        fill_refs = refs[14:16]
+        out, tiles = refs[16:18]
+        bufs = refs[18:27]
+        pairs, sems = refs[27:29]
+        factor_bufs = refs[29:34]
+        aif, daf, aof, kvb, gub = factor_bufs
+        fill_refs = fill_refs + refs[34:]
         order = [(0, lambda c: rows_of([aif[i, :, c] for i in (0, 1, 2)]), (0,)),
                  (4, lambda c: aof[0, :, c], (24,)),
                  (5, lambda c: rows_of([kvb[i, :, c] for i in (0, 1)]), (32, 40)),
@@ -111,8 +114,12 @@
                 view = (slice(None),) * (len(data[arg].shape) - 1) + (pl.ds(start, step),)
                 copies.append((arg, start, step, pltpu.make_async_copy(
                     data[arg].at[view], bufs[arg].at[view], sems.at[len(copies)])))
-        for copy in copies:
-            copy[3].start()
+        loads = [pltpu.make_async_copy(weights[i], factor_bufs[i], sems.at[len(copies) + i]) for i in range(5)]
+        for copy in loads + [copy[3] for copy in copies]:
+            copy.start()
+        finish = fill_tables(plan, 0, count, fill_refs, tiles)
+        for load in loads:
+            load.wait()
         for arg, factor, places in order:
             total = None
             for one, start, step, copy in copies:
@@ -135,6 +142,7 @@
             else:
                 out[:, places[0]:places[0] + total.shape[1]] = total
         out[:, 112:] = jnp.zeros((plan.tokens, 16), jnp.float32)
+        finish()
 
     return kernel
 
@@ -147,27 +155,32 @@
     return [pltpu.VMEM(x.shape, jnp.bfloat16) for x in data]
 
 
-def products(plan, data, factors):
+def products(plan, data, factors, table, seeds, count, total):
     anywhere = pl.BlockSpec(memory_space=pl.ANY)
+    smem = pl.BlockSpec(memory_space=pltpu.SMEM)
     whole = pl.BlockSpec(memory_space=pltpu.VMEM)
     return pl.pallas_call(
-        product_kernel(plan),
-        in_specs=[anywhere] * 9 + [whole] * 5,
-        out_specs=whole,
-        out_shape=jax.ShapeDtypeStruct((plan.tokens, 128), jnp.float32),
+        product_kernel(plan, count),
+        in_specs=[anywhere] * 14 + [smem, smem],
+        out_specs=[whole, anywhere],
+        out_shape=[jax.ShapeDtypeStruct((plan.tokens, 128), jnp.float32), tiles_shape(plan, total)],
         scratch_shapes=data_buffers(plan, data)
-        + [pltpu.VMEM((2 * plan.tokens, 128), jnp.float32), pltpu.SemaphoreType.DMA((copy_count(plan),))],
+        + [pltpu.VMEM((2 * plan.tokens, 128), jnp.float32), pltpu.SemaphoreType.DMA((copy_count(plan) + 5,))]
+        + [pltpu.VMEM(x.shape, x.dtype) for x in factors]
+        + fill_scratch(plan, count),
         name="products",
-    )(*data, *factors)
-
-
-def gradient_kernel(plan, split):
+    )(*data, *factors, table, seeds)
+
+
+def gradient_kernel(plan, split, first, count):
     def kernel(*refs):
         data = refs[:9]
         own, other, mask = refs[9:12]
-        keep, send = refs[12:14]
-        bufs = refs[14:23]
-        grads, sems, out_sems = refs[23:26]
+        fill_refs = refs[12:14]
+        keep, send, tiles = refs[15:18]
+        bufs = refs[18:27]
+        grads, sems, out_sems = refs[27:30]
+        fill_refs = fill_refs + refs[30:]
         copies = {}
         number = 0
         for arg, _, _, width in plan.pieces:
@@ -178,6 +191,7 @@
                 number += 1
         for copy in copies.values():
             copy.start()
+        finish = fill_tables(plan, first, count, fill_refs, tiles)
         total = own[...] + other[...]
         turned = total.T * mask[...].astype(jnp.float32)
         tokens = plan.tokens
@@ -208,36 +222,44 @@
                         grads[block // half, block % half] = got[
                             i * RANK:(i + 1) * RANK, k * plan.block:(k + 1) * plan.block]
         bit = (lax.axis_index("proj") >> split) & 1
-        first = pltpu.make_async_copy(grads.at[1 - bit], send, out_sems.at[0])
-        second = pltpu.make_async_copy(grads.at[bit], keep, out_sems.at[1])
-        first.start()
-        second.start()
-        first.wait()
-        second.wait()
+        sent = pltpu.make_async_copy(grads.at[1 - bit], send, out_sems.at[0])
+        kept = pltpu.make_async_copy(grads.at[bit], keep, out_sems.at[1])
+        sent.start()
+        kept.start()
+        finish()
+        sent.wait()
+        kept.wait()
 
     return kernel
 
 
-def gradients(plan, data, own, other, mask, split):
+def gradients(plan, data, own, other, mask, split, table, seeds, first, count, so_far):
     anywhere = pl.BlockSpec(memory_space=pl.ANY)
+    smem = pl.BlockSpec(memory_space=pltpu.SMEM)
     whole = pl.BlockSpec(memory_space=pltpu.VMEM)
     half = jax.ShapeDtypeStruct((plan.blocks // 2, RANK, plan.block), jnp.float32)
     return pl.pallas_call(
-        gradient_kernel(plan, split),
-        in_specs=[anywhere] * 9 + [whole] * 3,
-        out_specs=[anywhere] * 2,
-        out_shape=[half, half],
+        gradient_kernel(plan, split, first, count),
+        in_specs=[anywhere] * 9 + [whole] * 3 + [smem, smem, anywhere],
+        out_specs=[anywhere] * 3,
+        out_shape=[half, half, jax.ShapeDtypeStruct(so_far.shape, so_far.dtype)],
         scratch_shapes=data_buffers(plan, data)
         + [
             pltpu.VMEM((2, plan.blocks // 2, RANK, plan.block), jnp.float32),
             pltpu.SemaphoreType.DMA((copy_count(plan),)),
             pltpu.SemaphoreType.DMA((2,)),
-        ],
+        ]
+        + fill_scratch(plan, count),
+        input_output_aliases={14: 2},
         name="gradients",
-    )(*data, own, other, mask)
-
-
-def hashed(plan, step, seeds, table, columns):
+    )(*data, own, other, mask, table, seeds, so_far)
+
+
+def row_offsets(plan):
+    return lax.broadcasted_iota(jnp.int32, (plan.sub, COLS), 0) * wrapped(RANK * ROW_MULT)
+
+
+def step_keys(plan, step, seeds, table, offsets):
     number = step // RANK
     rank = step % RANK
     parts = plan.block // plan.sub
@@ -245,17 +267,19 @@
     seg = table[0, block]
     feature = lax.axis_index("mp") * table[2, block] + table[1, block] + (number % parts) * plan.sub
     base = seeds[seg] * SEED_MULT + (feature * RANK + rank) * ROW_MULT
-    key = base + lax.broadcasted_iota(jnp.int32, (plan.sub, 1), 0) * wrapped(RANK * ROW_MULT)
+    key = base + offsets
     return key ^ srl(key, 16)
 
 
-def column_keys():
-    cols = lax.broadcasted_iota(jnp.int32, (1, K), 1) * COL_MULT
+def column_keys(copies=1):
+    cols = lax.broadcasted_iota(jnp.int32, (copies, K), 1) * COL_MULT
     return cols ^ srl(cols, 16)
 
 
 def mixed(rows, cols):
-    h = (rows ^ cols) * MIX_A
+    shape = rows.shape[0], cols.shape[1]
+    h = rows.reshape(shape[0] // RANK, RANK, rows.shape[1]) ^ cols[None]
+    h = h.reshape(shape) * MIX_A
     h = h ^ srl(h, 13)
     return h * MIX_B
 
@@ -276,38 +300,72 @@
 
 
 COLS = 256
-
-
-def table_kernel(plan, first):
-    def kernel(table, seeds, *refs):
-        out = refs[-1]
-        step = pl.program_id(0) + first
-        columns = column_keys()
-        rows = hashed(plan, step, seeds, table, columns)
-        for c in range(0, K, COLS):
-            out[0, :, c:c + COLS] = centred_sum(mixed(rows, columns[:, c:c + COLS]))
-
-    return kernel
-
-
-def stored_table(plan, table, seeds, first, count, total, after, so_far):
+LANES = 128
+
+
+def fill_step(plan, step, seeds, table, row_base, col_base, tile):
+    rows = step_keys(plan, step, seeds, table, row_base[...])
+    for c in range(0, K, COLS):
+        part = centred_sum(mixed(rows, col_base[:, c:c + COLS]))
+        for n in range(0, COLS, LANES):
+            tile[(c + n) // LANES] = part[:, n:n + LANES]
+
+
+def fill_tables(plan, first, count, refs, out):
+    table, seeds, row_base, col_base, tiles, sems = refs
+    row_base[...] = row_offsets(plan)
+    col_base[...] = column_keys(RANK)
+
+    def body(n, carry):
+        fill_step(plan, n + first, seeds, table, row_base, col_base, tiles.at[n])
+        pltpu.make_async_copy(tiles.at[n], out.at[n + first], sems.at[n]).start()
+        return carry
+
+    lax.fori_loop(0, count, body, 0)
+
+    def wait():
+        for n in range(count):
+            pltpu.make_async_copy(tiles.at[n], out.at[n + first], sems.at[n]).wait()
+
+    return wait
+
+
+def fill_scratch(plan, count):
+    return [
+        pltpu.VMEM((plan.sub, COLS), jnp.int32),
+        pltpu.VMEM((RANK, K), jnp.int32),
+        pltpu.VMEM((count, K // LANES, plan.sub, LANES), jnp.bfloat16),
+        pltpu.SemaphoreType.DMA((count,)),
+    ]
+
+
+def tiles_shape(plan, total):
+    return jax.ShapeDtypeStruct((total, K // LANES, plan.sub, LANES), jnp.bfloat16)
+
+
+def stored_table(plan, table, seeds, first, count, after, so_far):
     smem = pl.BlockSpec(memory_space=pltpu.SMEM)
     anywhere = pl.BlockSpec(memory_space=pl.ANY)
-    extra = [after] + ([so_far] if so_far is not None else [])
+
+    def kernel(table, seeds, after, so_far, out, *scratch):
+        fill_tables(plan, first, count, (table, seeds) + scratch, out)()
+
     return pl.pallas_call(
-        table_kernel(plan, first),
-        grid=(count,),
-        in_specs=[smem, smem] + [anywhere] * len(extra),
-        out_specs=pl.BlockSpec((1, plan.sub, K), lambda i: (i + first, 0, 0)),
-        out_shape=jax.ShapeDtypeStruct((total, plan.sub, K), jnp.bfloat16),
-        input_output_aliases={3: 0} if so_far is not None else {},
+        kernel,
+        in_specs=[smem, smem, anywhere, anywhere],
+        out_specs=anywhere,
+        out_shape=jax.ShapeDtypeStruct(so_far.shape, so_far.dtype),
+        scratch_shapes=fill_scratch(plan, count),
+        input_output_aliases={3: 0},
         name="stored_table",
-    )(table, seeds, *extra)
-
-
-def project_kernel(plan, stored, scale):
+    )(table, seeds, after, so_far)
+
+
+def project_kernel(plan, stored, scale, devices):
     fresh = plan.steps - stored
     depth = 2 * RANK * plan.examples
+    parts = 4
+    slab = plan.sub // parts
 
     def pick(grads, step):
         rank = step % RANK
@@ -319,39 +377,46 @@
             parts += [top, g - top]
         return rows_of(parts).astype(jnp.bfloat16)
 
-    def kernel(table, seeds, grads, old_grads, tiles, out, acc):
+    def kernel(table, seeds, grads, old_grads, tiles, out, acc, row_base, col_base):
         i = pl.program_id(0)
 
         @pl.when(i == 0)
         def _():
             acc[...] = jnp.zeros_like(acc)
-
-        columns = column_keys()
-        rows = hashed(plan, i + stored, seeds, table, columns)
+            row_base[...] = row_offsets(plan)
+            col_base[...] = column_keys(RANK)
+
+        rows = step_keys(plan, i + stored, seeds, table, row_base[...])
         left = pick(grads, i + stored)
         fix = -510.0 * jnp.sum(left.astype(jnp.float32), axis=1, keepdims=True)
         old = pick(old_grads, i)
         old = jnp.where(i < stored, old.astype(jnp.float32), 0.0)
         fix = fix + jnp.sum(old, axis=1, keepdims=True)
         old = (old * (1.0 / 65536.0)).astype(jnp.bfloat16)
+        lefts = [jnp.concatenate([left[:, b:b + slab]] * parts, axis=1) for b in range(0, plan.sub, slab)]
         for c in range(0, K, COLS):
             a = acc[:, c:c + COLS] + fix
-            for plane in byte_planes(mixed(rows, columns[:, c:c + COLS])):
-                a = a + jnp.dot(left, plane, preferred_element_type=jnp.float32)
-            a = a + jnp.dot(old, tiles[0, :, c:c + COLS], preferred_element_type=jnp.float32)
+            for n in range(parts):
+                planes = byte_planes(mixed(rows[n * slab:(n + 1) * slab], col_base[:, c:c + COLS]))
+                a = a + jnp.dot(lefts[n], rows_of(planes), preferred_element_type=jnp.float32)
+            tile = jnp.concatenate([tiles[0, (c + n) // LANES] for n in range(0, COLS, LANES)], axis=1)
+            a = a + jnp.dot(old, tile, preferred_element_type=jnp.float32)
             acc[:, c:c + COLS] = a
 
         @pl.when(i == fresh - 1)
         def _():
+            width = K // devices
             for e in range(plan.examples):
                 part = acc[e * 2 * RANK:(e + 1) * 2 * RANK, :]
-                out[e:e + 1, :] = jnp.sum(part, axis=0, keepdims=True) * scale
+                total = jnp.sum(part, axis=0, keepdims=True) * scale
+                for d in range(devices):
+                    out[d, e:e + 1, :] = total[:, d * width:(d + 1) * width]
 
     return kernel, depth, fresh
 
 
-def project(plan, table, seeds, grads, tiles, stored, scale):
-    kernel, depth, fresh = project_kernel(plan, stored, scale)
+def project(plan, table, seeds, grads, tiles, stored, scale, devices):
+    kernel, depth, fresh = project_kernel(plan, stored, scale, devices)
     smem = pl.BlockSpec(memory_space=pltpu.SMEM)
     parts = plan.block // plan.sub
 
@@ -368,11 +433,15 @@
             smem,
             pl.BlockSpec((plan.examples, 1, RANK, plan.sub), lambda i: place(i + stored)),
             pl.BlockSpec((plan.examples, 1, RANK, plan.sub), lambda i: place(jnp.minimum(i, last))),
-            pl.BlockSpec((1, plan.sub, K), lambda i: (jnp.minimum(i, last), 0, 0)),
+            pl.BlockSpec((1, K // LANES, plan.sub, LANES), lambda i: (jnp.minimum(i, last), 0, 0, 0)),
         ],
-        out_specs=pl.BlockSpec((plan.examples, K), lambda i: (0, 0)),
-        out_shape=jax.ShapeDtypeStruct((plan.examples, K), jnp.float32),
-        scratch_shapes=[pltpu.VMEM((depth, K), jnp.float32)],
+        out_specs=pl.BlockSpec((devices, plan.examples, K // devices), lambda i: (0, 0, 0)),
+        out_shape=jax.ShapeDtypeStruct((devices, plan.examples, K // devices), jnp.float32),
+        scratch_shapes=[
+            pltpu.VMEM((depth, K), jnp.float32),
+            pltpu.VMEM((plan.sub, COLS), jnp.int32),
+            pltpu.VMEM((RANK, K), jnp.int32),
+        ],
         name="project",
     )(table, seeds, grads, grads, tiles)
 
@@ -388,26 +457,25 @@
     mask, seeds = args[14:16]
     plan = Plan(tuple(x.shape[-1] for x in data), data[0].shape[0], lax.axis_size("proj"))
     table = jnp.asarray(plan.table)
-    counts = [max(1, c * plan.steps // 128) for c in STORED_STEPS][:1 + len(plan.bits)]
+    counts = [max(1, c * plan.steps // 128) for c in STORED_STEPS][:3 + len(plan.bits)]
+    starts = [sum(counts[:n]) for n in range(len(counts))]
     stored = sum(counts)
-    tiles = None
-    first = 0
+    own, tiles = products(plan, data, factors, table, seeds, counts[0], stored)
 
     def cover(received, sent, number):
-        nonlocal tiles, first
-        tiles = stored_table(plan, table, seeds, first, counts[number], stored, sent, tiles)
-        first += counts[number]
+        nonlocal tiles
+        tiles = stored_table(plan, table, seeds, starts[number], counts[number], sent, tiles)
         received, tiles = lax.optimization_barrier((received, tiles))
         return received
 
-    own = products(plan, data, factors)
     if lax.axis_size("mp") == 2:
         other = swap(own, "mp", 0)
     else:
         own = lax.psum(own, "mp")
         other = jnp.zeros_like(own)
-    other = cover(other, own, 0)
-    keep, send = gradients(plan, data, own, other, mask.reshape(1, -1), plan.bits[0])
+    other = cover(other, own, 1)
+    keep, send, tiles = gradients(
+        plan, data, own, other, mask.reshape(1, -1), plan.bits[0], table, seeds, starts[2], counts[2], tiles)
     j = lax.axis_index("proj")
     x = None
     for number, bit in enumerate(plan.bits):
@@ -416,7 +484,7 @@
             side = (j >> bit) & 1
             send = lax.dynamic_slice_in_dim(x, (1 - side) * half, half, 0)
             keep = lax.dynamic_slice_in_dim(x, side * half, half, 0)
-        received = cover(swap(send, "proj", bit), send, number + 1)
+        received = cover(swap(send, "proj", bit), send, number + 3)
         x = keep + received
     x = x[None]
     if plan.examples > 1:
@@ -424,9 +492,8 @@
         x = x.reshape((plan.examples, plan.own_blocks) + x.shape[2:])
         x = lax.all_to_all(x, "proj", 0, 0, axis_index_groups=groups, tiled=True)
     scale = 1.0 / (LENGTH * math.sqrt(21845.0 * K))
-    partial = project(plan, table, seeds, x, tiles, stored, scale)
     devices = lax.axis_size("mp") * plan.owners
-    pieces = partial.reshape(plan.examples, devices, K // devices).transpose(1, 0, 2)
+    pieces = project(plan, table, seeds, x, tiles, stored, scale, devices)
     got = lax.all_to_all(pieces, ("mp", "proj"), 0, 0, tiled=True)
     return got.sum(axis=0)
 

time: 208 us -> 197 us (0.947)
  Pallas kernels: 178 us -> 170 us
    pallas_call x1, Pallas kernels: 117 us -> 103 us  [project(): pl.pallas_call(kernel, grid=(fresh,), in_specs=[smem, smem, pl.BlockSpec(...]
    pallas_call x7, Pallas kernels: 60.8 us -> 66.7 us  [the longest x5 38.7 us: stored_table(): pl.pallas_call(kernel, in_specs=[smem, smem, anywhere, anywhere], out_spe...]
where the time goes in v2:
time: 197 us; the launch traced here: 196 us
  Pallas kernels  170 us (86%)
  blocking collectives  11.9 us (6%)
  starting transfers between devices  8.08 us (4%)
  waiting for transfers between devices  3.47 us (2%)
    pallas_call x1, Pallas kernels, project(): pl.pallas_call(kernel, grid=(fresh,), in_specs=[smem, smem, pl.BlockSpec(...  103 us
    pallas_call x5, Pallas kernels, stored_table(): pl.pallas_call(kernel, in_specs=[smem, smem, anywhere, anywhere], out_spe...  38.7 us
    pallas_call x1, Pallas kernels, products(): pl.pallas_call(product_kernel(plan, count), in_specs=[anywhere] * 14 + [s...  16.8 us
    all_to_all x1, blocking collectives, shards(): got = lax.all_to_all(pieces, ('mp', 'proj'), 0, 0, tiled=True)  11.9 us
    pallas_call x1, Pallas kernels, gradients(): pl.pallas_call(gradient_kernel(plan, split, first, count), in_specs=[anyw...  11.2 us
    ppermute x5, starting transfers between devices, swap(): return lax.ppermute(x, axis, [(i, i ^ 1 << bit) for i in range(size)])  8.08 us
  transfers between devices with their start and end apart: 5, of which 2 were waited for; matrix products, arithmetic and copies ran while one was open for 0% of the time, Pallas kernels for 20%

profile of v2, /device:TPU:0, one launch (start us, length us, event | category | flops | bytes accessed | tf_op | source)
XLA Modules:
  0.0 195.6 jit_solution(659181005606084540)
XLA Ops:
  0.0 16.8 %products.1 = (f32[128,128]{1,0:T(8,128)}, bf16[40,16,256,128]{3,2,1,0:T(8,128)(2,1)}) custom-call(bf16[128,2560]{1,0:T(8,128)(2,1)} %refs_0_.3, bf16[128,2560]{1,0:T(8,128)(2,1)} %refs_1_.3, bf16[128,2560]{1,0:T(8,128)(2,1)} %refs_2_.3, bf16[128,13824]{1,0:T(8,128)(2,1)} %refs_3_.3, bf16[128,2560]{1,0:T(8,128)(2,1)} %refs_4_.3, ...), custom_call_target="tpu_custom_call" | custom-call | tf_op jit(solution)/shard_map/products/pallas_call | solution.py:162
  16.8 3.0 %collective-permute-start = (f32[128,128]{1,0:T(8,128)}, f32[128,128]{1,0:T(8,128)S(1)}, u32[]{:S(2)}, u32[]{:S(2)}) collective-permute-start(f32[128,128]{1,0:T(8,128)} %get-tuple-element.20.after.refs_9_), channel_id=1, source_target_pairs={{0,16},{16,0},{1,17},{17,1},{2,18},{18,2},{3,19},{19,3},{4,20},{20... | collective-permute-start | bytes 196616 | tf_op jit(solution)/shard_map/ppermute | solution.py:451
  19.8 4.9 %stored_table.5.refs_14_ = bf16[40,16,256,128]{3,2,1,0:T(8,128)(2,1)} custom-call(s32[3,128]{1,0:T(4,128)} %constant.24.clone.refs_14_.table.refs_12_, s32[14]{0:T(128)} %seeds.11, f32[128,128]{1,0:T(8,128)} %get-tuple-element.20.after.refs_9_, bf16[40,16,256,128]{3,2,1,0:T(8,128)(2,1)} %get-tuple-element.21.so_far), custom_call_target="tpu_custom_call", output_to_operand_aliasing={{}: (3, {})} | custom-call | tf_op jit(solution)/shard_map/stored_table/pallas_call | solution.py:353
  24.7 0.0 collective-permute-done.refs_10_
  24.7 0.0 copy-start.4
  24.7 0.6 copy-done.4
  25.3 11.2 %gradients.1 = (f32[64,8,512]{2,1,0:T(8,128)}, f32[64,8,512]{2,1,0:T(8,128)}, bf16[40,16,256,128]{3,2,1,0:T(8,128)(2,1)}) custom-call(bf16[128,2560]{1,0:T(8,128)(2,1)} %refs_0_.3, bf16[128,2560]{1,0:T(8,128)(2,1)} %refs_1_.3, bf16[128,2560]{1,0:T(8,128)(2,1)} %refs_2_.3, bf16[128,13824]{1,0:T(8,128)(2,1)} %refs_3_.3, ...), custom_call_target="tpu_custom_call", output_to_operand_aliasing={{2}: (14, {})} | custom-call | tf_op jit(solution)/shard_map/gradients/pallas_call | solution.py:241
  36.5 0.1 collective-permute-start.1
  36.6 0.0 copy-start.2
  36.6 8.0 %stored_table.6.so_far = bf16[40,16,256,128]{3,2,1,0:T(8,128)(2,1)} custom-call(s32[3,128]{1,0:T(4,128)} %constant.24.clone.refs_14_.table.refs_12_, s32[14]{0:T(128)} %seeds.11, f32[64,8,512]{2,1,0:T(8,128)} %get-tuple-element.25.after, bf16[40,16,256,128]{3,2,1,0:T(8,128)(2,1)} %get-tuple-element.26.so_far), custom_call_target="tpu_custom_call", output_to_operand_aliasing={{}: (3, {})} | custom-call | tf_op jit(solution)/shard_map/stored_table/pallas_call | solution.py:353
  44.7 0.0 collective-permute-done.1
  44.7 0.0 copy-done.2
  44.7 0.2 add.30
  44.9 0.0 copy-start
  45.0 1.6 collective-permute-start.2
  46.5 0.0 copy-done
  46.5 12.2 %stored_table.7.so_far = bf16[40,16,256,128]{3,2,1,0:T(8,128)(2,1)} custom-call(s32[3,128]{1,0:T(4,128)} %constant.24.clone.refs_14_.table.refs_12_, s32[14]{0:T(128)} %seeds.11, f32[32,8,512]{2,1,0:T(8,128)} %copy-done, bf16[40,16,256,128]{3,2,1,0:T(8,128)(2,1)} %stored_table.6.so_far), custom_call_target="tpu_custom_call", output_to_operand_aliasing={{}: (3, {})} | custom-call | tf_op jit(solution)/shard_map/stored_table/pallas_call | solution.py:353
  58.7 0.6 collective-permute-done.2
  59.3 0.1 dynamic-slice_add_fusion
  59.5 0.0 copy-start.1
  59.5 2.7 %collective-permute-start.3 = (f32[16,8,512]{2,1,0:T(8,128)S(1)}, f32[16,8,512]{2,1,0:T(8,128)S(1)}, u32[]{:S(2)}, u32[]{:S(2)}) collective-permute-start(f32[16,8,512]{2,1,0:T(8,128)S(1)} %constant_dynamic-slice_fusion.1.after), channel_id=1, source_target_pairs={{0,8},{1,9},{2,10},{3,11},{4,12},{5,13},{6,14},{7,15},{8,0},{9,1},... | collective-permute-start | bytes 786440 | tf_op jit(solution)/shard_map/ppermute | solution.py:451
  62.1 0.0 copy-done.1
  62.1 8.9 %stored_table.8.so_far = bf16[40,16,256,128]{3,2,1,0:T(8,128)(2,1)} custom-call(s32[3,128]{1,0:T(4,128)} %constant.24.clone.refs_14_.table.refs_12_, s32[14]{0:T(128)} %seeds.11, f32[16,8,512]{2,1,0:T(8,128)} %copy-done.1, bf16[40,16,256,128]{3,2,1,0:T(8,128)(2,1)} %stored_table.7.so_far), custom_call_target="tpu_custom_call", output_to_operand_aliasing={{}: (3, {})} | custom-call | tf_op jit(solution)/shard_map/stored_table/pallas_call | solution.py:353
  71.0 2.8 %collective-permute-done.3 = f32[16,8,512]{2,1,0:T(8,128)S(1)} collective-permute-done((f32[16,8,512]{2,1,0:T(8,128)S(1)}, f32[16,8,512]{2,1,0:T(8,128)S(1)}, u32[]{:S(2)}, u32[]{:S(2)}) %collective-permute-start.3) | collective-permute-done | bytes 262176 | tf_op jit(solution)/shard_map/ppermute | solution.py:451
  73.9 0.0 copy-start.3
  74.0 0.7 collective-permute-start.4
  74.7 0.0 copy-done.3
  74.7 4.8 %stored_table.9.tiles = bf16[40,16,256,128]{3,2,1,0:T(8,128)(2,1)} custom-call(s32[3,128]{1,0:T(4,128)} %constant.24.clone.refs_14_.table.refs_12_, s32[14]{0:T(128)} %seeds.11, f32[8,8,512]{2,1,0:T(8,128)} %copy-done.3, bf16[40,16,256,128]{3,2,1,0:T(8,128)(2,1)} %stored_table.8.so_far), custom_call_target="tpu_custom_call", output_to_operand_aliasing={{}: (3, {})} | custom-call | tf_op jit(solution)/shard_map/stored_table/pallas_call | solution.py:353
  79.5 0.0 collective-permute-done.4
  79.5 0.7 add_bitcast_fusion.grads.old_grads
  80.2 103.0 %project.1 = f32[32,1,64]{2,1,0:T(1,128)} custom-call(s32[3,128]{1,0:T(4,128)} %constant.24.clone.refs_14_.table.refs_12_, s32[14]{0:T(128)} %seeds.11, f32[1,8,8,512]{3,2,1,0:T(8,128)} %add_bitcast_fusion.grads.old_grads, f32[1,8,8,512]{3,2,1,0:T(8,128)} %add_bitcast_fusion.grads.old_grads, bf16[40,16,256,128]{3,2,1,0:T(8,128)(2,1)} %stored_table.9.tiles), custom_call_target="tpu_custom_call" | custom-call | tf_op jit(solution)/shard_map/project/pallas_call | solution.py:428
  183.2 11.9 %all_to_all.5 = f32[32,1,64]{2,1,0:T(1,128)S(1)} all-to-all(f32[32,1,64]{2,1,0:T(1,128)} %project.1), channel_id=1, replica_groups=mesh['mp'=2,'proj'=16] {'mp','proj'}, dimensions={0} | all-to-all | bytes 16384 | tf_op jit(solution)/shard_map/all_to_all | solution.py:497
  195.1 0.6 reduce_sum.11
  (4 shorter events, 0.1 us)
Async XLA Ops:
  16.8 7.9 %collective-permute-start = (f32[128,128]{1,0:T(8,128)}, f32[128,128]{1,0:T(8,128)S(1)}, u32[]{:S(2)}, u32[]{:S(2)}) collective-permute-start(f32[128,128]{1,0:T(8,128)} %get-tuple-element.20.after.refs_9_), channel_id=1, source_target_pairs={{0,16},{16,0},{1,17},{17,1},{2,18},{18,2},{3,19},{19,3},{4,20},{20... | collective-permute-start | bytes 196616 | tf_op jit(solution)/shard_map/ppermute | solution.py:451
  24.7 0.6 copy-start.4
  36.5 8.1 %collective-permute-start.1 = (f32[64,8,512]{2,1,0:T(8,128)}, f32[64,8,512]{2,1,0:T(8,128)S(1)}, u32[]{:S(2)}, u32[]{:S(2)}) collective-permute-start(f32[64,8,512]{2,1,0:T(8,128)} %get-tuple-element.25.after), channel_id=1, source_target_pairs={{0,1},{1,0},{2,3},{3,2},{4,5},{5,4},{6,7},{7,6},{8,9},{9,8},{10,11... | collective-permute-start | bytes 3145736 | tf_op jit(solution)/shard_map/ppermute | solution.py:451
  36.6 8.0 %copy-start.2 = (f32[64,8,512]{2,1,0:T(8,128)S(1)}, f32[64,8,512]{2,1,0:T(8,128)}, u32[]{:S(2)}) copy-start(f32[64,8,512]{2,1,0:T(8,128)} %get-tuple-element.24) | copy-start | bytes 3145732
  44.9 1.6 copy-start
  45.0 14.4 %collective-permute-start.2 = (f32[32,8,512]{2,1,0:T(8,128)S(1)}, f32[32,8,512]{2,1,0:T(8,128)S(1)}, u32[]{:S(2)}, u32[]{:S(2)}) collective-permute-start(f32[32,8,512]{2,1,0:T(8,128)S(1)} %constant_dynamic-slice_fusion.2.after), channel_id=1, source_target_pairs={{0,2},{1,3},{2,0},{3,1},{4,6},{5,7},{6,4},{7,5},{8,10},{9,11},{10,... | collective-permute-start | bytes 1572872 | tf_op jit(solution)/shard_map/ppermute | solution.py:451
  59.5 2.7 %copy-start.1 = (f32[16,8,512]{2,1,0:T(8,128)}, f32[16,8,512]{2,1,0:T(8,128)S(1)}, u32[]{:S(2)}) copy-start(f32[16,8,512]{2,1,0:T(8,128)S(1)} %constant_dynamic-slice_fusion.1.after) | copy-start | bytes 786436
  59.5 14.4 %collective-permute-start.3 = (f32[16,8,512]{2,1,0:T(8,128)S(1)}, f32[16,8,512]{2,1,0:T(8,128)S(1)}, u32[]{:S(2)}, u32[]{:S(2)}) collective-permute-start(f32[16,8,512]{2,1,0:T(8,128)S(1)} %constant_dynamic-slice_fusion.1.after), channel_id=1, source_target_pairs={{0,8},{1,9},{2,10},{3,11},{4,12},{5,13},{6,14},{7,15},{8,0},{9,1},... | collective-permute-start | bytes 786440 | tf_op jit(solution)/shard_map/ppermute | solution.py:451
  73.9 0.8 copy-start.3
  74.0 5.6 %collective-permute-start.4 = (f32[8,8,512]{2,1,0:T(8,128)S(1)}, f32[8,8,512]{2,1,0:T(8,128)S(1)}, u32[]{:S(2)}, u32[]{:S(2)}) collective-permute-start(f32[8,8,512]{2,1,0:T(8,128)S(1)} %constant_dynamic-slice_fusion.after), channel_id=1, source_target_pairs={{0,4},{1,5},{2,6},{3,7},{4,0},{5,1},{6,2},{7,3},{8,12},{9,13},{10,... | collective-permute-start | bytes 393224 | tf_op jit(solution)/shard_map/ppermute | solution.py:451

commit v3 on v2

--- a/solution.py
+++ b/solution.py
@@ -17,7 +17,7 @@
 COL_MULT = -1640531535
 MIX_A = -2048144789
 MIX_B = -1028477387
-STORED_STEPS = (6, 3, 5, 6, 10, 7, 3)
+STORED_STEPS = (6, 2, 5, 5, 11, 10, 3)
 
 srl = lax.shift_right_logical
 
@@ -86,17 +86,31 @@
         return piece * (self.blocks // self.group) + (j // self.group) * self.own_blocks
 
 
+def every_other(x, first):
+    wide = x.shape[1]
+    u = lax.broadcasted_iota(jnp.int32, (wide, wide // 2), 0)
+    t = lax.broadcasted_iota(jnp.int32, (wide, wide // 2), 1)
+    choose = (u == 2 * t + first).astype(jnp.float32).astype(jnp.bfloat16)
+    total = None
+    for _ in range(3):
+        term = x.astype(jnp.bfloat16)
+        x = x - term.astype(jnp.float32)
+        got = jnp.dot(term, choose, preferred_element_type=jnp.float32)
+        total = got if total is None else total + got
+    return total
+
+
 def product_kernel(plan, count):
     def kernel(*refs):
         data = refs[:9]
         weights = refs[9:14]
         fill_refs = refs[14:16]
-        out, tiles = refs[16:18]
-        bufs = refs[18:27]
-        pairs, sems = refs[27:29]
+        out, tiles, bases = refs[16:19]
+        bufs = refs[19:28]
+        sems = refs[28]
         factor_bufs = refs[29:34]
         aif, daf, aof, kvb, gub = factor_bufs
-        fill_refs = fill_refs + refs[34:]
+        table, seeds = fill_refs
         order = [(0, lambda c: rows_of([aif[i, :, c] for i in (0, 1, 2)]), (0,)),
                  (4, lambda c: aof[0, :, c], (24,)),
                  (5, lambda c: rows_of([kvb[i, :, c] for i in (0, 1)]), (32, 40)),
@@ -117,7 +131,14 @@
         loads = [pltpu.make_async_copy(weights[i], factor_bufs[i], sems.at[len(copies) + i]) for i in range(5)]
         for copy in loads + [copy[3] for copy in copies]:
             copy.start()
-        finish = fill_tables(plan, 0, count, fill_refs, tiles)
+        block = plan.first_own()
+        for n in range(plan.steps // RANK):
+            parts = plan.block // plan.sub
+            seg = table[0, block + n // parts]
+            feature = lax.axis_index("mp") * table[2, block + n // parts] + table[1, block + n // parts]
+            feature = feature + (n % parts) * plan.sub
+            bases[n] = seeds[seg] * SEED_MULT + feature * wrapped(RANK * ROW_MULT)
+        finish = fill_tables(plan, 0, count, (bases,) + refs[34:], tiles)
         for load in loads:
             load.wait()
         for arg, factor, places in order:
@@ -128,20 +149,17 @@
                 copy.wait()
                 cols = pl.ds(start, step)
                 if len(data[arg].shape) == 3:
-                    left = bufs[arg][:, :, cols].reshape(2 * plan.tokens, step)
+                    right = bufs[arg][:, :, cols].reshape(2 * plan.tokens, step)
                 else:
-                    left = bufs[arg][:, cols]
-                part = lax.dot_general(left, factor(cols), (((1,), (1,)), ((), ())),
+                    right = bufs[arg][:, cols]
+                part = lax.dot_general(factor(cols), right, (((1,), (1,)), ((), ())),
                                        preferred_element_type=jnp.float32)
                 total = part if total is None else total + part
             if len(places) == 2:
-                pairs[:, 0:2 * RANK] = total
                 for i, place in enumerate(places):
-                    got = pairs[pl.ds(i, plan.tokens, stride=2), :]
-                    out[:, place:place + RANK] = got[:, i * RANK:(i + 1) * RANK]
+                    out[place:place + RANK, :] = every_other(total[i * RANK:(i + 1) * RANK], i)
             else:
-                out[:, places[0]:places[0] + total.shape[1]] = total
-        out[:, 112:] = jnp.zeros((plan.tokens, 16), jnp.float32)
+                out[places[0]:places[0] + total.shape[0], :] = total
         finish()
 
     return kernel
@@ -162,10 +180,14 @@
     return pl.pallas_call(
         product_kernel(plan, count),
         in_specs=[anywhere] * 14 + [smem, smem],
-        out_specs=[whole, anywhere],
-        out_shape=[jax.ShapeDtypeStruct((plan.tokens, 128), jnp.float32), tiles_shape(plan, total)],
+        out_specs=[whole, anywhere, smem],
+        out_shape=[
+            jax.ShapeDtypeStruct((14 * RANK, plan.tokens), jnp.float32),
+            tiles_shape(plan, total),
+            jax.ShapeDtypeStruct((plan.steps // RANK,), jnp.int32),
+        ],
         scratch_shapes=data_buffers(plan, data)
-        + [pltpu.VMEM((2 * plan.tokens, 128), jnp.float32), pltpu.SemaphoreType.DMA((copy_count(plan) + 5,))]
+        + [pltpu.SemaphoreType.DMA((copy_count(plan) + 5,))]
         + [pltpu.VMEM(x.shape, x.dtype) for x in factors]
         + fill_scratch(plan, count),
         name="products",
@@ -176,11 +198,11 @@
     def kernel(*refs):
         data = refs[:9]
         own, other, mask = refs[9:12]
-        fill_refs = refs[12:14]
-        keep, send, tiles = refs[15:18]
-        bufs = refs[18:27]
-        grads, sems, out_sems = refs[27:30]
-        fill_refs = fill_refs + refs[30:]
+        bases = refs[12]
+        keep, send, tiles = refs[14:17]
+        bufs = refs[17:26]
+        grads, sems, out_sems = refs[26:29]
+        fill_refs = (bases,) + refs[29:]
         copies = {}
         number = 0
         for arg, _, _, width in plan.pieces:
@@ -193,7 +215,7 @@
             copy.start()
         finish = fill_tables(plan, first, count, fill_refs, tiles)
         total = own[...] + other[...]
-        turned = total.T * mask[...].astype(jnp.float32)
+        turned = total * mask[...].astype(jnp.float32)
         tokens = plan.tokens
         half = plan.blocks // 2
         for arg, places, segs, width in plan.pieces:
@@ -233,14 +255,14 @@
     return kernel
 
 
-def gradients(plan, data, own, other, mask, split, table, seeds, first, count, so_far):
+def gradients(plan, data, own, other, mask, split, bases, first, count, so_far):
     anywhere = pl.BlockSpec(memory_space=pl.ANY)
     smem = pl.BlockSpec(memory_space=pltpu.SMEM)
     whole = pl.BlockSpec(memory_space=pltpu.VMEM)
     half = jax.ShapeDtypeStruct((plan.blocks // 2, RANK, plan.block), jnp.float32)
     return pl.pallas_call(
         gradient_kernel(plan, split, first, count),
-        in_specs=[anywhere] * 9 + [whole] * 3 + [smem, smem, anywhere],
+        in_specs=[anywhere] * 9 + [whole] * 3 + [smem, anywhere],
         out_specs=[anywhere] * 3,
         out_shape=[half, half, jax.ShapeDtypeStruct(so_far.shape, so_far.dtype)],
         scratch_shapes=data_buffers(plan, data)
@@ -250,24 +272,17 @@
             pltpu.SemaphoreType.DMA((2,)),
         ]
         + fill_scratch(plan, count),
-        input_output_aliases={14: 2},
+        input_output_aliases={13: 2},
         name="gradients",
-    )(*data, own, other, mask, table, seeds, so_far)
+    )(*data, own, other, mask, bases, so_far)
 
 
 def row_offsets(plan):
     return lax.broadcasted_iota(jnp.int32, (plan.sub, COLS), 0) * wrapped(RANK * ROW_MULT)
 
 
-def step_keys(plan, step, seeds, table, offsets):
-    number = step // RANK
-    rank = step % RANK
-    parts = plan.block // plan.sub
-    block = plan.first_own() + number // parts
-    seg = table[0, block]
-    feature = lax.axis_index("mp") * table[2, block] + table[1, block] + (number % parts) * plan.sub
-    base = seeds[seg] * SEED_MULT + (feature * RANK + rank) * ROW_MULT
-    key = base + offsets
+def step_keys(step, bases, offsets):
+    key = bases[step // RANK] + (step % RANK) * ROW_MULT + offsets
     return key ^ srl(key, 16)
 
 
@@ -301,10 +316,11 @@
 
 COLS = 256
 LANES = 128
-
-
-def fill_step(plan, step, seeds, table, row_base, col_base, tile):
-    rows = step_keys(plan, step, seeds, table, row_base[...])
+PAIR = 2
+
+
+def fill_step(step, bases, row_base, col_base, tile):
+    rows = step_keys(step, bases, row_base[...])
     for c in range(0, K, COLS):
         part = centred_sum(mixed(rows, col_base[:, c:c + COLS]))
         for n in range(0, COLS, LANES):
@@ -312,12 +328,12 @@
 
 
 def fill_tables(plan, first, count, refs, out):
-    table, seeds, row_base, col_base, tiles, sems = refs
+    bases, row_base, col_base, tiles, sems = refs
     row_base[...] = row_offsets(plan)
     col_base[...] = column_keys(RANK)
 
     def body(n, carry):
-        fill_step(plan, n + first, seeds, table, row_base, col_base, tiles.at[n])
+        fill_step(n + first, bases, row_base, col_base, tiles.at[n])
         pltpu.make_async_copy(tiles.at[n], out.at[n + first], sems.at[n]).start()
         return carry
 
@@ -343,26 +359,26 @@
     return jax.ShapeDtypeStruct((total, K // LANES, plan.sub, LANES), jnp.bfloat16)
 
 
-def stored_table(plan, table, seeds, first, count, after, so_far):
+def stored_table(plan, bases, first, count, after, so_far):
     smem = pl.BlockSpec(memory_space=pltpu.SMEM)
     anywhere = pl.BlockSpec(memory_space=pl.ANY)
 
-    def kernel(table, seeds, after, so_far, out, *scratch):
-        fill_tables(plan, first, count, (table, seeds) + scratch, out)()
+    def kernel(bases, after, so_far, out, *scratch):
+        fill_tables(plan, first, count, (bases,) + scratch, out)()
 
     return pl.pallas_call(
         kernel,
-        in_specs=[smem, smem, anywhere, anywhere],
+        in_specs=[smem, anywhere, anywhere],
         out_specs=anywhere,
         out_shape=jax.ShapeDtypeStruct(so_far.shape, so_far.dtype),
         scratch_shapes=fill_scratch(plan, count),
-        input_output_aliases={3: 0},
+        input_output_aliases={2: 0},
         name="stored_table",
-    )(table, seeds, after, so_far)
+    )(bases, after, so_far)
 
 
 def project_kernel(plan, stored, scale, devices):
-    fresh = plan.steps - stored
+    rounds = (plan.steps - stored) // PAIR
     depth = 2 * RANK * plan.examples
     parts = 4
     slab = plan.sub // parts
@@ -377,7 +393,7 @@
             parts += [top, g - top]
         return rows_of(parts).astype(jnp.bfloat16)
 
-    def kernel(table, seeds, grads, old_grads, tiles, out, acc, row_base, col_base):
+    def kernel(bases, grads, old_grads, tiles, out, acc, row_base, col_base):
         i = pl.program_id(0)
 
         @pl.when(i == 0)
@@ -386,24 +402,28 @@
             row_base[...] = row_offsets(plan)
             col_base[...] = column_keys(RANK)
 
-        rows = step_keys(plan, i + stored, seeds, table, row_base[...])
-        left = pick(grads, i + stored)
-        fix = -510.0 * jnp.sum(left.astype(jnp.float32), axis=1, keepdims=True)
         old = pick(old_grads, i)
         old = jnp.where(i < stored, old.astype(jnp.float32), 0.0)
-        fix = fix + jnp.sum(old, axis=1, keepdims=True)
+        fix = jnp.sum(old, axis=1, keepdims=True)
         old = (old * (1.0 / 65536.0)).astype(jnp.bfloat16)
-        lefts = [jnp.concatenate([left[:, b:b + slab]] * parts, axis=1) for b in range(0, plan.sub, slab)]
+        lefts, rows = [], []
+        for p in range(PAIR):
+            step = stored + PAIR * i + p
+            rows.append(step_keys(step, bases, row_base[...]))
+            left = pick(grads, step)
+            fix = fix - 510.0 * jnp.sum(left.astype(jnp.float32), axis=1, keepdims=True)
+            lefts.append([jnp.concatenate([left[:, b:b + slab]] * parts, axis=1) for b in range(0, plan.sub, slab)])
         for c in range(0, K, COLS):
             a = acc[:, c:c + COLS] + fix
-            for n in range(parts):
-                planes = byte_planes(mixed(rows[n * slab:(n + 1) * slab], col_base[:, c:c + COLS]))
-                a = a + jnp.dot(lefts[n], rows_of(planes), preferred_element_type=jnp.float32)
+            for p in range(PAIR):
+                for n in range(parts):
+                    planes = byte_planes(mixed(rows[p][n * slab:(n + 1) * slab], col_base[:, c:c + COLS]))
+                    a = a + jnp.dot(lefts[p][n], rows_of(planes), preferred_element_type=jnp.float32)
             tile = jnp.concatenate([tiles[0, (c + n) // LANES] for n in range(0, COLS, LANES)], axis=1)
             a = a + jnp.dot(old, tile, preferred_element_type=jnp.float32)
             acc[:, c:c + COLS] = a
 
-        @pl.when(i == fresh - 1)
+        @pl.when(i == rounds - 1)
         def _():
             width = K // devices
             for e in range(plan.examples):
@@ -412,11 +432,11 @@
                 for d in range(devices):
                     out[d, e:e + 1, :] = total[:, d * width:(d + 1) * width]
 
-    return kernel, depth, fresh
-
-
-def project(plan, table, seeds, grads, tiles, stored, scale, devices):
-    kernel, depth, fresh = project_kernel(plan, stored, scale, devices)
+    return kernel, depth, rounds
+
+
+def project(plan, bases, grads, tiles, stored, scale, devices):
+    kernel, depth, rounds = project_kernel(plan, stored, scale, devices)
     smem = pl.BlockSpec(memory_space=pltpu.SMEM)
     parts = plan.block // plan.sub
 
@@ -427,11 +447,10 @@
     last = stored - 1
     return pl.pallas_call(
         kernel,
-        grid=(fresh,),
+        grid=(rounds,),
         in_specs=[
             smem,
-            smem,
-            pl.BlockSpec((plan.examples, 1, RANK, plan.sub), lambda i: place(i + stored)),
+            pl.BlockSpec((plan.examples, 1, RANK, plan.sub), lambda i: place(PAIR * i + stored)),
             pl.BlockSpec((plan.examples, 1, RANK, plan.sub), lambda i: place(jnp.minimum(i, last))),
             pl.BlockSpec((1, K // LANES, plan.sub, LANES), lambda i: (jnp.minimum(i, last), 0, 0, 0)),
         ],
@@ -443,7 +462,7 @@
             pltpu.VMEM((RANK, K), jnp.int32),
         ],
         name="project",
-    )(table, seeds, grads, grads, tiles)
+    )(bases, grads, grads, tiles)
 
 
 def swap(x, axis, bit):
@@ -458,13 +477,14 @@
     plan = Plan(tuple(x.shape[-1] for x in data), data[0].shape[0], lax.axis_size("proj"))
     table = jnp.asarray(plan.table)
     counts = [max(1, c * plan.steps // 128) for c in STORED_STEPS][:3 + len(plan.bits)]
+    counts[-1] += sum(counts) % PAIR
     starts = [sum(counts[:n]) for n in range(len(counts))]
     stored = sum(counts)
-    own, tiles = products(plan, data, factors, table, seeds, counts[0], stored)
+    own, tiles, bases = products(plan, data, factors, table, seeds, counts[0], stored)
 
     def cover(received, sent, number):
         nonlocal tiles
-        tiles = stored_table(plan, table, seeds, starts[number], counts[number], sent, tiles)
+        tiles = stored_table(plan, bases, starts[number], counts[number], sent, tiles)
         received, tiles = lax.optimization_barrier((received, tiles))
         return received
 
@@ -475,7 +495,7 @@
         other = jnp.zeros_like(own)
     other = cover(other, own, 1)
     keep, send, tiles = gradients(
-        plan, data, own, other, mask.reshape(1, -1), plan.bits[0], table, seeds, starts[2], counts[2], tiles)
+        plan, data, own, other, mask.reshape(1, -1), plan.bits[0], bases, starts[2], counts[2], tiles)
     j = lax.axis_index("proj")
     x = None
     for number, bit in enumerate(plan.bits):
@@ -493,7 +513,7 @@
         x = lax.all_to_all(x, "proj", 0, 0, axis_index_groups=groups, tiled=True)
     scale = 1.0 / (LENGTH * math.sqrt(21845.0 * K))
     devices = lax.axis_size("mp") * plan.owners
-    pieces = project(plan, table, seeds, x, tiles, stored, scale, devices)
+    pieces = project(plan, bases, x, tiles, stored, scale, devices)
     got = lax.all_to_all(pieces, ("mp", "proj"), 0, 0, tiled=True)
     return got.sum(axis=0)
 

time: 197 us -> 179 us (0.909)
  Pallas kernels: 170 us -> 156 us
  waiting for transfers between devices: 3.47 us -> 0.6 us
    pallas_call x6, Pallas kernels: 142 us -> 128 us  [the longest x1 88.3 us: project(): pl.pallas_call(kernel, grid=(rounds,), in_specs=[smem, pl.BlockSpec((plan...]
    ppermute x5, waiting for transfers between devices: 3.47 us -> 0.6 us  [swap(): return lax.ppermute(x, axis, [(i, i ^ 1 << bit) for i in range(size)])]
  transfers between devices with their start and end apart: 5 -> 5, of which waited for: 2 -> 1; matrix products, arithmetic and copies ran while one was open for 0% -> 0% of each run, Pallas kernels for 20% -> 22%
where the time goes in v3:
time: 179 us; the launch traced here: 178 us
  Pallas kernels  156 us (87%)
  blocking collectives  11.2 us (6%)
  starting transfers between devices  8.41 us (5%)
    pallas_call x1, Pallas kernels, project(): pl.pallas_call(kernel, grid=(rounds,), in_specs=[smem, pl.BlockSpec((plan...  88.3 us
    pallas_call x5, Pallas kernels, stored_table(): pl.pallas_call(kernel, in_specs=[smem, anywhere, anywhere], out_specs=any...  39.8 us
    pallas_call x1, Pallas kernels, products(): pl.pallas_call(product_kernel(plan, count), in_specs=[anywhere] * 14 + [s...  16.6 us
    all_to_all x1, blocking collectives, shards(): got = lax.all_to_all(pieces, ('mp', 'proj'), 0, 0, tiled=True)  11.2 us
    pallas_call x1, Pallas kernels, gradients(): pl.pallas_call(gradient_kernel(plan, split, first, count), in_specs=[anyw...  11 us
    ppermute x5, starting transfers between devices, swap(): return lax.ppermute(x, axis, [(i, i ^ 1 << bit) for i in range(size)])  8.41 us
  transfers between devices with their start and end apart: 5, of which 1 were waited for; matrix products, arithmetic and copies ran while one was open for 0% of the time, Pallas kernels for 22%

profile of v3, /device:TPU:0, one launch (start us, length us, event | category | flops | bytes accessed | tf_op | source)
XLA Modules:
  0.0 178.4 jit_solution(6777425565575153921)
XLA Ops:
  0.0 16.6 %products.1 = (f32[112,128]{1,0:T(8,128)}, bf16[42,16,256,128]{3,2,1,0:T(8,128)(2,1)}, s32[16]{0:T(128)}) custom-call(bf16[128,2560]{1,0:T(8,128)(2,1)} %refs_0_.3, bf16[128,2560]{1,0:T(8,128)(2,1)} %refs_1_.3, bf16[128,2560]{1,0:T(8,128)(2,1)} %refs_2_.3, bf16[128,13824]{1,0:T(8,128)(2,1)} %refs_3_.3, bf16[128,2560]{1,0:T(8,128)(2,1)} %refs_4_.3, ...), custom_call_target="tpu_custom_call" | custom-call | tf_op jit(solution)/shard_map/products/pallas_call | solution.py:180
  16.6 3.0 %collective-permute-start = (f32[112,128]{1,0:T(8,128)}, f32[112,128]{1,0:T(8,128)S(1)}, u32[]{:S(2)}, u32[]{:S(2)}) collective-permute-start(f32[112,128]{1,0:T(8,128)} %get-tuple-element.22.after.refs_9_), channel_id=1, source_target_pairs={{0,16},{16,0},{1,17},{17,1},{2,18},{18,2},{3,19},{19,3},{4,20},{20... | collective-permute-start | bytes 172040 | tf_op jit(solution)/shard_map/ppermute | solution.py:470
  19.6 3.7 %stored_table.5.refs_13_ = bf16[42,16,256,128]{3,2,1,0:T(8,128)(2,1)} custom-call(s32[16]{0:T(128)} %get-tuple-element.21.bases.refs_12_, f32[112,128]{1,0:T(8,128)} %get-tuple-element.22.after.refs_9_, bf16[42,16,256,128]{3,2,1,0:T(8,128)(2,1)} %get-tuple-element.23.so_far), custom_call_target="tpu_custom_call", output_to_operand_aliasing={{}: (2, {})} | custom-call | tf_op jit(solution)/shard_map/stored_table/pallas_call | solution.py:369
  23.3 0.0 collective-permute-done.refs_10_
  23.4 0.0 copy-start.4
  23.4 0.6 copy-done.4
  24.0 11.0 %gradients.1 = (f32[64,8,512]{2,1,0:T(8,128)}, f32[64,8,512]{2,1,0:T(8,128)}, bf16[42,16,256,128]{3,2,1,0:T(8,128)(2,1)}) custom-call(bf16[128,2560]{1,0:T(8,128)(2,1)} %refs_0_.3, bf16[128,2560]{1,0:T(8,128)(2,1)} %refs_1_.3, bf16[128,2560]{1,0:T(8,128)(2,1)} %refs_2_.3, bf16[128,13824]{1,0:T(8,128)(2,1)} %refs_3_.3, ...), custom_call_target="tpu_custom_call", output_to_operand_aliasing={{2}: (13, {})} | custom-call | tf_op jit(solution)/shard_map/gradients/pallas_call | solution.py:263
  35.0 0.1 collective-permute-start.1
  35.0 0.0 copy-start.2
  35.0 6.9 %stored_table.6.so_far = bf16[42,16,256,128]{3,2,1,0:T(8,128)(2,1)} custom-call(s32[16]{0:T(128)} %get-tuple-element.21.bases.refs_12_, f32[64,8,512]{2,1,0:T(8,128)} %get-tuple-element.27.after, bf16[42,16,256,128]{3,2,1,0:T(8,128)(2,1)} %get-tuple-element.28.so_far), custom_call_target="tpu_custom_call", output_to_operand_aliasing={{}: (2, {})} | custom-call | tf_op jit(solution)/shard_map/stored_table/pallas_call | solution.py:369
  41.9 0.0 collective-permute-done.1
  41.9 0.0 copy-done.2
  41.9 0.2 add.30
  42.2 0.0 copy-start
  42.2 1.6 collective-permute-start.2
  43.8 0.0 copy-done
  43.8 12.8 %stored_table.7.so_far = bf16[42,16,256,128]{3,2,1,0:T(8,128)(2,1)} custom-call(s32[16]{0:T(128)} %get-tuple-element.21.bases.refs_12_, f32[32,8,512]{2,1,0:T(8,128)} %copy-done, bf16[42,16,256,128]{3,2,1,0:T(8,128)(2,1)} %stored_table.6.so_far), custom_call_target="tpu_custom_call", output_to_operand_aliasing={{}: (2, {})} | custom-call | tf_op jit(solution)/shard_map/stored_table/pallas_call | solution.py:369
  56.6 0.0 collective-permute-done.2
  56.6 0.1 dynamic-slice_add_fusion
  56.7 0.0 copy-start.1
  56.7 2.7 %collective-permute-start.3 = (f32[16,8,512]{2,1,0:T(8,128)S(1)}, f32[16,8,512]{2,1,0:T(8,128)S(1)}, u32[]{:S(2)}, u32[]{:S(2)}) collective-permute-start(f32[16,8,512]{2,1,0:T(8,128)S(1)} %constant_dynamic-slice_fusion.1.after), channel_id=1, source_target_pairs={{0,8},{1,9},{2,10},{3,11},{4,12},{5,13},{6,14},{7,15},{8,0},{9,1},... | collective-permute-start | bytes 786440 | tf_op jit(solution)/shard_map/ppermute | solution.py:470
  59.4 0.0 copy-done.1
  59.4 11.7 %stored_table.8.so_far = bf16[42,16,256,128]{3,2,1,0:T(8,128)(2,1)} custom-call(s32[16]{0:T(128)} %get-tuple-element.21.bases.refs_12_, f32[16,8,512]{2,1,0:T(8,128)} %copy-done.1, bf16[42,16,256,128]{3,2,1,0:T(8,128)(2,1)} %stored_table.7.so_far), custom_call_target="tpu_custom_call", output_to_operand_aliasing={{}: (2, {})} | custom-call | tf_op jit(solution)/shard_map/stored_table/pallas_call | solution.py:369
  71.2 0.6 collective-permute-done.3
  71.8 0.0 copy-start.3
  71.8 1.1 collective-permute-start.4
  72.9 0.0 copy-done.3
  72.9 4.7 %stored_table.9.tiles = bf16[42,16,256,128]{3,2,1,0:T(8,128)(2,1)} custom-call(s32[16]{0:T(128)} %get-tuple-element.21.bases.refs_12_, f32[8,8,512]{2,1,0:T(8,128)} %copy-done.3, bf16[42,16,256,128]{3,2,1,0:T(8,128)(2,1)} %stored_table.8.so_far), custom_call_target="tpu_custom_call", output_to_operand_aliasing={{}: (2, {})} | custom-call | tf_op jit(solution)/shard_map/stored_table/pallas_call | solution.py:369
  77.6 0.0 collective-permute-done.4
  77.6 0.7 add_bitcast_fusion.grads.old_grads
  78.3 88.3 %project.1 = f32[32,1,64]{2,1,0:T(1,128)} custom-call(s32[16]{0:T(128)} %get-tuple-element.21.bases.refs_12_, f32[1,8,8,512]{3,2,1,0:T(8,128)} %add_bitcast_fusion.grads.old_grads, f32[1,8,8,512]{3,2,1,0:T(8,128)} %add_bitcast_fusion.grads.old_grads, bf16[42,16,256,128]{3,2,1,0:T(8,128)(2,1)} %stored_table.9.tiles), custom_call_target="tpu_custom_call" | custom-call | tf_op jit(solution)/shard_map/project/pallas_call | solution.py:448
  166.6 11.2 %all_to_all.5 = f32[32,1,64]{2,1,0:T(1,128)S(1)} all-to-all(f32[32,1,64]{2,1,0:T(1,128)} %project.1), channel_id=1, replica_groups=mesh['mp'=2,'proj'=16] {'mp','proj'}, dimensions={0} | all-to-all | bytes 16384 | tf_op jit(solution)/shard_map/all_to_all | solution.py:517
  177.8 0.6 reduce_sum.11
  (4 shorter events, 0.1 us)
Async XLA Ops:
  16.6 6.7 %collective-permute-start = (f32[112,128]{1,0:T(8,128)}, f32[112,128]{1,0:T(8,128)S(1)}, u32[]{:S(2)}, u32[]{:S(2)}) collective-permute-start(f32[112,128]{1,0:T(8,128)} %get-tuple-element.22.after.refs_9_), channel_id=1, source_target_pairs={{0,16},{16,0},{1,17},{17,1},{2,18},{18,2},{3,19},{19,3},{4,20},{20... | collective-permute-start | bytes 172040 | tf_op jit(solution)/shard_map/ppermute | solution.py:470
  23.4 0.6 copy-start.4
  35.0 7.0 %collective-permute-start.1 = (f32[64,8,512]{2,1,0:T(8,128)}, f32[64,8,512]{2,1,0:T(8,128)S(1)}, u32[]{:S(2)}, u32[]{:S(2)}) collective-permute-start(f32[64,8,512]{2,1,0:T(8,128)} %get-tuple-element.27.after), channel_id=1, source_target_pairs={{0,1},{1,0},{2,3},{3,2},{4,5},{5,4},{6,7},{7,6},{8,9},{9,8},{10,11... | collective-permute-start | bytes 3145736 | tf_op jit(solution)/shard_map/ppermute | solution.py:470
  35.0 6.9 %copy-start.2 = (f32[64,8,512]{2,1,0:T(8,128)S(1)}, f32[64,8,512]{2,1,0:T(8,128)}, u32[]{:S(2)}) copy-start(f32[64,8,512]{2,1,0:T(8,128)} %get-tuple-element.26) | copy-start | bytes 3145732
  42.2 1.6 copy-start
  42.2 14.4 %collective-permute-start.2 = (f32[32,8,512]{2,1,0:T(8,128)S(1)}, f32[32,8,512]{2,1,0:T(8,128)S(1)}, u32[]{:S(2)}, u32[]{:S(2)}) collective-permute-start(f32[32,8,512]{2,1,0:T(8,128)S(1)} %constant_dynamic-slice_fusion.2.after), channel_id=1, source_target_pairs={{0,2},{1,3},{2,0},{3,1},{4,6},{5,7},{6,4},{7,5},{8,10},{9,11},{10,... | collective-permute-start | bytes 1572872 | tf_op jit(solution)/shard_map/ppermute | solution.py:470
  56.7 2.7 %copy-start.1 = (f32[16,8,512]{2,1,0:T(8,128)}, f32[16,8,512]{2,1,0:T(8,128)S(1)}, u32[]{:S(2)}) copy-start(f32[16,8,512]{2,1,0:T(8,128)S(1)} %constant_dynamic-slice_fusion.1.after) | copy-start | bytes 786436
  56.7 15.0 %collective-permute-start.3 = (f32[16,8,512]{2,1,0:T(8,128)S(1)}, f32[16,8,512]{2,1,0:T(8,128)S(1)}, u32[]{:S(2)}, u32[]{:S(2)}) collective-permute-start(f32[16,8,512]{2,1,0:T(8,128)S(1)} %constant_dynamic-slice_fusion.1.after), channel_id=1, source_target_pairs={{0,8},{1,9},{2,10},{3,11},{4,12},{5,13},{6,14},{7,15},{8,0},{9,1},... | collective-permute-start | bytes 786440 | tf_op jit(solution)/shard_map/ppermute | solution.py:470
  71.8 1.1 copy-start.3
  71.8 5.8 %collective-permute-start.4 = (f32[8,8,512]{2,1,0:T(8,128)S(1)}, f32[8,8,512]{2,1,0:T(8,128)S(1)}, u32[]{:S(2)}, u32[]{:S(2)}) collective-permute-start(f32[8,8,512]{2,1,0:T(8,128)S(1)} %constant_dynamic-slice_fusion.after), channel_id=1, source_target_pairs={{0,4},{1,5},{2,6},{3,7},{4,0},{5,1},{6,2},{7,3},{8,12},{9,13},{10,... | collective-permute-start | bytes 393224 | tf_op jit(solution)/shard_map/ppermute | solution.py:470

commit v4 on v3

--- a/solution.py
+++ b/solution.py
@@ -17,7 +17,7 @@
 COL_MULT = -1640531535
 MIX_A = -2048144789
 MIX_B = -1028477387
-STORED_STEPS = (6, 2, 5, 5, 11, 10, 3)
+STORED_STEPS = (6, 2, 5, 5, 11, 13)
 
 srl = lax.shift_right_logical
 
@@ -100,37 +100,50 @@
     return total
 
 
+NARROW = (0, 4, 1, 6, 2, 8)
+NARROW_ROWS = ((0, 24), (24, 8), (48, 8), (56, 8), (64, 16), (104, 8))
+
+
 def product_kernel(plan, count):
+    wide = plan.widths[3]
+    part = chunk_of(wide, plan.block, PART)
+    trips = wide // part
+
     def kernel(*refs):
         data = refs[:9]
-        weights = refs[9:14]
-        fill_refs = refs[14:16]
+        aif, daf, aof, kvb, gub = refs[9:14]
+        table, seeds = refs[14:16]
         out, tiles, bases = refs[16:19]
-        bufs = refs[19:28]
-        sems = refs[28]
-        factor_bufs = refs[29:34]
-        aif, daf, aof, kvb, gub = factor_bufs
-        table, seeds = fill_refs
-        order = [(0, lambda c: rows_of([aif[i, :, c] for i in (0, 1, 2)]), (0,)),
-                 (4, lambda c: aof[0, :, c], (24,)),
-                 (5, lambda c: rows_of([kvb[i, :, c] for i in (0, 1)]), (32, 40)),
-                 (1, lambda c: aif[3, :, c], (48,)),
-                 (6, lambda c: aof[1, :, c], (56,)),
-                 (2, lambda c: rows_of([aif[i, :, c] for i in (4, 5)]), (64,)),
-                 (7, lambda c: rows_of([gub[i, :, c] for i in (0, 1)]), (80, 88)),
-                 (3, lambda c: daf[:, c], (96,)),
-                 (8, lambda c: aof[2, :, c], (104,))]
-        copies = []
-        for arg, _, _ in order:
-            width = plan.widths[arg]
-            step = chunk_of(width, plan.block)
-            for start in range(0, width, step):
-                view = (slice(None),) * (len(data[arg].shape) - 1) + (pl.ds(start, step),)
-                copies.append((arg, start, step, pltpu.make_async_copy(
-                    data[arg].at[view], bufs[arg].at[view], sems.at[len(copies)])))
-        loads = [pltpu.make_async_copy(weights[i], factor_bufs[i], sems.at[len(copies) + i]) for i in range(5)]
-        for copy in loads + [copy[3] for copy in copies]:
-            copy.start()
+        narrow, kv, gate_up, down, narrow_sems, wide_sems = refs[19:25]
+        narrow_fac, kv_fac, gate_up_fac, down_fac, fac_sems = refs[25:30]
+        fill_refs = (bases,) + refs[30:]
+        pairs = [(aif.at[0], narrow_fac.at[0, pl.ds(0, RANK)]), (aif.at[1], narrow_fac.at[0, pl.ds(RANK, RANK)]),
+                 (aif.at[2], narrow_fac.at[0, pl.ds(2 * RANK, RANK)]), (aof.at[0], narrow_fac.at[1, pl.ds(0, RANK)]),
+                 (aif.at[3], narrow_fac.at[2, pl.ds(0, RANK)]), (aof.at[1], narrow_fac.at[3, pl.ds(0, RANK)]),
+                 (aif.at[4], narrow_fac.at[4, pl.ds(0, RANK)]), (aif.at[5], narrow_fac.at[4, pl.ds(RANK, RANK)]),
+                 (aof.at[2], narrow_fac.at[5, pl.ds(0, RANK)]), (daf, down_fac)]
+        pairs += [(kvb.at[i], kv_fac.at[pl.ds(i * RANK, RANK)]) for i in range(2)]
+        pairs += [(gub.at[i], gate_up_fac.at[pl.ds(i * RANK, RANK)]) for i in range(2)]
+        loads = [pltpu.make_async_copy(x, y, fac_sems.at[n]) for n, (x, y) in enumerate(pairs)]
+        loads += [pltpu.make_async_copy(data[arg], narrow.at[n], narrow_sems.at[n]) for n, arg in enumerate(NARROW)]
+        loads.append(pltpu.make_async_copy(data[5], kv, narrow_sems.at[len(NARROW)]))
+
+        def wide_copies(j):
+            cols = pl.ds(pl.multiple_of(j * part, LANES), part)
+            return [
+                pltpu.make_async_copy(data[7].at[:, :, cols], gate_up.at[:, :, cols], wide_sems.at[0, j]),
+                pltpu.make_async_copy(data[3].at[:, cols], down.at[:, cols], wide_sems.at[1, j]),
+            ]
+
+        for load in loads:
+            load.start()
+
+        def begin(j, carry):
+            for copy in wide_copies(j):
+                copy.start()
+            return carry
+
+        lax.fori_loop(0, trips, begin, 0)
         block = plan.first_own()
         for n in range(plan.steps // RANK):
             parts = plan.block // plan.sub
@@ -138,28 +151,36 @@
             feature = lax.axis_index("mp") * table[2, block + n // parts] + table[1, block + n // parts]
             feature = feature + (n % parts) * plan.sub
             bases[n] = seeds[seg] * SEED_MULT + feature * wrapped(RANK * ROW_MULT)
-        finish = fill_tables(plan, 0, count, (bases,) + refs[34:], tiles)
+
+        def contract(left, right):
+            return lax.dot_general(left, right, (((1,), (1,)), ((), ())), preferred_element_type=jnp.float32)
+
+        def wide_part(j, carry):
+            for copy in wide_copies(j):
+                copy.wait()
+            cols = pl.ds(pl.multiple_of(j * part, LANES), part)
+            both = gate_up[:, :, cols].reshape(2 * plan.tokens, part)
+            return carry[0] + contract(gate_up_fac[:, cols], both), carry[1] + contract(down_fac[:, cols], down[:, cols])
+
+        zero = jnp.zeros((2 * RANK, 2 * plan.tokens), jnp.float32), jnp.zeros((RANK, plan.tokens), jnp.float32)
+        finish = fill_tables(plan, 0, count, fill_refs, tiles)
         for load in loads:
             load.wait()
-        for arg, factor, places in order:
-            total = None
-            for one, start, step, copy in copies:
-                if one != arg:
-                    continue
-                copy.wait()
-                cols = pl.ds(start, step)
-                if len(data[arg].shape) == 3:
-                    right = bufs[arg][:, :, cols].reshape(2 * plan.tokens, step)
-                else:
-                    right = bufs[arg][:, cols]
-                part = lax.dot_general(factor(cols), right, (((1,), (1,)), ((), ())),
-                                       preferred_element_type=jnp.float32)
-                total = part if total is None else total + part
-            if len(places) == 2:
-                for i, place in enumerate(places):
-                    out[place:place + RANK, :] = every_other(total[i * RANK:(i + 1) * RANK], i)
-            else:
-                out[places[0]:places[0] + total.shape[0], :] = total
+
+        def narrow_part(n, carry):
+            sums[n] = contract(narrow_fac[n], narrow[n])
+            return carry
+
+        sums = refs[-1]
+        lax.fori_loop(0, len(NARROW), narrow_part, 0)
+        for n, (place, rows) in enumerate(NARROW_ROWS):
+            out[place:place + rows, :] = sums[n, 0:rows]
+        kv_sum = contract(kv_fac[...], kv[...].reshape(2 * plan.tokens, plan.widths[5]))
+        gate_up_sum, down_sum = lax.fori_loop(0, trips, wide_part, zero)
+        out[96:104, :] = down_sum
+        for i in range(2):
+            out[32 + i * RANK:32 + (i + 1) * RANK, :] = every_other(kv_sum[i * RANK:(i + 1) * RANK], i)
+            out[80 + i * RANK:80 + (i + 1) * RANK, :] = every_other(gate_up_sum[i * RANK:(i + 1) * RANK], i)
         finish()
 
     return kernel
@@ -186,10 +207,21 @@
             tiles_shape(plan, total),
             jax.ShapeDtypeStruct((plan.steps // RANK,), jnp.int32),
         ],
-        scratch_shapes=data_buffers(plan, data)
-        + [pltpu.SemaphoreType.DMA((copy_count(plan) + 5,))]
-        + [pltpu.VMEM(x.shape, x.dtype) for x in factors]
-        + fill_scratch(plan, count),
+        scratch_shapes=[
+            pltpu.VMEM((len(NARROW),) + data[0].shape, jnp.bfloat16),
+            pltpu.VMEM(data[5].shape, jnp.bfloat16),
+            pltpu.VMEM(data[7].shape, jnp.bfloat16),
+            pltpu.VMEM(data[3].shape, jnp.bfloat16),
+            pltpu.SemaphoreType.DMA((len(NARROW) + 1,)),
+            pltpu.SemaphoreType.DMA((2, plan.widths[3] // chunk_of(plan.widths[3], plan.block, PART))),
+            pltpu.VMEM((len(NARROW), 3 * RANK, plan.widths[0]), jnp.bfloat16),
+            pltpu.VMEM((2 * RANK, plan.widths[5]), jnp.bfloat16),
+            pltpu.VMEM((2 * RANK, plan.widths[7]), jnp.bfloat16),
+            pltpu.VMEM((RANK, plan.widths[3]), jnp.bfloat16),
+            pltpu.SemaphoreType.DMA((14,)),
+        ]
+        + fill_scratch(plan, count)
+        + [pltpu.VMEM((len(NARROW), 3 * RANK, plan.tokens), jnp.float32)],
         name="products",
     )(*data, *factors, table, seeds)
 
@@ -278,12 +310,14 @@
 
 
 def row_offsets(plan):
-    return lax.broadcasted_iota(jnp.int32, (plan.sub, COLS), 0) * wrapped(RANK * ROW_MULT)
+    return lax.broadcasted_iota(jnp.int32, (plan.sub, LANES), 0) * wrapped(RANK * ROW_MULT)
 
 
 def step_keys(step, bases, offsets):
-    key = bases[step // RANK] + (step % RANK) * ROW_MULT + offsets
-    return key ^ srl(key, 16)
+    turn = wrapped(step % RANK * ROW_MULT) if isinstance(step, int) else (step % RANK) * ROW_MULT
+    key = bases[step // RANK] + turn + offsets
+    key = key ^ srl(key, 16)
+    return jnp.concatenate([key] * (COLS // LANES), axis=1)
 
 
 def column_keys(copies=1):
@@ -317,6 +351,7 @@
 COLS = 256
 LANES = 128
 PAIR = 2
+PART = 1536
 
 
 def fill_step(step, bases, row_base, col_base, tile):
@@ -328,7 +363,7 @@
 
 
 def fill_tables(plan, first, count, refs, out):
-    bases, row_base, col_base, tiles, sems = refs
+    bases, row_base, col_base, tiles, sems = refs[:5]
     row_base[...] = row_offsets(plan)
     col_base[...] = column_keys(RANK)
 
@@ -348,7 +383,7 @@
 
 def fill_scratch(plan, count):
     return [
-        pltpu.VMEM((plan.sub, COLS), jnp.int32),
+        pltpu.VMEM((plan.sub, LANES), jnp.int32),
         pltpu.VMEM((RANK, K), jnp.int32),
         pltpu.VMEM((count, K // LANES, plan.sub, LANES), jnp.bfloat16),
         pltpu.SemaphoreType.DMA((count,)),
@@ -458,7 +493,7 @@
         out_shape=jax.ShapeDtypeStruct((devices, plan.examples, K // devices), jnp.float32),
         scratch_shapes=[
             pltpu.VMEM((depth, K), jnp.float32),
-            pltpu.VMEM((plan.sub, COLS), jnp.int32),
+            pltpu.VMEM((plan.sub, LANES), jnp.int32),
             pltpu.VMEM((RANK, K), jnp.int32),
         ],
         name="project",
@@ -476,7 +511,7 @@
     mask, seeds = args[14:16]
     plan = Plan(tuple(x.shape[-1] for x in data), data[0].shape[0], lax.axis_size("proj"))
     table = jnp.asarray(plan.table)
-    counts = [max(1, c * plan.steps // 128) for c in STORED_STEPS][:3 + len(plan.bits)]
+    counts = [max(1, c * plan.steps // 128) for c in STORED_STEPS][:6]
     counts[-1] += sum(counts) % PAIR
     starts = [sum(counts[:n]) for n in range(len(counts))]
     stored = sum(counts)
@@ -497,8 +532,9 @@
     keep, send, tiles = gradients(
         plan, data, own, other, mask.reshape(1, -1), plan.bits[0], bases, starts[2], counts[2], tiles)
     j = lax.axis_index("proj")
+    low = len(plan.bits[:2])
     x = None
-    for number, bit in enumerate(plan.bits):
+    for number, bit in enumerate(plan.bits[:2]):
         if number > 0:
             half = x.shape[0] // 2
             side = (j >> bit) & 1
@@ -506,6 +542,16 @@
             keep = lax.dynamic_slice_in_dim(x, side * half, half, 0)
         received = cover(swap(send, "proj", bit), send, number + 3)
         x = keep + received
+    ways = plan.group >> low
+    if ways > 1:
+        size = x.shape[0] // ways
+        place = (j >> low) % ways
+        sends = [lax.dynamic_slice_in_dim(x, (place ^ d) * size, size, 0) for d in range(ways)]
+        got = [lax.ppermute(sends[d], "proj", [(i, i ^ (d << low)) for i in range(plan.owners)]) for d in range(1, ways)]
+        got = cover(got, sends[0], low + 3)
+        x = sends[0]
+        for one in got:
+            x = x + one
     x = x[None]
     if plan.examples > 1:
         groups = [[e * plan.group + i for e in range(plan.examples)] for i in range(plan.group)]

time: 179 us -> 174 us (0.972)
  Pallas kernels: 156 us -> 149 us
    ppermute x0 -> x3, starting transfers between devices: none -> 4.39 us  [shards(): lax.ppermute(sends[d], 'proj', [(i, i ^ d << low) for i in range(plan.own...]
    ppermute x5 -> x3, starting transfers between devices: 8.41 us -> 4.69 us  [swap(): return lax.ppermute(x, axis, [(i, i ^ 1 << bit) for i in range(size)])]
    pallas_call x5 -> x4, Pallas kernels: 39.8 us -> 36.8 us  [stored_table(): pl.pallas_call(kernel, in_specs=[smem, anywhere, anywhere], out_specs=any...]
    pallas_call x1, Pallas kernels: 16.6 us -> 14.2 us  [products(): pl.pallas_call(product_kernel(plan, count), in_specs=[anywhere] * 14 + [s...]
  transfers between devices with their start and end apart: 5 -> 6, of which waited for: 1 -> 1; matrix products, arithmetic and copies ran while one was open for 0% -> 0% of each run, Pallas kernels for 22% -> 21%
where the time goes in v4:
time: 174 us
  Pallas kernels  149 us (86%)
  blocking collectives  12.3 us (7%)
  starting transfers between devices  9.07 us (5%)
    pallas_call x1, Pallas kernels, project(): pl.pallas_call(kernel, grid=(rounds,), in_specs=[smem, pl.BlockSpec((plan...  87.1 us
    pallas_call x4, Pallas kernels, stored_table(): pl.pallas_call(kernel, in_specs=[smem, anywhere, anywhere], out_specs=any...  36.8 us
    pallas_call x1, Pallas kernels, products(): pl.pallas_call(product_kernel(plan, count), in_specs=[anywhere] * 14 + [s...  14.2 us
    all_to_all x1, blocking collectives, shards(): got = lax.all_to_all(pieces, ('mp', 'proj'), 0, 0, tiled=True)  12.3 us
    pallas_call x1, Pallas kernels, gradients(): pl.pallas_call(gradient_kernel(plan, split, first, count), in_specs=[anyw...  10.8 us
    ppermute x3, starting transfers between devices, swap(): return lax.ppermute(x, axis, [(i, i ^ 1 << bit) for i in range(size)])  4.69 us
    ppermute x3, starting transfers between devices, shards(): lax.ppermute(sends[d], 'proj', [(i, i ^ d << low) for i in range(plan.own...  4.39 us
  transfers between devices with their start and end apart: 6, of which 1 were waited for; matrix products, arithmetic and copies ran while one was open for 0% of the time, Pallas kernels for 21%

profile of v4, /device:TPU:0, one launch (start us, length us, event | category | flops | bytes accessed | tf_op | source)
XLA Modules:
  0.0 173.8 jit_solution(10712789994330463671)
XLA Ops:
  0.0 14.2 %products.1 = (f32[112,128]{1,0:T(8,128)}, bf16[42,16,256,128]{3,2,1,0:T(8,128)(2,1)}, s32[16]{0:T(128)}) custom-call(bf16[128,2560]{1,0:T(8,128)(2,1)} %refs_0_.3, bf16[128,2560]{1,0:T(8,128)(2,1)} %refs_1_.3, bf16[128,2560]{1,0:T(8,128)(2,1)} %refs_2_.3, bf16[128,13824]{1,0:T(8,128)(2,1)} %refs_3_.3, bf16[128,2560]{1,0:T(8,128)(2,1)} %refs_4_.3, ...), custom_call_target="tpu_custom_call" | custom-call | tf_op jit(solution)/shard_map/products/pallas_call | solution.py:201
  14.2 3.0 %collective-permute-start = (f32[112,128]{1,0:T(8,128)}, f32[112,128]{1,0:T(8,128)S(1)}, u32[]{:S(2)}, u32[]{:S(2)}) collective-permute-start(f32[112,128]{1,0:T(8,128)} %get-tuple-element.22.after.refs_9_), channel_id=1, source_target_pairs={{0,16},{16,0},{1,17},{17,1},{2,18},{18,2},{3,19},{19,3},{4,20},{20... | collective-permute-start | bytes 172040 | tf_op jit(solution)/shard_map/ppermute | solution.py:505
  17.2 3.6 %stored_table.4.refs_13_ = bf16[42,16,256,128]{3,2,1,0:T(8,128)(2,1)} custom-call(s32[16]{0:T(128)} %get-tuple-element.21.bases.refs_12_, f32[112,128]{1,0:T(8,128)} %get-tuple-element.22.after.refs_9_, bf16[42,16,256,128]{3,2,1,0:T(8,128)(2,1)} %get-tuple-element.23.so_far), custom_call_target="tpu_custom_call", output_to_operand_aliasing={{}: (2, {})} | custom-call | tf_op jit(solution)/shard_map/stored_table/pallas_call | solution.py:404
  20.8 0.0 collective-permute-done.refs_10_
  20.8 0.0 copy-start.3
  20.9 0.6 copy-done.3
  21.5 10.8 %gradients.1 = (f32[64,8,512]{2,1,0:T(8,128)}, f32[64,8,512]{2,1,0:T(8,128)}, bf16[42,16,256,128]{3,2,1,0:T(8,128)(2,1)}) custom-call(bf16[128,2560]{1,0:T(8,128)(2,1)} %refs_0_.3, bf16[128,2560]{1,0:T(8,128)(2,1)} %refs_1_.3, bf16[128,2560]{1,0:T(8,128)(2,1)} %refs_2_.3, bf16[128,13824]{1,0:T(8,128)(2,1)} %refs_3_.3, ...), custom_call_target="tpu_custom_call", output_to_operand_aliasing={{2}: (13, {})} | custom-call | tf_op jit(solution)/shard_map/gradients/pallas_call | solution.py:295
  32.2 0.1 collective-permute-start.1
  32.3 0.0 copy-start.2
  32.3 6.6 %stored_table.5.so_far = bf16[42,16,256,128]{3,2,1,0:T(8,128)(2,1)} custom-call(s32[16]{0:T(128)} %get-tuple-element.21.bases.refs_12_, f32[64,8,512]{2,1,0:T(8,128)} %get-tuple-element.27.after, bf16[42,16,256,128]{3,2,1,0:T(8,128)(2,1)} %get-tuple-element.28.so_far), custom_call_target="tpu_custom_call", output_to_operand_aliasing={{}: (2, {})} | custom-call | tf_op jit(solution)/shard_map/stored_table/pallas_call | solution.py:404
  39.0 0.0 collective-permute-done.1
  39.0 0.0 copy-done.2
  39.0 0.2 add.37
  39.2 0.0 copy-start
  39.3 1.6 collective-permute-start.2
  40.8 0.0 copy-done
  40.8 12.3 %stored_table.6.so_far = bf16[42,16,256,128]{3,2,1,0:T(8,128)(2,1)} custom-call(s32[16]{0:T(128)} %get-tuple-element.21.bases.refs_12_, f32[32,8,512]{2,1,0:T(8,128)} %copy-done, bf16[42,16,256,128]{3,2,1,0:T(8,128)(2,1)} %stored_table.5.so_far), custom_call_target="tpu_custom_call", output_to_operand_aliasing={{}: (2, {})} | custom-call | tf_op jit(solution)/shard_map/stored_table/pallas_call | solution.py:404
  53.1 0.5 collective-permute-done.2
  53.6 0.1 dynamic-slice_add_fusion
  53.7 0.7 constant_dynamic-slice_fusion.3
  54.4 1.6 collective-permute-start.3
  56.0 2.6 %collective-permute-start.4 = (f32[8,8,512]{2,1,0:T(8,128)S(1)}, f32[8,8,512]{2,1,0:T(8,128)S(1)}, u32[]{:S(2)}, u32[]{:S(2)}) collective-permute-start(f32[8,8,512]{2,1,0:T(8,128)S(1)} %get-tuple-element.39), channel_id=1, source_target_pairs={{0,8},{1,9},{2,10},{3,11},{4,12},{5,13},{6,14},{7,15},{8,0},{9,1},... | collective-permute-start | bytes 393224 | tf_op jit(solution)/shard_map/ppermute | solution.py:550
  58.6 0.2 collective-permute-start.5
  58.8 0.0 copy-start.1
  58.8 14.3 %stored_table.7.tiles = bf16[42,16,256,128]{3,2,1,0:T(8,128)(2,1)} custom-call(s32[16]{0:T(128)} %get-tuple-element.21.bases.refs_12_, f32[8,8,512]{2,1,0:T(8,128)} %get-tuple-element.37.after, bf16[42,16,256,128]{3,2,1,0:T(8,128)(2,1)} %stored_table.6.so_far), custom_call_target="tpu_custom_call", output_to_operand_aliasing={{}: (2, {})} | custom-call | tf_op jit(solution)/shard_map/stored_table/pallas_call | solution.py:404
  73.1 0.0 collective-permute-done.3
  73.1 0.0 collective-permute-done.4
  73.1 0.0 collective-permute-done.5
  73.1 0.0 copy-done.1
  73.1 0.7 add_bitcast_fusion.grads.old_grads
  73.8 87.1 %project.1 = f32[32,1,64]{2,1,0:T(1,128)} custom-call(s32[16]{0:T(128)} %get-tuple-element.21.bases.refs_12_, f32[1,8,8,512]{3,2,1,0:T(8,128)} %add_bitcast_fusion.grads.old_grads, f32[1,8,8,512]{3,2,1,0:T(8,128)} %add_bitcast_fusion.grads.old_grads, bf16[42,16,256,128]{3,2,1,0:T(8,128)(2,1)} %stored_table.7.tiles), custom_call_target="tpu_custom_call" | custom-call | tf_op jit(solution)/shard_map/project/pallas_call | solution.py:483
  161.0 12.3 %all_to_all.5 = f32[32,1,64]{2,1,0:T(1,128)S(1)} all-to-all(f32[32,1,64]{2,1,0:T(1,128)} %project.1), channel_id=1, replica_groups=mesh['mp'=2,'proj'=16] {'mp','proj'}, dimensions={0} | all-to-all | bytes 16384 | tf_op jit(solution)/shard_map/all_to_all | solution.py:563
  173.2 0.6 reduce_sum.11
  (1 shorter events, 0.0 us)
Async XLA Ops:
  14.2 6.7 %collective-permute-start = (f32[112,128]{1,0:T(8,128)}, f32[112,128]{1,0:T(8,128)S(1)}, u32[]{:S(2)}, u32[]{:S(2)}) collective-permute-start(f32[112,128]{1,0:T(8,128)} %get-tuple-element.22.after.refs_9_), channel_id=1, source_target_pairs={{0,16},{16,0},{1,17},{17,1},{2,18},{18,2},{3,19},{19,3},{4,20},{20... | collective-permute-start | bytes 172040 | tf_op jit(solution)/shard_map/ppermute | solution.py:505
  20.8 0.6 copy-start.3
  32.2 6.7 %collective-permute-start.1 = (f32[64,8,512]{2,1,0:T(8,128)}, f32[64,8,512]{2,1,0:T(8,128)S(1)}, u32[]{:S(2)}, u32[]{:S(2)}) collective-permute-start(f32[64,8,512]{2,1,0:T(8,128)} %get-tuple-element.27.after), channel_id=1, source_target_pairs={{0,1},{1,0},{2,3},{3,2},{4,5},{5,4},{6,7},{7,6},{8,9},{9,8},{10,11... | collective-permute-start | bytes 3145736 | tf_op jit(solution)/shard_map/ppermute | solution.py:505
  32.3 6.7 %copy-start.2 = (f32[64,8,512]{2,1,0:T(8,128)S(1)}, f32[64,8,512]{2,1,0:T(8,128)}, u32[]{:S(2)}) copy-start(f32[64,8,512]{2,1,0:T(8,128)} %get-tuple-element.26) | copy-start | bytes 3145732
  39.2 1.6 copy-start
  39.3 14.4 %collective-permute-start.2 = (f32[32,8,512]{2,1,0:T(8,128)S(1)}, f32[32,8,512]{2,1,0:T(8,128)S(1)}, u32[]{:S(2)}, u32[]{:S(2)}) collective-permute-start(f32[32,8,512]{2,1,0:T(8,128)S(1)} %constant_dynamic-slice_fusion.4.after), channel_id=1, source_target_pairs={{0,2},{1,3},{2,0},{3,1},{4,6},{5,7},{6,4},{7,5},{8,10},{9,11},{10,... | collective-permute-start | bytes 1572872 | tf_op jit(solution)/shard_map/ppermute | solution.py:505
  54.4 18.7 %collective-permute-start.3 = (f32[8,8,512]{2,1,0:T(8,128)S(1)}, f32[8,8,512]{2,1,0:T(8,128)S(1)}, u32[]{:S(2)}, u32[]{:S(2)}) collective-permute-start(f32[8,8,512]{2,1,0:T(8,128)S(1)} %get-tuple-element.40), channel_id=1, source_target_pairs={{0,4},{1,5},{2,6},{3,7},{4,0},{5,1},{6,2},{7,3},{8,12},{9,13},{10,... | collective-permute-start | bytes 393224 | tf_op jit(solution)/shard_map/ppermute | solution.py:550
  56.0 17.1 %collective-permute-start.4 = (f32[8,8,512]{2,1,0:T(8,128)S(1)}, f32[8,8,512]{2,1,0:T(8,128)S(1)}, u32[]{:S(2)}, u32[]{:S(2)}) collective-permute-start(f32[8,8,512]{2,1,0:T(8,128)S(1)} %get-tuple-element.39), channel_id=1, source_target_pairs={{0,8},{1,9},{2,10},{3,11},{4,12},{5,13},{6,14},{7,15},{8,0},{9,1},... | collective-permute-start | bytes 393224 | tf_op jit(solution)/shard_map/ppermute | solution.py:550
  58.6 14.5 %collective-permute-start.5 = (f32[8,8,512]{2,1,0:T(8,128)S(1)}, f32[8,8,512]{2,1,0:T(8,128)S(1)}, u32[]{:S(2)}, u32[]{:S(2)}) collective-permute-start(f32[8,8,512]{2,1,0:T(8,128)S(1)} %get-tuple-element.38), channel_id=1, source_target_pairs={{0,12},{1,13},{2,14},{3,15},{4,8},{5,9},{6,10},{7,11},{8,4},{9,5},... | collective-permute-start | bytes 393224 | tf_op jit(solution)/shard_map/ppermute | solution.py:550
  58.8 14.3 %copy-start.1 = (f32[8,8,512]{2,1,0:T(8,128)S(1)}, f32[8,8,512]{2,1,0:T(8,128)}, u32[]{:S(2)}) copy-start(f32[8,8,512]{2,1,0:T(8,128)} %get-tuple-element.37.after) | copy-start | bytes 393220

commit v5 on v4

--- a/solution.py
+++ b/solution.py
@@ -236,11 +236,13 @@
         grads, sems, out_sems = refs[26:29]
         fill_refs = (bases,) + refs[29:]
         copies = {}
+        numbers = {}
         number = 0
         for arg, _, _, width in plan.pieces:
             step = chunk_of(width, plan.block)
             for start in range(0, width, step):
                 view = (slice(None),) * (len(data[arg].shape) - 1) + (pl.ds(start, step),)
+                numbers[arg, start] = number
                 copies[arg, start] = pltpu.make_async_copy(data[arg].at[view], bufs[arg].at[view], sems.at[number])
                 number += 1
         for copy in copies.values():
@@ -250,7 +252,7 @@
         turned = total * mask[...].astype(jnp.float32)
         tokens = plan.tokens
         half = plan.blocks // 2
-        for arg, places, segs, width in plan.pieces:
+        def left_of(arg, places):
             left = rows_of([turned[p:p + RANK] for p in places]).astype(jnp.bfloat16)
             if len(data[arg].shape) == 3:
                 t = lax.broadcasted_iota(jnp.int32, (tokens, 2 * tokens), 0)
@@ -261,23 +263,45 @@
                     one = turned[places[i]:places[i] + RANK].astype(jnp.bfloat16)
                     parts.append(jnp.dot(one, spread, preferred_element_type=jnp.float32))
                 left = rows_of(parts).astype(jnp.bfloat16)
+            return left
+
+        def one_part(arg, left, segs, start, step, copy):
+            copy.wait()
+            cols = pl.ds(start, step)
+            if len(data[arg].shape) == 3:
+                right = bufs[arg][:, :, cols].reshape(2 * tokens, step)
+            else:
+                right = bufs[arg][:, cols]
+            got = jnp.dot(left, right, preferred_element_type=jnp.float32)
+            for i, seg in enumerate(segs):
+                for k in range(step // plan.block):
+                    grads[plan.first_block[seg] + start // plan.block + k] = got[
+                        i * RANK:(i + 1) * RANK, k * plan.block:(k + 1) * plan.block]
+
+        looped = [piece for piece in plan.pieces if piece[0] in (3, 7)]
+        for arg, places, segs, width in plan.pieces:
+            if (arg, places, segs, width) in looped:
+                continue
             step = chunk_of(width, plan.block)
+            left = left_of(arg, places)
             for start in range(0, width, step):
-                copies[arg, start].wait()
-                cols = pl.ds(start, step)
-                if len(data[arg].shape) == 3:
-                    right = bufs[arg][:, :, cols].reshape(2 * tokens, step)
-                else:
-                    right = bufs[arg][:, cols]
-                got = jnp.dot(left, right, preferred_element_type=jnp.float32)
-                for i, seg in enumerate(segs):
-                    for k in range(step // plan.block):
-                        block = plan.first_block[seg] + start // plan.block + k
-                        grads[block // half, block % half] = got[
-                            i * RANK:(i + 1) * RANK, k * plan.block:(k + 1) * plan.block]
+                one_part(arg, left, segs, start, step, copies[arg, start])
+        lefts = [left_of(arg, places) for arg, places, _, _ in looped]
+        step = chunk_of(looped[0][3], plan.block)
+
+        def trip(n, carry):
+            start = pl.multiple_of(n * step, LANES)
+            for (arg, _, segs, _), left in zip(looped, lefts):
+                view = (slice(None),) * (len(data[arg].shape) - 1) + (pl.ds(start, step),)
+                copy = pltpu.make_async_copy(
+                    data[arg].at[view], bufs[arg].at[view], sems.at[numbers[arg, 0] + n])
+                one_part(arg, left, segs, start, step, copy)
+            return carry
+
+        lax.fori_loop(0, looped[0][3] // step, trip, 0)
         bit = (lax.axis_index("proj") >> split) & 1
-        sent = pltpu.make_async_copy(grads.at[1 - bit], send, out_sems.at[0])
-        kept = pltpu.make_async_copy(grads.at[bit], keep, out_sems.at[1])
+        sent = pltpu.make_async_copy(grads.at[pl.ds((1 - bit) * half, half)], send, out_sems.at[0])
+        kept = pltpu.make_async_copy(grads.at[pl.ds(bit * half, half)], keep, out_sems.at[1])
         sent.start()
         kept.start()
         finish()
@@ -299,7 +323,7 @@
         out_shape=[half, half, jax.ShapeDtypeStruct(so_far.shape, so_far.dtype)],
         scratch_shapes=data_buffers(plan, data)
         + [
-            pltpu.VMEM((2, plan.blocks // 2, RANK, plan.block), jnp.float32),
+            pltpu.VMEM((plan.blocks, RANK, plan.block), jnp.float32),
             pltpu.SemaphoreType.DMA((copy_count(plan),)),
             pltpu.SemaphoreType.DMA((2,)),
         ]
@@ -351,7 +375,7 @@
 COLS = 256
 LANES = 128
 PAIR = 2
-PART = 1536
+PART = 4608
 
 
 def fill_step(step, bases, row_base, col_base, tile):
@@ -529,6 +553,7 @@
         own = lax.psum(own, "mp")
         other = jnp.zeros_like(own)
     other = cover(other, own, 1)
+    other = pltpu.with_memory_space_constraint(other, pltpu.VMEM)
     keep, send, tiles = gradients(
         plan, data, own, other, mask.reshape(1, -1), plan.bits[0], bases, starts[2], counts[2], tiles)
     j = lax.axis_index("proj")

time: 174 us -> 173 us (level)
  no operation moved by 1% of the time
where the time goes in v5:
time: 173 us
  Pallas kernels  149 us (86%)
  blocking collectives  12.3 us (7%)
  starting transfers between devices  9.07 us (5%)
    pallas_call x1, Pallas kernels, project(): pl.pallas_call(kernel, grid=(rounds,), in_specs=[smem, pl.BlockSpec((plan...  87.1 us
    pallas_call x4, Pallas kernels, stored_table(): pl.pallas_call(kernel, in_specs=[smem, anywhere, anywhere], out_specs=any...  36.8 us
    pallas_call x1, Pallas kernels, products(): pl.pallas_call(product_kernel(plan, count), in_specs=[anywhere] * 14 + [s...  13 us
    all_to_all x1, blocking collectives, shards(): got = lax.all_to_all(pieces, ('mp', 'proj'), 0, 0, tiled=True)  12.3 us
    pallas_call x1, Pallas kernels, gradients(): pl.pallas_call(gradient_kernel(plan, split, first, count), in_specs=[anyw...  11.8 us
    ppermute x3, starting transfers between devices, swap(): return lax.ppermute(x, axis, [(i, i ^ 1 << bit) for i in range(size)])  4.69 us
    ppermute x3, starting transfers between devices, shards(): lax.ppermute(sends[d], 'proj', [(i, i ^ d << low) for i in range(plan.own...  4.39 us
  transfers between devices with their start and end apart: 6, of which 1 were waited for; matrix products, arithmetic and copies ran while one was open for 0% of the time, Pallas kernels for 21%

profile of v5, /device:TPU:0, one launch (start us, length us, event | category | flops | bytes accessed | tf_op | source)
XLA Modules:
  0.0 173.1 jit_solution(15677338786160758540)
XLA Ops:
  0.0 13.0 %products.1 = (f32[112,128]{1,0:T(8,128)}, bf16[42,16,256,128]{3,2,1,0:T(8,128)(2,1)}, s32[16]{0:T(128)}) custom-call(bf16[128,2560]{1,0:T(8,128)(2,1)} %refs_0_.3, bf16[128,2560]{1,0:T(8,128)(2,1)} %refs_1_.3, bf16[128,2560]{1,0:T(8,128)(2,1)} %refs_2_.3, bf16[128,13824]{1,0:T(8,128)(2,1)} %refs_3_.3, bf16[128,2560]{1,0:T(8,128)(2,1)} %refs_4_.3, ...), custom_call_target="tpu_custom_call" | custom-call | tf_op jit(solution)/shard_map/products/pallas_call | solution.py:201
  13.0 3.0 %collective-permute-start = (f32[112,128]{1,0:T(8,128)}, f32[112,128]{1,0:T(8,128)S(1)}, u32[]{:S(2)}, u32[]{:S(2)}) collective-permute-start(f32[112,128]{1,0:T(8,128)} %get-tuple-element.22.after.refs_9_), channel_id=1, source_target_pairs={{0,16},{16,0},{1,17},{17,1},{2,18},{18,2},{3,19},{19,3},{4,20},{20... | collective-permute-start | bytes 172040 | tf_op jit(solution)/shard_map/ppermute | solution.py:529
  16.1 3.6 %stored_table.4.refs_13_ = bf16[42,16,256,128]{3,2,1,0:T(8,128)(2,1)} custom-call(s32[16]{0:T(128)} %get-tuple-element.21.bases.refs_12_, f32[112,128]{1,0:T(8,128)} %get-tuple-element.22.after.refs_9_, bf16[42,16,256,128]{3,2,1,0:T(8,128)(2,1)} %get-tuple-element.23.so_far), custom_call_target="tpu_custom_call", output_to_operand_aliasing={{}: (2, {})} | custom-call | tf_op jit(solution)/shard_map/stored_table/pallas_call | solution.py:428
  19.7 0.0 collective-permute-done.refs_10_
  19.7 11.8 %gradients.1 = (f32[64,8,512]{2,1,0:T(8,128)}, f32[64,8,512]{2,1,0:T(8,128)}, bf16[42,16,256,128]{3,2,1,0:T(8,128)(2,1)}) custom-call(bf16[128,2560]{1,0:T(8,128)(2,1)} %refs_0_.3, bf16[128,2560]{1,0:T(8,128)(2,1)} %refs_1_.3, bf16[128,2560]{1,0:T(8,128)(2,1)} %refs_2_.3, bf16[128,13824]{1,0:T(8,128)(2,1)} %refs_3_.3, ...), custom_call_target="tpu_custom_call", output_to_operand_aliasing={{2}: (13, {})} | custom-call | tf_op jit(solution)/shard_map/gradients/pallas_call | solution.py:319
  31.5 0.1 collective-permute-start.1
  31.6 0.0 copy-start.2
  31.6 6.6 %stored_table.5.so_far = bf16[42,16,256,128]{3,2,1,0:T(8,128)(2,1)} custom-call(s32[16]{0:T(128)} %get-tuple-element.21.bases.refs_12_, f32[64,8,512]{2,1,0:T(8,128)} %get-tuple-element.27.after, bf16[42,16,256,128]{3,2,1,0:T(8,128)(2,1)} %get-tuple-element.28.so_far), custom_call_target="tpu_custom_call", output_to_operand_aliasing={{}: (2, {})} | custom-call | tf_op jit(solution)/shard_map/stored_table/pallas_call | solution.py:428
  38.3 0.0 collective-permute-done.1
  38.3 0.0 copy-done.2
  38.3 0.2 add.37
  38.5 0.0 copy-start
  38.5 1.6 collective-permute-start.2
  40.1 0.0 copy-done
  40.1 12.3 %stored_table.6.so_far = bf16[42,16,256,128]{3,2,1,0:T(8,128)(2,1)} custom-call(s32[16]{0:T(128)} %get-tuple-element.21.bases.refs_12_, f32[32,8,512]{2,1,0:T(8,128)} %copy-done, bf16[42,16,256,128]{3,2,1,0:T(8,128)(2,1)} %stored_table.5.so_far), custom_call_target="tpu_custom_call", output_to_operand_aliasing={{}: (2, {})} | custom-call | tf_op jit(solution)/shard_map/stored_table/pallas_call | solution.py:428
  52.4 0.5 collective-permute-done.2
  52.9 0.1 dynamic-slice_add_fusion
  53.0 0.7 constant_dynamic-slice_fusion.3
  53.7 1.6 collective-permute-start.3
  55.3 2.6 %collective-permute-start.4 = (f32[8,8,512]{2,1,0:T(8,128)S(1)}, f32[8,8,512]{2,1,0:T(8,128)S(1)}, u32[]{:S(2)}, u32[]{:S(2)}) collective-permute-start(f32[8,8,512]{2,1,0:T(8,128)S(1)} %get-tuple-element.39), channel_id=1, source_target_pairs={{0,8},{1,9},{2,10},{3,11},{4,12},{5,13},{6,14},{7,15},{8,0},{9,1},... | collective-permute-start | bytes 393224 | tf_op jit(solution)/shard_map/ppermute | solution.py:575
  57.9 0.2 collective-permute-start.5
  58.1 0.0 copy-start.1
  58.1 14.3 %stored_table.7.tiles = bf16[42,16,256,128]{3,2,1,0:T(8,128)(2,1)} custom-call(s32[16]{0:T(128)} %get-tuple-element.21.bases.refs_12_, f32[8,8,512]{2,1,0:T(8,128)} %get-tuple-element.37.after, bf16[42,16,256,128]{3,2,1,0:T(8,128)(2,1)} %stored_table.6.so_far), custom_call_target="tpu_custom_call", output_to_operand_aliasing={{}: (2, {})} | custom-call | tf_op jit(solution)/shard_map/stored_table/pallas_call | solution.py:428
  72.4 0.0 collective-permute-done.3
  72.4 0.0 collective-permute-done.4
  72.4 0.0 collective-permute-done.5
  72.4 0.0 copy-done.1
  72.4 0.7 add_bitcast_fusion.grads.old_grads
  73.1 87.1 %project.1 = f32[32,1,64]{2,1,0:T(1,128)} custom-call(s32[16]{0:T(128)} %get-tuple-element.21.bases.refs_12_, f32[1,8,8,512]{3,2,1,0:T(8,128)} %add_bitcast_fusion.grads.old_grads, f32[1,8,8,512]{3,2,1,0:T(8,128)} %add_bitcast_fusion.grads.old_grads, bf16[42,16,256,128]{3,2,1,0:T(8,128)(2,1)} %stored_table.7.tiles), custom_call_target="tpu_custom_call" | custom-call | tf_op jit(solution)/shard_map/project/pallas_call | solution.py:507
  160.3 12.3 %all_to_all.5 = f32[32,1,64]{2,1,0:T(1,128)S(1)} all-to-all(f32[32,1,64]{2,1,0:T(1,128)} %project.1), channel_id=1, replica_groups=mesh['mp'=2,'proj'=16] {'mp','proj'}, dimensions={0} | all-to-all | bytes 16384 | tf_op jit(solution)/shard_map/all_to_all | solution.py:588
  172.5 0.6 reduce_sum.11
  (1 shorter events, 0.0 us)
Async XLA Ops:
  13.0 6.6 %collective-permute-start = (f32[112,128]{1,0:T(8,128)}, f32[112,128]{1,0:T(8,128)S(1)}, u32[]{:S(2)}, u32[]{:S(2)}) collective-permute-start(f32[112,128]{1,0:T(8,128)} %get-tuple-element.22.after.refs_9_), channel_id=1, source_target_pairs={{0,16},{16,0},{1,17},{17,1},{2,18},{18,2},{3,19},{19,3},{4,20},{20... | collective-permute-start | bytes 172040 | tf_op jit(solution)/shard_map/ppermute | solution.py:529
  31.5 6.7 %collective-permute-start.1 = (f32[64,8,512]{2,1,0:T(8,128)}, f32[64,8,512]{2,1,0:T(8,128)S(1)}, u32[]{:S(2)}, u32[]{:S(2)}) collective-permute-start(f32[64,8,512]{2,1,0:T(8,128)} %get-tuple-element.27.after), channel_id=1, source_target_pairs={{0,1},{1,0},{2,3},{3,2},{4,5},{5,4},{6,7},{7,6},{8,9},{9,8},{10,11... | collective-permute-start | bytes 3145736 | tf_op jit(solution)/shard_map/ppermute | solution.py:529
  31.6 6.7 %copy-start.2 = (f32[64,8,512]{2,1,0:T(8,128)S(1)}, f32[64,8,512]{2,1,0:T(8,128)}, u32[]{:S(2)}) copy-start(f32[64,8,512]{2,1,0:T(8,128)} %get-tuple-element.26) | copy-start | bytes 3145732
  38.5 1.6 copy-start
  38.5 14.4 %collective-permute-start.2 = (f32[32,8,512]{2,1,0:T(8,128)S(1)}, f32[32,8,512]{2,1,0:T(8,128)S(1)}, u32[]{:S(2)}, u32[]{:S(2)}) collective-permute-start(f32[32,8,512]{2,1,0:T(8,128)S(1)} %constant_dynamic-slice_fusion.4.after), channel_id=1, source_target_pairs={{0,2},{1,3},{2,0},{3,1},{4,6},{5,7},{6,4},{7,5},{8,10},{9,11},{10,... | collective-permute-start | bytes 1572872 | tf_op jit(solution)/shard_map/ppermute | solution.py:529
  53.7 18.7 %collective-permute-start.3 = (f32[8,8,512]{2,1,0:T(8,128)S(1)}, f32[8,8,512]{2,1,0:T(8,128)S(1)}, u32[]{:S(2)}, u32[]{:S(2)}) collective-permute-start(f32[8,8,512]{2,1,0:T(8,128)S(1)} %get-tuple-element.40), channel_id=1, source_target_pairs={{0,4},{1,5},{2,6},{3,7},{4,0},{5,1},{6,2},{7,3},{8,12},{9,13},{10,... | collective-permute-start | bytes 393224 | tf_op jit(solution)/shard_map/ppermute | solution.py:575
  55.3 17.1 %collective-permute-start.4 = (f32[8,8,512]{2,1,0:T(8,128)S(1)}, f32[8,8,512]{2,1,0:T(8,128)S(1)}, u32[]{:S(2)}, u32[]{:S(2)}) collective-permute-start(f32[8,8,512]{2,1,0:T(8,128)S(1)} %get-tuple-element.39), channel_id=1, source_target_pairs={{0,8},{1,9},{2,10},{3,11},{4,12},{5,13},{6,14},{7,15},{8,0},{9,1},... | collective-permute-start | bytes 393224 | tf_op jit(solution)/shard_map/ppermute | solution.py:575
  57.9 14.5 %collective-permute-start.5 = (f32[8,8,512]{2,1,0:T(8,128)S(1)}, f32[8,8,512]{2,1,0:T(8,128)S(1)}, u32[]{:S(2)}, u32[]{:S(2)}) collective-permute-start(f32[8,8,512]{2,1,0:T(8,128)S(1)} %get-tuple-element.38), channel_id=1, source_target_pairs={{0,12},{1,13},{2,14},{3,15},{4,8},{5,9},{6,10},{7,11},{8,4},{9,5},... | collective-permute-start | bytes 393224 | tf_op jit(solution)/shard_map/ppermute | solution.py:575
  58.1 14.3 %copy-start.1 = (f32[8,8,512]{2,1,0:T(8,128)S(1)}, f32[8,8,512]{2,1,0:T(8,128)}, u32[]{:S(2)}) copy-start(f32[8,8,512]{2,1,0:T(8,128)} %get-tuple-element.37.after) | copy-start | bytes 393220

commit v6 on v4

--- a/solution.py
+++ b/solution.py
@@ -17,7 +17,7 @@
 COL_MULT = -1640531535
 MIX_A = -2048144789
 MIX_B = -1028477387
-STORED_STEPS = (6, 2, 5, 5, 11, 13)
+STORED_STEPS = (5, 2, 5, 5, 11, 12)
 
 srl = lax.shift_right_logical
 
@@ -350,8 +350,8 @@
 
 COLS = 256
 LANES = 128
-PAIR = 2
-PART = 1536
+PAIR = 4
+PART = 4608
 
 
 def fill_step(step, bases, row_base, col_base, tile):
@@ -412,8 +412,16 @@
     )(bases, after, so_far)
 
 
+def round_sizes(plan, stored):
+    rounds = (plan.steps - stored) // PAIR
+    batch = 1
+    while batch * rounds < stored:
+        batch *= 2
+    return rounds, batch
+
+
 def project_kernel(plan, stored, scale, devices):
-    rounds = (plan.steps - stored) // PAIR
+    rounds, batch = round_sizes(plan, stored)
     depth = 2 * RANK * plan.examples
     parts = 4
     slab = plan.sub // parts
@@ -437,11 +445,13 @@
             row_base[...] = row_offsets(plan)
             col_base[...] = column_keys(RANK)
 
-        old = pick(old_grads, i)
-        old = jnp.where(i < stored, old.astype(jnp.float32), 0.0)
-        fix = jnp.sum(old, axis=1, keepdims=True)
-        old = (old * (1.0 / 65536.0)).astype(jnp.bfloat16)
-        lefts, rows = [], []
+        fix = 0.0
+        olds, lefts, rows = [], [], []
+        for q in range(batch):
+            old = pick(old_grads, batch * i + q)
+            old = jnp.where(batch * i + q < stored, old.astype(jnp.float32), 0.0)
+            fix = fix + jnp.sum(old, axis=1, keepdims=True)
+            olds.append((old * (1.0 / 65536.0)).astype(jnp.bfloat16))
         for p in range(PAIR):
             step = stored + PAIR * i + p
             rows.append(step_keys(step, bases, row_base[...]))
@@ -454,8 +464,9 @@
                 for n in range(parts):
                     planes = byte_planes(mixed(rows[p][n * slab:(n + 1) * slab], col_base[:, c:c + COLS]))
                     a = a + jnp.dot(lefts[p][n], rows_of(planes), preferred_element_type=jnp.float32)
-            tile = jnp.concatenate([tiles[0, (c + n) // LANES] for n in range(0, COLS, LANES)], axis=1)
-            a = a + jnp.dot(old, tile, preferred_element_type=jnp.float32)
+            for q in range(batch):
+                tile = jnp.concatenate([tiles[q, (c + n) // LANES] for n in range(0, COLS, LANES)], axis=1)
+                a = a + jnp.dot(olds[q], tile, preferred_element_type=jnp.float32)
             acc[:, c:c + COLS] = a
 
         @pl.when(i == rounds - 1)
@@ -467,11 +478,11 @@
                 for d in range(devices):
                     out[d, e:e + 1, :] = total[:, d * width:(d + 1) * width]
 
-    return kernel, depth, rounds
+    return kernel, depth, rounds, batch
 
 
 def project(plan, bases, grads, tiles, stored, scale, devices):
-    kernel, depth, rounds = project_kernel(plan, stored, scale, devices)
+    kernel, depth, rounds, batch = project_kernel(plan, stored, scale, devices)
     smem = pl.BlockSpec(memory_space=pltpu.SMEM)
     parts = plan.block // plan.sub
 
@@ -479,15 +490,15 @@
         number = step // RANK
         return (0, number // parts, 0, number % parts)
 
-    last = stored - 1
+    last = stored // batch - 1
     return pl.pallas_call(
         kernel,
         grid=(rounds,),
         in_specs=[
             smem,
             pl.BlockSpec((plan.examples, 1, RANK, plan.sub), lambda i: place(PAIR * i + stored)),
-            pl.BlockSpec((plan.examples, 1, RANK, plan.sub), lambda i: place(jnp.minimum(i, last))),
-            pl.BlockSpec((1, K // LANES, plan.sub, LANES), lambda i: (jnp.minimum(i, last), 0, 0, 0)),
+            pl.BlockSpec((plan.examples, 1, RANK, plan.sub), lambda i: place(jnp.minimum(i, last) * batch)),
+            pl.BlockSpec((batch, K // LANES, plan.sub, LANES), lambda i: (jnp.minimum(i, last), 0, 0, 0)),
         ],
         out_specs=pl.BlockSpec((devices, plan.examples, K // devices), lambda i: (0, 0, 0)),
         out_shape=jax.ShapeDtypeStruct((devices, plan.examples, K // devices), jnp.float32),
@@ -512,7 +523,7 @@
     plan = Plan(tuple(x.shape[-1] for x in data), data[0].shape[0], lax.axis_size("proj"))
     table = jnp.asarray(plan.table)
     counts = [max(1, c * plan.steps // 128) for c in STORED_STEPS][:6]
-    counts[-1] += sum(counts) % PAIR
+    counts[-1] += -sum(counts) % PAIR
     starts = [sum(counts[:n]) for n in range(len(counts))]
     stored = sum(counts)
     own, tiles, bases = products(plan, data, factors, table, seeds, counts[0], stored)
@@ -529,6 +540,7 @@
         own = lax.psum(own, "mp")
         other = jnp.zeros_like(own)
     other = cover(other, own, 1)
+    other = pltpu.with_memory_space_constraint(other, pltpu.VMEM)
     keep, send, tiles = gradients(
         plan, data, own, other, mask.reshape(1, -1), plan.bits[0], bases, starts[2], counts[2], tiles)
     j = lax.axis_index("proj")

time: 174 us -> 169 us (0.971)
  Pallas kernels: 149 us -> 145 us
    pallas_call x1, Pallas kernels: 14.2 us -> 12.1 us  [products(): pl.pallas_call(product_kernel(plan, count), in_specs=[anywhere] * 14 + [s...]
where the time goes in v6:
time: 169 us
  Pallas kernels  145 us (86%)
  blocking collectives  12.3 us (7%)
  starting transfers between devices  9.07 us (5%)
    pallas_call x1, Pallas kernels, project(): pl.pallas_call(kernel, grid=(rounds,), in_specs=[smem, pl.BlockSpec((plan...  86.2 us
    pallas_call x4, Pallas kernels, stored_table(): pl.pallas_call(kernel, in_specs=[smem, anywhere, anywhere], out_specs=any...  35.7 us
    all_to_all x1, blocking collectives, shards(): got = lax.all_to_all(pieces, ('mp', 'proj'), 0, 0, tiled=True)  12.3 us
    pallas_call x1, Pallas kernels, products(): pl.pallas_call(product_kernel(plan, count), in_specs=[anywhere] * 14 + [s...  12.1 us
    pallas_call x1, Pallas kernels, gradients(): pl.pallas_call(gradient_kernel(plan, split, first, count), in_specs=[anyw...  10.7 us
    ppermute x3, starting transfers between devices, swap(): return lax.ppermute(x, axis, [(i, i ^ 1 << bit) for i in range(size)])  4.69 us
    ppermute x3, starting transfers between devices, shards(): lax.ppermute(sends[d], 'proj', [(i, i ^ d << low) for i in range(plan.own...  4.39 us
  transfers between devices with their start and end apart: 6, of which 1 were waited for; matrix products, arithmetic and copies ran while one was open for 0% of the time, Pallas kernels for 21%

profile of v6, /device:TPU:0, one launch (start us, length us, event | category | flops | bytes accessed | tf_op | source)
XLA Modules:
  0.0 169.2 jit_solution(7454656995326896058)
XLA Ops:
  0.0 12.1 %products.1 = (f32[112,128]{1,0:T(8,128)}, bf16[40,16,256,128]{3,2,1,0:T(8,128)(2,1)}, s32[16]{0:T(128)}) custom-call(bf16[128,2560]{1,0:T(8,128)(2,1)} %refs_0_.3, bf16[128,2560]{1,0:T(8,128)(2,1)} %refs_1_.3, bf16[128,2560]{1,0:T(8,128)(2,1)} %refs_2_.3, bf16[128,13824]{1,0:T(8,128)(2,1)} %refs_3_.3, bf16[128,2560]{1,0:T(8,128)(2,1)} %refs_4_.3, ...), custom_call_target="tpu_custom_call" | custom-call | tf_op jit(solution)/shard_map/products/pallas_call | solution.py:201
  12.1 3.0 %collective-permute-start = (f32[112,128]{1,0:T(8,128)}, f32[112,128]{1,0:T(8,128)S(1)}, u32[]{:S(2)}, u32[]{:S(2)}) collective-permute-start(f32[112,128]{1,0:T(8,128)} %get-tuple-element.22.after.refs_9_), channel_id=1, source_target_pairs={{0,16},{16,0},{1,17},{17,1},{2,18},{18,2},{3,19},{19,3},{4,20},{20... | collective-permute-start | bytes 172040 | tf_op jit(solution)/shard_map/ppermute | solution.py:516
  15.1 3.6 %stored_table.4.refs_13_ = bf16[40,16,256,128]{3,2,1,0:T(8,128)(2,1)} custom-call(s32[16]{0:T(128)} %get-tuple-element.21.bases.refs_12_, f32[112,128]{1,0:T(8,128)} %get-tuple-element.22.after.refs_9_, bf16[40,16,256,128]{3,2,1,0:T(8,128)(2,1)} %get-tuple-element.23.so_far), custom_call_target="tpu_custom_call", output_to_operand_aliasing={{}: (2, {})} | custom-call | tf_op jit(solution)/shard_map/stored_table/pallas_call | solution.py:404
  18.7 0.0 collective-permute-done.refs_10_
  18.7 10.7 %gradients.1 = (f32[64,8,512]{2,1,0:T(8,128)}, f32[64,8,512]{2,1,0:T(8,128)}, bf16[40,16,256,128]{3,2,1,0:T(8,128)(2,1)}) custom-call(bf16[128,2560]{1,0:T(8,128)(2,1)} %refs_0_.3, bf16[128,2560]{1,0:T(8,128)(2,1)} %refs_1_.3, bf16[128,2560]{1,0:T(8,128)(2,1)} %refs_2_.3, bf16[128,13824]{1,0:T(8,128)(2,1)} %refs_3_.3, ...), custom_call_target="tpu_custom_call", output_to_operand_aliasing={{2}: (13, {})} | custom-call | tf_op jit(solution)/shard_map/gradients/pallas_call | solution.py:295
  29.5 0.1 collective-permute-start.1
  29.6 0.0 copy-start.2
  29.6 6.6 %stored_table.5.so_far = bf16[40,16,256,128]{3,2,1,0:T(8,128)(2,1)} custom-call(s32[16]{0:T(128)} %get-tuple-element.21.bases.refs_12_, f32[64,8,512]{2,1,0:T(8,128)} %get-tuple-element.27.after, bf16[40,16,256,128]{3,2,1,0:T(8,128)(2,1)} %get-tuple-element.28.so_far), custom_call_target="tpu_custom_call", output_to_operand_aliasing={{}: (2, {})} | custom-call | tf_op jit(solution)/shard_map/stored_table/pallas_call | solution.py:404
  36.2 0.0 collective-permute-done.1
  36.2 0.0 copy-done.2
  36.2 0.2 add.37
  36.4 0.0 copy-start
  36.5 1.6 collective-permute-start.2
  38.0 0.0 copy-done
  38.0 12.2 %stored_table.6.so_far = bf16[40,16,256,128]{3,2,1,0:T(8,128)(2,1)} custom-call(s32[16]{0:T(128)} %get-tuple-element.21.bases.refs_12_, f32[32,8,512]{2,1,0:T(8,128)} %copy-done, bf16[40,16,256,128]{3,2,1,0:T(8,128)(2,1)} %stored_table.5.so_far), custom_call_target="tpu_custom_call", output_to_operand_aliasing={{}: (2, {})} | custom-call | tf_op jit(solution)/shard_map/stored_table/pallas_call | solution.py:404
  50.3 0.5 collective-permute-done.2
  50.8 0.1 dynamic-slice_add_fusion
  50.9 0.7 constant_dynamic-slice_fusion.3
  51.6 1.6 collective-permute-start.3
  53.2 2.6 %collective-permute-start.4 = (f32[8,8,512]{2,1,0:T(8,128)S(1)}, f32[8,8,512]{2,1,0:T(8,128)S(1)}, u32[]{:S(2)}, u32[]{:S(2)}) collective-permute-start(f32[8,8,512]{2,1,0:T(8,128)S(1)} %get-tuple-element.39), channel_id=1, source_target_pairs={{0,8},{1,9},{2,10},{3,11},{4,12},{5,13},{6,14},{7,15},{8,0},{9,1},... | collective-permute-start | bytes 393224 | tf_op jit(solution)/shard_map/ppermute | solution.py:562
  55.8 0.2 collective-permute-start.5
  56.0 0.0 copy-start.1
  56.0 13.3 %stored_table.7.tiles = bf16[40,16,256,128]{3,2,1,0:T(8,128)(2,1)} custom-call(s32[16]{0:T(128)} %get-tuple-element.21.bases.refs_12_, f32[8,8,512]{2,1,0:T(8,128)} %get-tuple-element.37.after, bf16[40,16,256,128]{3,2,1,0:T(8,128)(2,1)} %stored_table.6.so_far), custom_call_target="tpu_custom_call", output_to_operand_aliasing={{}: (2, {})} | custom-call | tf_op jit(solution)/shard_map/stored_table/pallas_call | solution.py:404
  69.3 0.0 collective-permute-done.3
  69.3 0.0 collective-permute-done.4
  69.3 0.0 collective-permute-done.5
  69.3 0.0 copy-done.1
  69.4 0.7 add_bitcast_fusion.grads.old_grads
  70.0 86.2 %project.1 = f32[32,1,64]{2,1,0:T(1,128)} custom-call(s32[16]{0:T(128)} %get-tuple-element.21.bases.refs_12_, f32[1,8,8,512]{3,2,1,0:T(8,128)} %add_bitcast_fusion.grads.old_grads, f32[1,8,8,512]{3,2,1,0:T(8,128)} %add_bitcast_fusion.grads.old_grads, bf16[40,16,256,128]{3,2,1,0:T(8,128)(2,1)} %stored_table.7.tiles), custom_call_target="tpu_custom_call" | custom-call | tf_op jit(solution)/shard_map/project/pallas_call | solution.py:494
  156.3 12.3 %all_to_all.5 = f32[32,1,64]{2,1,0:T(1,128)S(1)} all-to-all(f32[32,1,64]{2,1,0:T(1,128)} %project.1), channel_id=1, replica_groups=mesh['mp'=2,'proj'=16] {'mp','proj'}, dimensions={0} | all-to-all | bytes 16384 | tf_op jit(solution)/shard_map/all_to_all | solution.py:575
  168.6 0.6 reduce_sum.11
  (1 shorter events, 0.0 us)
Async XLA Ops:
  12.1 6.6 %collective-permute-start = (f32[112,128]{1,0:T(8,128)}, f32[112,128]{1,0:T(8,128)S(1)}, u32[]{:S(2)}, u32[]{:S(2)}) collective-permute-start(f32[112,128]{1,0:T(8,128)} %get-tuple-element.22.after.refs_9_), channel_id=1, source_target_pairs={{0,16},{16,0},{1,17},{17,1},{2,18},{18,2},{3,19},{19,3},{4,20},{20... | collective-permute-start | bytes 172040 | tf_op jit(solution)/shard_map/ppermute | solution.py:516
  29.5 6.7 %collective-permute-start.1 = (f32[64,8,512]{2,1,0:T(8,128)}, f32[64,8,512]{2,1,0:T(8,128)S(1)}, u32[]{:S(2)}, u32[]{:S(2)}) collective-permute-start(f32[64,8,512]{2,1,0:T(8,128)} %get-tuple-element.27.after), channel_id=1, source_target_pairs={{0,1},{1,0},{2,3},{3,2},{4,5},{5,4},{6,7},{7,6},{8,9},{9,8},{10,11... | collective-permute-start | bytes 3145736 | tf_op jit(solution)/shard_map/ppermute | solution.py:516
  29.6 6.6 %copy-start.2 = (f32[64,8,512]{2,1,0:T(8,128)S(1)}, f32[64,8,512]{2,1,0:T(8,128)}, u32[]{:S(2)}) copy-start(f32[64,8,512]{2,1,0:T(8,128)} %get-tuple-element.26) | copy-start | bytes 3145732
  36.4 1.6 copy-start
  36.5 14.4 %collective-permute-start.2 = (f32[32,8,512]{2,1,0:T(8,128)S(1)}, f32[32,8,512]{2,1,0:T(8,128)S(1)}, u32[]{:S(2)}, u32[]{:S(2)}) collective-permute-start(f32[32,8,512]{2,1,0:T(8,128)S(1)} %constant_dynamic-slice_fusion.4.after), channel_id=1, source_target_pairs={{0,2},{1,3},{2,0},{3,1},{4,6},{5,7},{6,4},{7,5},{8,10},{9,11},{10,... | collective-permute-start | bytes 1572872 | tf_op jit(solution)/shard_map/ppermute | solution.py:516
  51.6 17.7 %collective-permute-start.3 = (f32[8,8,512]{2,1,0:T(8,128)S(1)}, f32[8,8,512]{2,1,0:T(8,128)S(1)}, u32[]{:S(2)}, u32[]{:S(2)}) collective-permute-start(f32[8,8,512]{2,1,0:T(8,128)S(1)} %get-tuple-element.40), channel_id=1, source_target_pairs={{0,4},{1,5},{2,6},{3,7},{4,0},{5,1},{6,2},{7,3},{8,12},{9,13},{10,... | collective-permute-start | bytes 393224 | tf_op jit(solution)/shard_map/ppermute | solution.py:562
  53.2 16.1 %collective-permute-start.4 = (f32[8,8,512]{2,1,0:T(8,128)S(1)}, f32[8,8,512]{2,1,0:T(8,128)S(1)}, u32[]{:S(2)}, u32[]{:S(2)}) collective-permute-start(f32[8,8,512]{2,1,0:T(8,128)S(1)} %get-tuple-element.39), channel_id=1, source_target_pairs={{0,8},{1,9},{2,10},{3,11},{4,12},{5,13},{6,14},{7,15},{8,0},{9,1},... | collective-permute-start | bytes 393224 | tf_op jit(solution)/shard_map/ppermute | solution.py:562
  55.8 13.6 %collective-permute-start.5 = (f32[8,8,512]{2,1,0:T(8,128)S(1)}, f32[8,8,512]{2,1,0:T(8,128)S(1)}, u32[]{:S(2)}, u32[]{:S(2)}) collective-permute-start(f32[8,8,512]{2,1,0:T(8,128)S(1)} %get-tuple-element.38), channel_id=1, source_target_pairs={{0,12},{1,13},{2,14},{3,15},{4,8},{5,9},{6,10},{7,11},{8,4},{9,5},... | collective-permute-start | bytes 393224 | tf_op jit(solution)/shard_map/ppermute | solution.py:562
  56.0 13.4 %copy-start.1 = (f32[8,8,512]{2,1,0:T(8,128)S(1)}, f32[8,8,512]{2,1,0:T(8,128)}, u32[]{:S(2)}) copy-start(f32[8,8,512]{2,1,0:T(8,128)} %get-tuple-element.37.after) | copy-start | bytes 393220

commit v7 on v6

--- a/solution.py
+++ b/solution.py
@@ -17,7 +17,7 @@
 COL_MULT = -1640531535
 MIX_A = -2048144789
 MIX_B = -1028477387
-STORED_STEPS = (5, 2, 5, 5, 11, 12)
+STORED_STEPS = (5, 2, 5, 3, 10, 11)
 
 srl = lax.shift_right_logical
 
@@ -394,16 +394,20 @@
     return jax.ShapeDtypeStruct((total, K // LANES, plan.sub, LANES), jnp.bfloat16)
 
 
-def stored_table(plan, bases, first, count, after, so_far):
+def stored_table(plan, bases, first, count, after, so_far, in_vmem):
     smem = pl.BlockSpec(memory_space=pltpu.SMEM)
     anywhere = pl.BlockSpec(memory_space=pl.ANY)
+    place = anywhere
+    if in_vmem:
+        after = pltpu.with_memory_space_constraint(after, pltpu.VMEM)
+        place = pl.BlockSpec(memory_space=pltpu.VMEM)
 
     def kernel(bases, after, so_far, out, *scratch):
         fill_tables(plan, first, count, (bases,) + scratch, out)()
 
     return pl.pallas_call(
         kernel,
-        in_specs=[smem, anywhere, anywhere],
+        in_specs=[smem, place, anywhere],
         out_specs=anywhere,
         out_shape=jax.ShapeDtypeStruct(so_far.shape, so_far.dtype),
         scratch_shapes=fill_scratch(plan, count),
@@ -530,7 +534,7 @@
 
     def cover(received, sent, number):
         nonlocal tiles
-        tiles = stored_table(plan, bases, starts[number], counts[number], sent, tiles)
+        tiles = stored_table(plan, bases, starts[number], counts[number], sent, tiles, number > 3)
         received, tiles = lax.optimization_barrier((received, tiles))
         return received
 

time: 169 us -> 170 us (level)
    pallas_call x4, Pallas kernels: 35.7 us -> 31.8 us  [stored_table(): pl.pallas_call(kernel, in_specs=[smem, place, anywhere], out_specs=anywhe...]
    pallas_call x1, Pallas kernels: 86.2 us -> 90 us  [project(): pl.pallas_call(kernel, grid=(rounds,), in_specs=[smem, pl.BlockSpec((plan...]
  transfers between devices with their start and end apart: 6 -> 6, of which waited for: 1 -> 1; matrix products, arithmetic and copies ran while one was open for 0% -> 0% of each run, Pallas kernels for 21% -> 19%
where the time goes in v7:
time: 170 us; the launch traced here: 169 us
  Pallas kernels  145 us (85%)
  blocking collectives  12.3 us (7%)
  starting transfers between devices  9.14 us (5%)
    pallas_call x1, Pallas kernels, project(): pl.pallas_call(kernel, grid=(rounds,), in_specs=[smem, pl.BlockSpec((plan...  90 us
    pallas_call x4, Pallas kernels, stored_table(): pl.pallas_call(kernel, in_specs=[smem, place, anywhere], out_specs=anywhe...  31.8 us
    all_to_all x1, blocking collectives, shards(): got = lax.all_to_all(pieces, ('mp', 'proj'), 0, 0, tiled=True)  12.3 us
    pallas_call x1, Pallas kernels, products(): pl.pallas_call(product_kernel(plan, count), in_specs=[anywhere] * 14 + [s...  12.1 us
    pallas_call x1, Pallas kernels, gradients(): pl.pallas_call(gradient_kernel(plan, split, first, count), in_specs=[anyw...  10.7 us
    ppermute x3, starting transfers between devices, swap(): return lax.ppermute(x, axis, [(i, i ^ 1 << bit) for i in range(size)])  4.69 us
    ppermute x3, starting transfers between devices, shards(): lax.ppermute(sends[d], 'proj', [(i, i ^ d << low) for i in range(plan.own...  4.45 us
  transfers between devices with their start and end apart: 6, of which 1 were waited for; matrix products, arithmetic and copies ran while one was open for 0% of the time, Pallas kernels for 19%

profile of v7, /device:TPU:0, one launch (start us, length us, event | category | flops | bytes accessed | tf_op | source)
XLA Modules:
  0.0 169.4 jit_solution(8403395879091134605)
XLA Ops:
  0.0 12.1 %products.1 = (f32[112,128]{1,0:T(8,128)}, bf16[36,16,256,128]{3,2,1,0:T(8,128)(2,1)}, s32[16]{0:T(128)}) custom-call(bf16[128,2560]{1,0:T(8,128)(2,1)} %refs_0_.3, bf16[128,2560]{1,0:T(8,128)(2,1)} %refs_1_.3, bf16[128,2560]{1,0:T(8,128)(2,1)} %refs_2_.3, bf16[128,13824]{1,0:T(8,128)(2,1)} %refs_3_.3, bf16[128,2560]{1,0:T(8,128)(2,1)} %refs_4_.3, ...), custom_call_target="tpu_custom_call" | custom-call | tf_op jit(solution)/shard_map/products/pallas_call | solution.py:201
  12.1 3.0 %collective-permute-start = (f32[112,128]{1,0:T(8,128)}, f32[112,128]{1,0:T(8,128)S(1)}, u32[]{:S(2)}, u32[]{:S(2)}) collective-permute-start(f32[112,128]{1,0:T(8,128)} %get-tuple-element.22.after.refs_9_), channel_id=1, source_target_pairs={{0,16},{16,0},{1,17},{17,1},{2,18},{18,2},{3,19},{19,3},{4,20},{20... | collective-permute-start | bytes 172040 | tf_op jit(solution)/shard_map/ppermute | solution.py:520
  15.1 3.6 %stored_table.4.refs_13_ = bf16[36,16,256,128]{3,2,1,0:T(8,128)(2,1)} custom-call(s32[16]{0:T(128)} %get-tuple-element.21.bases.refs_12_, f32[112,128]{1,0:T(8,128)} %get-tuple-element.22.after.refs_9_, bf16[36,16,256,128]{3,2,1,0:T(8,128)(2,1)} %get-tuple-element.23.so_far), custom_call_target="tpu_custom_call", output_to_operand_aliasing={{}: (2, {})} | custom-call | tf_op jit(solution)/shard_map/stored_table/pallas_call | solution.py:408
  18.7 0.0 collective-permute-done.refs_10_
  18.7 10.7 %gradients.1 = (f32[64,8,512]{2,1,0:T(8,128)}, f32[64,8,512]{2,1,0:T(8,128)}, bf16[36,16,256,128]{3,2,1,0:T(8,128)(2,1)}) custom-call(bf16[128,2560]{1,0:T(8,128)(2,1)} %refs_0_.3, bf16[128,2560]{1,0:T(8,128)(2,1)} %refs_1_.3, bf16[128,2560]{1,0:T(8,128)(2,1)} %refs_2_.3, bf16[128,13824]{1,0:T(8,128)(2,1)} %refs_3_.3, ...), custom_call_target="tpu_custom_call", output_to_operand_aliasing={{2}: (13, {})} | custom-call | tf_op jit(solution)/shard_map/gradients/pallas_call | solution.py:295
  29.4 0.1 collective-permute-start.1
  29.5 0.0 copy-start
  29.5 4.7 %stored_table.5.so_far = bf16[36,16,256,128]{3,2,1,0:T(8,128)(2,1)} custom-call(s32[16]{0:T(128)} %get-tuple-element.21.bases.refs_12_, f32[64,8,512]{2,1,0:T(8,128)} %get-tuple-element.27.after, bf16[36,16,256,128]{3,2,1,0:T(8,128)(2,1)} %get-tuple-element.28.so_far), custom_call_target="tpu_custom_call", output_to_operand_aliasing={{}: (2, {})} | custom-call | tf_op jit(solution)/shard_map/stored_table/pallas_call | solution.py:408
  34.2 0.0 collective-permute-done.1
  34.2 0.0 copy-done
  34.3 0.2 add.37
  34.5 1.6 collective-permute-start.2
  36.1 11.3 %stored_table.6.so_far = bf16[36,16,256,128]{3,2,1,0:T(8,128)(2,1)} custom-call(s32[16]{0:T(128)} %get-tuple-element.21.bases.refs_12_, f32[32,8,512]{2,1,0:T(8,128)S(1)} %constant_dynamic-slice_fusion.4.after, bf16[36,16,256,128]{3,2,1,0:T(8,128)(2,1)} %stored_table.5.so_far), custom_call_target="tpu_custom_call", output_to_operand_aliasing={{}: (2, {})} | custom-call | tf_op jit(solution)/shard_map/stored_table/pallas_call | solution.py:408
  47.4 1.5 collective-permute-done.2
  48.9 0.1 dynamic-slice_add_fusion
  49.0 1.6 collective-permute-start.3
  50.7 2.6 %collective-permute-start.4 = (f32[8,8,512]{2,1,0:T(8,128)S(1)}, f32[8,8,512]{2,1,0:T(8,128)S(1)}, u32[]{:S(2)}, u32[]{:S(2)}) collective-permute-start(f32[8,8,512]{2,1,0:T(8,128)S(1)} %get-tuple-element.39), channel_id=1, source_target_pairs={{0,8},{1,9},{2,10},{3,11},{4,12},{5,13},{6,14},{7,15},{8,0},{9,1},... | collective-permute-start | bytes 393224 | tf_op jit(solution)/shard_map/ppermute | solution.py:566
  53.3 0.2 collective-permute-start.5
  53.5 12.3 %stored_table.7.tiles = bf16[36,16,256,128]{3,2,1,0:T(8,128)(2,1)} custom-call(s32[16]{0:T(128)} %get-tuple-element.21.bases.refs_12_, f32[8,8,512]{2,1,0:T(8,128)S(1)} %get-tuple-element.37.after, bf16[36,16,256,128]{3,2,1,0:T(8,128)(2,1)} %stored_table.6.so_far), custom_call_target="tpu_custom_call", output_to_operand_aliasing={{}: (2, {})} | custom-call | tf_op jit(solution)/shard_map/stored_table/pallas_call | solution.py:408
  65.8 0.0 collective-permute-done.3
  65.8 0.0 collective-permute-done.4
  65.8 0.0 collective-permute-done.5
  65.8 0.7 add_bitcast_fusion.grads.old_grads
  66.5 90.0 %project.1 = f32[32,1,64]{2,1,0:T(1,128)} custom-call(s32[16]{0:T(128)} %get-tuple-element.21.bases.refs_12_, f32[1,8,8,512]{3,2,1,0:T(8,128)} %add_bitcast_fusion.grads.old_grads, f32[1,8,8,512]{3,2,1,0:T(8,128)} %add_bitcast_fusion.grads.old_grads, bf16[36,16,256,128]{3,2,1,0:T(8,128)(2,1)} %stored_table.7.tiles), custom_call_target="tpu_custom_call" | custom-call | tf_op jit(solution)/shard_map/project/pallas_call | solution.py:498
  156.5 12.3 %all_to_all.5 = f32[32,1,64]{2,1,0:T(1,128)S(1)} all-to-all(f32[32,1,64]{2,1,0:T(1,128)} %project.1), channel_id=1, replica_groups=mesh['mp'=2,'proj'=16] {'mp','proj'}, dimensions={0} | all-to-all | bytes 16384 | tf_op jit(solution)/shard_map/all_to_all | solution.py:579
  168.8 0.6 reduce_sum.11
  (2 shorter events, 0.1 us)
Async XLA Ops:
  12.1 6.6 %collective-permute-start = (f32[112,128]{1,0:T(8,128)}, f32[112,128]{1,0:T(8,128)S(1)}, u32[]{:S(2)}, u32[]{:S(2)}) collective-permute-start(f32[112,128]{1,0:T(8,128)} %get-tuple-element.22.after.refs_9_), channel_id=1, source_target_pairs={{0,16},{16,0},{1,17},{17,1},{2,18},{18,2},{3,19},{19,3},{4,20},{20... | collective-permute-start | bytes 172040 | tf_op jit(solution)/shard_map/ppermute | solution.py:520
  29.4 4.8 %collective-permute-start.1 = (f32[64,8,512]{2,1,0:T(8,128)}, f32[64,8,512]{2,1,0:T(8,128)S(1)}, u32[]{:S(2)}, u32[]{:S(2)}) collective-permute-start(f32[64,8,512]{2,1,0:T(8,128)} %get-tuple-element.27.after), channel_id=1, source_target_pairs={{0,1},{1,0},{2,3},{3,2},{4,5},{5,4},{6,7},{7,6},{8,9},{9,8},{10,11... | collective-permute-start | bytes 3145736 | tf_op jit(solution)/shard_map/ppermute | solution.py:520
  29.5 4.7 %copy-start = (f32[64,8,512]{2,1,0:T(8,128)S(1)}, f32[64,8,512]{2,1,0:T(8,128)}, u32[]{:S(2)}) copy-start(f32[64,8,512]{2,1,0:T(8,128)} %get-tuple-element.26) | copy-start | bytes 3145732
  34.5 14.4 %collective-permute-start.2 = (f32[32,8,512]{2,1,0:T(8,128)S(1)}, f32[32,8,512]{2,1,0:T(8,128)S(1)}, u32[]{:S(2)}, u32[]{:S(2)}) collective-permute-start(f32[32,8,512]{2,1,0:T(8,128)S(1)} %constant_dynamic-slice_fusion.4.after), channel_id=1, source_target_pairs={{0,2},{1,3},{2,0},{3,1},{4,6},{5,7},{6,4},{7,5},{8,10},{9,11},{10,... | collective-permute-start | bytes 1572872 | tf_op jit(solution)/shard_map/ppermute | solution.py:520
  49.0 16.7 %collective-permute-start.3 = (f32[8,8,512]{2,1,0:T(8,128)S(1)}, f32[8,8,512]{2,1,0:T(8,128)S(1)}, u32[]{:S(2)}, u32[]{:S(2)}) collective-permute-start(f32[8,8,512]{2,1,0:T(8,128)S(1)} %get-tuple-element.40), channel_id=1, source_target_pairs={{0,4},{1,5},{2,6},{3,7},{4,0},{5,1},{6,2},{7,3},{8,12},{9,13},{10,... | collective-permute-start | bytes 393224 | tf_op jit(solution)/shard_map/ppermute | solution.py:566
  50.7 15.1 %collective-permute-start.4 = (f32[8,8,512]{2,1,0:T(8,128)S(1)}, f32[8,8,512]{2,1,0:T(8,128)S(1)}, u32[]{:S(2)}, u32[]{:S(2)}) collective-permute-start(f32[8,8,512]{2,1,0:T(8,128)S(1)} %get-tuple-element.39), channel_id=1, source_target_pairs={{0,8},{1,9},{2,10},{3,11},{4,12},{5,13},{6,14},{7,15},{8,0},{9,1},... | collective-permute-start | bytes 393224 | tf_op jit(solution)/shard_map/ppermute | solution.py:566
  53.3 12.5 %collective-permute-start.5 = (f32[8,8,512]{2,1,0:T(8,128)S(1)}, f32[8,8,512]{2,1,0:T(8,128)S(1)}, u32[]{:S(2)}, u32[]{:S(2)}) collective-permute-start(f32[8,8,512]{2,1,0:T(8,128)S(1)} %get-tuple-element.38), channel_id=1, source_target_pairs={{0,12},{1,13},{2,14},{3,15},{4,8},{5,9},{6,10},{7,11},{8,4},{9,5},... | collective-permute-start | bytes 393224 | tf_op jit(solution)/shard_map/ppermute | solution.py:566
